TPU v7x, 32 devices: a whole 2x2x4 slice. The times are simulated.
32 devices in a mesh: row: 4 (over x, core), col: 8 (over z, y).
Axes of the slice: x: 2, y: 2, z: 4, core: 2. Of those that a mesh axis runs over, the one named last changes fastest.
Arguments:
- prior: float32 [16384, 16384], P('row', 'col'), may hold values from -6 to 6
- ozone_courant: float32 [16384], replicated, may hold values from 0.05 to 0.5
- ozone_diffusion: float32 [16384], replicated, may hold values from 0.02 to 0.25
- ozone_wind: int32 [16384], replicated, may hold values from 0 to 1
- carbon_courant: float32 [16384], replicated, may hold values from 0.05 to 0.5
- carbon_diffusion: float32 [16384], replicated, may hold values from 0.02 to 0.25
- carbon_wind: int32 [16384], replicated, may hold values from 0 to 1
- ozone_sites: int32 [2, 512], replicated, may hold values from 0 to 16383
- carbon_sites: int32 [2, 512], replicated, may hold values from 0 to 16383
- error_var: float32 [2, 512], replicated, may hold values from 32 to 256
Outputs:
- posterior: float32 [16384, 16384], P('row', 'col')
Inputs may be any that keep to these rules, and one draw needn't show every extreme that they name: `ozone_sites`: cells may repeat within a batch. `carbon_sites`: cells may repeat within a batch.
All inputs are finite; a program needn't handle non-finite values.
Results may differ from a plain program's by a relative error of at most 0.00012.
Values sent between devices are 32-bit elements; how exact they have to be, the bound alone decides.
A program may use at most 192 MiB of HBM per device.

v0:
```python
import functools
import jax
import jax.numpy as jnp
from jax import lax
from jax.experimental import pallas as pl
from jax.experimental.pallas import tpu as pltpu
from jax.sharding import PartitionSpec as P

STEPS = 2
BATCHES = 2
MARGIN = 8
LANES = 128
TILE = 128
HIGHEST = lax.Precision.HIGHEST
HIGH = lax.Precision.HIGH


def coefficients(courant, diffusion, wind, first_cell, before, after, count):
    pad = (before, after)
    total = count + before + after

    def cut(values):
        return lax.dynamic_slice_in_dim(jnp.pad(values, pad), first_cell, total)

    c, d, w = cut(courant), cut(diffusion), cut(wind)
    low = d + jnp.where(w == 0, c, 0.0)
    high = d + jnp.where(w == 0, 0.0, c)
    return low, 1.0 - c - 2.0 * d, high


def edges(value, axis, dim, width):
    size, length = lax.axis_size(axis), value.shape[dim]
    up = [(i, i + 1) for i in range(size - 1)]
    down = [(i + 1, i) for i in range(size - 1)]
    last = lax.slice_in_dim(value, length - width, length, axis=dim)
    leading = lax.slice_in_dim(value, 0, width, axis=dim)
    return lax.ppermute(last, axis, up), lax.ppermute(leading, axis, down)


def transport_kernel(main, prev, follow, above, below, side, row_weights, col_weights, chooser, out, picked):
    step = pl.program_id(0)
    last = pl.num_programs(0) - 1
    top = jnp.where(step == 0, above[...], prev[...])
    bottom = jnp.where(step == last, below[...], follow[...])
    body = jnp.concatenate([top, main[...], bottom], axis=0)
    value = jnp.concatenate([body, side[0]], axis=1)
    weights = row_weights[0]
    low, mid, high = weights[:, 0:1], weights[:, 1:2], weights[:, 2:3]
    rows = value.shape[0]
    for _ in range(STEPS):
        value = low * pltpu.roll(value, 1, 0) + mid * value + high * pltpu.roll(value, rows - 1, 0)
    value = value[MARGIN : rows - MARGIN]
    width = value.shape[1]
    low, mid, high = col_weights[0:1], col_weights[1:2], col_weights[2:3]
    for _ in range(STEPS):
        value = low * pltpu.roll(value, 1, 1) + mid * value + high * pltpu.roll(value, width - 1, 1)
    value = value[:, : out.shape[1]]
    out[...] = value
    coarse = value.astype(jnp.bfloat16)
    fine = (value - coarse.astype(jnp.float32)).astype(jnp.bfloat16)
    both = jnp.concatenate([coarse, fine], axis=0)
    chosen = jnp.dot(both, chooser[...], preferred_element_type=jnp.float32)
    picked[...] = chosen[: value.shape[0]] + chosen[value.shape[0] :]


def transport(prior, ozone, carbon, row_first, col_first, chooser):
    rows, cols = prior.shape
    tiles, per = rows // TILE, TILE // MARGIN
    above, below = edges(prior, "row", 0, MARGIN)
    left, right = edges(prior, "col", 1, STEPS)
    strips = jnp.concatenate([right, left], axis=1)
    strip_above, strip_below = edges(strips, "row", 0, MARGIN)
    strips = jnp.concatenate([strip_above, strips, strip_below], axis=0)
    strips = jnp.concatenate(
        [
            strips[:, :STEPS],
            jnp.zeros((strips.shape[0], LANES - 2 * STEPS), jnp.float32),
            strips[:, STEPS:],
        ],
        axis=1,
    )
    extent = TILE + 2 * MARGIN

    def windows(values):
        parts = values.reshape((tiles * per + 2, MARGIN) + values.shape[1:])
        main = parts[: tiles * per].reshape((tiles, TILE) + values.shape[1:])
        tail = parts[per:].reshape((-1,) + values.shape[1:])
        tail = jnp.stack([tail[i * TILE : i * TILE + 2 * MARGIN] for i in range(tiles)])
        return jnp.concatenate([main, tail], axis=1)

    side = windows(strips)
    row_weights = windows(
        jnp.stack(coefficients(*ozone, row_first, MARGIN, MARGIN, rows), axis=1)
    )
    row_weights = jnp.pad(row_weights, ((0, 0), (0, 0), (0, 5)))
    trio = coefficients(*carbon, col_first, STEPS, STEPS, cols)
    rolled = []
    for index, entry in enumerate(trio):
        filler = jnp.zeros((LANES - 2 * STEPS,), jnp.float32)
        rolled.append(jnp.concatenate([entry[STEPS:], filler, entry[:STEPS]]))
    col_weights = jnp.pad(jnp.stack(rolled), ((0, 5), (0, 0)))
    blocks = rows // MARGIN
    return pl.pallas_call(
        transport_kernel,
        grid=(tiles,),
        in_specs=[
            pl.BlockSpec((TILE, cols), lambda i: (i, 0)),
            pl.BlockSpec((MARGIN, cols), lambda i: (jnp.maximum(i * per - 1, 0), 0)),
            pl.BlockSpec((MARGIN, cols), lambda i: (jnp.minimum((i + 1) * per, blocks - 1), 0)),
            pl.BlockSpec((MARGIN, cols), lambda i: (0, 0)),
            pl.BlockSpec((MARGIN, cols), lambda i: (0, 0)),
            pl.BlockSpec((1, extent, LANES), lambda i: (i, 0, 0)),
            pl.BlockSpec((1, extent, 8), lambda i: (i, 0, 0)),
            pl.BlockSpec((8, cols + LANES), lambda i: (0, 0)),
            pl.BlockSpec(chooser.shape, lambda i: (0, 0)),
        ],
        out_specs=[
            pl.BlockSpec((TILE, cols), lambda i: (i, 0)),
            pl.BlockSpec((TILE, chooser.shape[1]), lambda i: (i, 0)),
        ],
        out_shape=[
            jax.ShapeDtypeStruct((rows, cols), jnp.float32),
            jax.ShapeDtypeStruct((rows, chooser.shape[1]), jnp.float32),
        ],
        compiler_params=pltpu.CompilerParams(vmem_limit_bytes=60 << 20),
    )(prior, prior, prior, above, below, side, row_weights, col_weights, chooser)


def inverse_of(matrix):
    factor = jnp.linalg.cholesky(matrix)
    identity = jnp.eye(matrix.shape[0], dtype=jnp.float32)
    return jax.scipy.linalg.cho_solve((factor, True), identity)


def exact(first_matrix, second_matrix):
    return jnp.dot(first_matrix, second_matrix, precision=HIGHEST)


def pick_rows(matrix, sites, first_cell):
    count = matrix.shape[0]
    offsets = sites - first_cell
    owned = (offsets >= 0) & (offsets < count)
    picked = matrix[jnp.clip(offsets, 0, count - 1)]
    return jnp.where(owned[:, None], picked, 0.0)


def shards(
    prior,
    ozone_courant,
    ozone_diffusion,
    ozone_wind,
    carbon_courant,
    carbon_diffusion,
    carbon_wind,
    ozone_sites,
    carbon_sites,
    error_var,
):
    rows, cols = prior.shape
    row_first = lax.axis_index("row") * rows
    col_first = lax.axis_index("col") * cols
    batches, k = ozone_sites.shape
    row_sites = ozone_sites.reshape(-1)
    col_sites = carbon_sites.reshape(-1)
    cells = col_first + lax.broadcasted_iota(jnp.int32, (cols, batches * k), 0)
    chooser = (cells == col_sites[None, :]).astype(jnp.bfloat16)
    field, picked = transport(
        prior,
        (ozone_courant, ozone_diffusion, ozone_wind),
        (carbon_courant, carbon_diffusion, carbon_wind),
        row_first,
        col_first,
        chooser,
    )
    crossing = lax.psum(pick_rows(picked, row_sites, row_first), ("row", "col"))
    row_part = pick_rows(field, row_sites, row_first)
    picked, row_part, crossing = lax.optimization_barrier((picked, row_part, crossing))
    row_panel = lax.psum(row_part, "row")
    column_panel = lax.psum(picked, "col")
    g00, g01 = crossing[:k, :k], crossing[:k, k:]
    g10, g11 = crossing[k:, :k], crossing[k:, k:]
    inv0 = inverse_of(jnp.diag(error_var[0]) + exact(g00, g00.T))
    carry = exact(g10, inv0)
    block = g11 - exact(carry, g01)
    inv1 = inverse_of(jnp.diag(error_var[1]) + exact(block, block.T))
    r0, r1 = row_panel[:k], row_panel[k:]
    w1 = exact(inv1, r1 - exact(carry, r0))
    w0 = exact(inv0, r0 - exact(g01, w1))
    weights = jnp.concatenate([w0, w1], axis=0)
    return field - jnp.dot(column_panel, weights, precision=HIGH)


def solution(mesh):
    placed = (P("row", "col"), P(), P(), P(), P(), P(), P(), P(), P(), P())
    return jax.shard_map(
        shards, mesh=mesh, in_specs=placed, out_specs=P("row", "col"), check_vma=False
    )
```

profile of v0, /device:TPU:0, one launch (start us, length us, event | category | flops | bytes accessed | tf_op | source)
XLA Modules:
  0.0 1034.8 jit_solution(13354692514392141603)
XLA Ops:
  8.7 3.0 collective-permute-start
  11.8 4.2 fusion.129
  16.0 2.3 copy.145
  20.3 5.5 collective-permute-start.3
  30.7 2.4 compare_convert_fusion.chooser
  36.9 3.6 collective-permute-start.4
  42.2 2.0 copy.93
  44.1 2.2 pad_maximum_fusion.1
  49.7 85.0 %shard_map.100 = (f32[4096,2048]{1,0:T(8,128)}, f32[4096,1024]{1,0:T(8,128)}) custom-call(f32[4096,2048]{1,0:T(8,128)} %follow.1, f32[4096,2048]{1,0:T(8,128)} %follow.1, f32[4096,2048]{1,0:T(8,128)} %follow.1, f32[8,2048]{1,0:T(8,128)} %copy-done.17, f32[8,2048]{1,0:T(8,128)} %copy-done.16, f32[32,144,128]{2,1,0:T(8,128)} %pad_maximum_fusion.side, ...), custom_call_target="tpu_custom_call" | custom-call | tf_op jit(solution)/shard_map/pallas_call | solution.py:103
  134.7 12.1 %gather_fusion.1 = f32[1024,1024]{1,0:T(8,128)} fusion(f32[4096,1024]{1,0:T(8,128)} %get-tuple-element.14, s32[1024]{0:T(1024)S(1)} %broadcast_clamp_fusion), kind=kCustom, calls=%fused_computation.1 | custom fusion | bytes 8392704 | tf_op jit(solution)/shard_map/gather | solution.py:143
  146.8 4.5 broadcast_select_fusion.1
  151.4 20.1 %gather_fusion = f32[1024,2048]{1,0:T(8,128)} fusion(f32[4096,2048]{1,0:T(8,128)} %get-tuple-element.12, s32[1024]{0:T(1024)S(1)} %broadcast_clamp_fusion), kind=kCustom, calls=%fused_computation | custom fusion | bytes 16781312 | tf_op jit(solution)/shard_map/gather | solution.py:143
  171.5 7.4 broadcast_select_fusion
  178.9 118.4 %all-reduce.13.cloned.1.call-done = f32[1024,1024]{1,0:T(8,128)} async-done(((f32[1024,1024]{1,0:T(8,128)}), f32[1024,1024]{1,0:T(8,128)}) %all-reduce.13.cloned.1.call-update) | async-done | bytes 4194320 | tf_op jit(solution)/shard_map/psum | solution.py:175
  297.7 3.5 convolution_add_fusion.1
  302.7 11.7 %cholesky.286 = f32[128,128]{1,0:T(8,128)S(1)} custom-call(f32[128,128]{1,0:T(8,128)S(1)} %cholesky.426), custom_call_target="Cholesky" | custom-call | tf_op jit(solution)/shard_map/jit(cholesky)/cholesky | solution.py:130
  314.5 9.8 custom-call.29
  327.0 12.1 %cholesky.305 = f32[128,128]{1,0:T(8,128)S(1)} custom-call(f32[128,128]{1,0:T(8,128)S(1)} %cholesky.430), custom_call_target="Cholesky" | custom-call | tf_op jit(solution)/shard_map/jit(cholesky)/cholesky | solution.py:130
  339.1 9.8 custom-call.30
  350.5 11.7 %cholesky.326 = f32[128,128]{1,0:T(8,128)S(1)} custom-call(f32[128,128]{1,0:T(8,128)S(1)} %cholesky.435), custom_call_target="Cholesky" | custom-call | tf_op jit(solution)/shard_map/jit(cholesky)/cholesky | solution.py:130
  362.2 9.8 custom-call.31
  373.5 11.9 %cholesky.343 = f32[128,128]{1,0:T(8,128)S(1)} custom-call(f32[128,128]{1,0:T(8,128)S(1)} %convolution_subtract_fusion.19), custom_call_target="Cholesky" | custom-call | tf_op jit(solution)/shard_map/jit(cholesky)/cholesky | solution.py:130
  390.0 7.6 while.4
  397.6 39.3 %custom-call.32 = f32[4,128,128]{1,2,0:T(8,128)S(1)} custom-call(f32[4,128,128]{2,1,0:T(8,128)S(1)} %get-tuple-element.31), custom_call_target="InvertDiagBlocksLowerTriangular" | custom-call | tf_op jit(solution)/shard_map/jit(_cho_solve)/triangular_solve | solution.py:132
  444.8 1.9 fusion.18
  446.7 1.9 convolution_subtract_fusion.1
  448.6 2.3 convolution_add_fusion
  454.6 11.7 %cholesky.358 = f32[128,128]{1,0:T(8,128)S(1)} custom-call(f32[128,128]{1,0:T(8,128)S(1)} %cholesky.439), custom_call_target="Cholesky" | custom-call | tf_op jit(solution)/shard_map/jit(cholesky)/cholesky | solution.py:130
  466.4 9.8 custom-call.33
  479.5 11.7 %cholesky.377 = f32[128,128]{1,0:T(8,128)S(1)} custom-call(f32[128,128]{1,0:T(8,128)S(1)} %cholesky.443), custom_call_target="Cholesky" | custom-call | tf_op jit(solution)/shard_map/jit(cholesky)/cholesky | solution.py:130
  491.3 10.0 custom-call.34
  504.3 13.2 %cholesky.398 = f32[128,128]{1,0:T(8,128)} custom-call(f32[128,128]{1,0:T(8,128)} %cholesky.448), custom_call_target="Cholesky" | custom-call | tf_op jit(solution)/shard_map/jit(cholesky)/cholesky | solution.py:130
  519.0 11.3 %custom-call.35 = f32[1,128,128]{1,2,0:T(8,128)} custom-call(f32[1,128,128]{2,1,0:T(8,128)} %get-tuple-element.102), custom_call_target="InvertDiagBlocksLowerTriangular" | custom-call | tf_op jit(solution)/shard_map/jit(cholesky)/cholesky | solution.py:130
  532.6 11.7 %cholesky.415 = f32[128,128]{1,0:T(8,128)S(1)} custom-call(f32[128,128]{1,0:T(8,128)S(1)} %convolution_subtract_fusion.18), custom_call_target="Cholesky" | custom-call | tf_op jit(solution)/shard_map/jit(cholesky)/cholesky | solution.py:130
  551.1 11.7 %while.5 = (s32[]{:T(128)}, f32[512,512]{1,0:T(8,128)}, s32[4,2]{0,1:T(2,128)S(1)}, f32[4,128,128]{2,1,0:T(8,128)S(1)}, s32[]{:T(128)}) while((s32[]{:T(128)}, f32[512,512]{1,0:T(8,128)}, s32[4,2]{0,1:T(2,128)S(1)}, f32[4,128,128]{2,1,0:T(8,128)S(1)}, s32[]{:T(128)}) %tuple.104), condition=%wide.while_cond.clone, body=%wide.while_body.clone.sunk | while | flops 2 | bytes 131189 | solution.py:132
  551.7 2.3 bitcast_dynamic-update-slice_fusion.5
  554.7 2.3 bitcast_dynamic-update-slice_fusion.5
  557.6 2.3 bitcast_dynamic-update-slice_fusion.5
  560.5 2.2 bitcast_dynamic-update-slice_fusion.5
  562.8 39.3 %custom-call.36 = f32[4,128,128]{1,2,0:T(8,128)S(1)} custom-call(f32[4,128,128]{2,1,0:T(8,128)S(1)} %get-tuple-element.32), custom_call_target="InvertDiagBlocksLowerTriangular" | custom-call | tf_op jit(solution)/shard_map/jit(_cho_solve)/triangular_solve | solution.py:132
  604.4 1.9 convolution_subtract_fusion.4
  606.7 2.4 convolution_subtract_fusion.11
  615.3 9.1 fusion.7
  624.4 6.8 fusion.3
  631.3 9.2 fusion.22
  640.5 8.6 fusion.4
  649.1 317.1 %all-reduce.15.cloned.1.call-done = f32[4096,1024]{1,0:T(8,128)} async-done(((f32[4096,1024]{1,0:T(8,128)}), f32[4096,1024]{1,0:T(8,128)}) %all-reduce.15.cloned.1.call-update) | async-done | bytes 16777232 | tf_op jit(solution)/shard_map/psum | solution.py:179
  966.2 61.9 %convolution_subtract_fusion = f32[4096,2048]{1,0:T(8,128)} fusion(f32[4096,2048]{1,0:T(8,128)} %get-tuple-element.12, f32[4096,1024]{1,0:T(8,128)} %all-reduce.15.cloned.1.call-done, f32[512,2048]{1,0:T(8,128)} %copy-done, f32[512,2048]{1,0:T(8,128)} %fusion.4), kind=kOutput, calls=%fused_computation.6 | convolution fusion | flops 51550093312 | bytes 92274688 | tf_op jit(solution)/shard_map/dot_general | solution.py:190
  (296 shorter events, 71.7 us)
Async XLA Ops:
  6.5 290.8 %all-reduce.13.cloned.1.call-start = ((), (), s32[]{:S(2)}) async-start(), calls=%async_computation | async-start | bytes 8388608 | tf_op jit(solution)/shard_map/psum | solution.py:175
  7.4 41.0 %collective-permute-start.1 = (f32[8,2048]{1,0:T(8,128)S(1)}, f32[8,2048]{1,0:T(8,128)S(1)}, u32[]{:S(2)}, u32[]{:S(2)}) collective-permute-start(f32[8,2048]{1,0:T(8,128)S(1)} %get-tuple-element.59), channel_id=1, source_target_pairs={{8,0},{16,8},{24,16},{9,1},{17,9},{25,17},{10,2},{18,10},{26,18},{... | collective-permute-start | bytes 196616 | tf_op jit(solution)/shard_map/ppermute | solution.py:37
  8.7 39.7 %collective-permute-start = (f32[8,2048]{1,0:T(8,128)S(1)}, f32[8,2048]{1,0:T(8,128)S(1)}, u32[]{:S(2)}, u32[]{:S(2)}) collective-permute-start(f32[8,2048]{1,0:T(8,128)S(1)} %get-tuple-element.60), channel_id=1, source_target_pairs={{0,8},{8,16},{16,24},{1,9},{9,17},{17,25},{2,10},{10,18},{18,26},{... | collective-permute-start | bytes 196616 | tf_op jit(solution)/shard_map/ppermute | solution.py:37
  16.0 9.8 copy-start.20
  16.0 9.9 copy-start.12
  16.0 9.9 copy-start.13
  16.0 9.9 copy-start.18
  16.0 10.3 copy-start.14
  16.0 10.3 copy-start.15
  16.0 10.3 copy-start.19
  16.0 10.7 %copy-start.21 = (s32[2,512]{1,0:T(2,128)S(1)}, s32[2,512]{1,0:T(2,128)}, u32[]{:S(2)}) copy-start(s32[2,512]{1,0:T(2,128)} %param.21) | copy-start | bytes 12292
  18.4 17.2 %collective-permute-start.2 = (f32[4096,2]{0,1:T(2,128)S(1)}, f32[4096,2]{0,1:T(2,128)S(1)}, u32[]{:S(2)}, u32[]{:S(2)}) collective-permute-start(f32[4096,2]{0,1:T(2,128)S(1)} %copy.145), channel_id=1, source_target_pairs={{1,0},{2,1},{3,2},{4,3},{5,4},{6,5},{7,6},{9,8},{10,9},{11,10},{12... | collective-permute-start | bytes 98312 | tf_op jit(solution)/shard_map/ppermute | solution.py:37
  20.3 15.3 %collective-permute-start.3 = (f32[4096,2]{0,1:T(2,128)S(1)}, f32[4096,2]{0,1:T(2,128)S(1)}, u32[]{:S(2)}, u32[]{:S(2)}) collective-permute-start(f32[4096,2]{0,1:T(2,128)S(1)} %copy.146), channel_id=1, source_target_pairs={{0,1},{1,2},{2,3},{3,4},{4,5},{5,6},{6,7},{8,9},{9,10},{10,11},{11... | collective-permute-start | bytes 98312 | tf_op jit(solution)/shard_map/ppermute | solution.py:37
  35.6 4.9 collective-permute-start.5
  36.9 4.4 collective-permute-start.4
  48.4 0.6 copy-start.16
  49.1 0.6 copy-start.17
  151.3 464.0 %all-reduce.17.cloned.1.call-start = ((), (), s32[]{:S(2)}) async-start(), calls=%async_computation.2 | async-start | bytes 16777216 | tf_op jit(solution)/shard_map/psum | solution.py:178
  178.9 118.8 %copy-start.22 = (f32[2,512]{1,0:T(2,128)S(1)}, f32[2,512]{1,0:T(2,128)}, u32[]{:S(2)}) copy-start(f32[2,512]{1,0:T(2,128)} %param.22) | copy-start | bytes 12292
  297.3 668.9 %all-reduce.15.cloned.1.call-start = ((), (), s32[]{:S(2)}) async-start(), calls=%async_computation.1 | async-start | bytes 33554432 | tf_op jit(solution)/shard_map/psum | solution.py:179
  301.8 1.0 copy-start.7
  439.4 5.4 copy-start.4
  442.9 5.7 copy-start.2
  443.8 4.8 copy-start.5
  444.8 3.8 copy-start.9
  453.6 1.0 copy-start.8
  478.8 0.7 copy-start.11
  615.3 9.1 copy-start.1
  631.2 9.3 copy-start
  631.2 9.3 copy-start.3
  631.3 9.3 copy-start.6
  631.3 9.3 copy-start.10
Sparse Core Ops, SparseCore 0:
  151.4 145.8 all-reduce.12
  299.8 152.2 all-reduce.16
  456.2 509.9 all-reduce.14
where the time goes:
time: 1040 us; the launch traced here: 1030 us
  waiting for transfers between devices  436 us (42%)
  other arithmetic  266 us (26%)
  matrix products  139 us (13%)
  Pallas kernels  85 us (8%)
  local copies, waits for them, and re-layouts  73 us (7%)
  between operations  20 us (2%)
  starting transfers between devices  16.3 us (2%)
    psum x1, waiting for transfers between devices, shards(): column_panel = lax.psum(picked, 'col')  317 us
    another operation x29, other arithmetic, inverse_of(): factor = jnp.linalg.cholesky(matrix)  163 us
    psum x1, waiting for transfers between devices, shards(): crossing = lax.psum(pick_rows(picked, row_sites, row_first), ('row', 'col'))  118 us
    pallas_call x1, Pallas kernels, transport(): pl.pallas_call(transport_kernel, grid=(tiles,), in_specs=[pl.BlockSpec((T...  85 us
    another operation x5, other arithmetic, inverse_of(): return jax.scipy.linalg.cho_solve((factor, True), identity)  79.9 us
    dot_general x1, matrix products, shards(): return field - jnp.dot(column_panel, weights, precision=HIGH)  61.9 us
    dot_general x8, matrix products, exact(): return jnp.dot(first_matrix, second_matrix, precision=HIGHEST)  43.2 us
    gather x2, local copies, waits for them, and re-layouts, pick_rows(): picked = matrix[jnp.clip(offsets, 0, count - 1)]  32.2 us
  transfers between devices with their start and end apart: 9, of which 3 were waited for; matrix products, arithmetic and copies ran while one was open for 38% of the time, Pallas kernels for 0%

commit v1 on v0

--- a/solution.py
+++ b/solution.py
@@ -1,4 +1,4 @@
-import functools
+import math
 import jax
 import jax.numpy as jnp
 from jax import lax
@@ -37,7 +37,13 @@
     return lax.ppermute(last, axis, up), lax.ppermute(leading, axis, down)
 
 
-def transport_kernel(main, prev, follow, above, below, side, row_weights, col_weights, chooser, out, picked):
+def across(left, right):
+    return lax.dot_general(
+        left, right, (((1,), (1,)), ((), ())), preferred_element_type=jnp.float32
+    )
+
+
+def transport_kernel(main, prev, follow, above, below, side, row_weights, col_weights, chooser, out, *picked):
     step = pl.program_id(0)
     last = pl.num_programs(0) - 1
     top = jnp.where(step == 0, above[...], prev[...])
@@ -58,12 +64,13 @@
     out[...] = value
     coarse = value.astype(jnp.bfloat16)
     fine = (value - coarse.astype(jnp.float32)).astype(jnp.bfloat16)
-    both = jnp.concatenate([coarse, fine], axis=0)
-    chosen = jnp.dot(both, chooser[...], preferred_element_type=jnp.float32)
-    picked[...] = chosen[: value.shape[0]] + chosen[value.shape[0] :]
-
-
-def transport(prior, ozone, carbon, row_first, col_first, chooser):
+    chosen = across(chooser[...], coarse) + across(chooser[...], fine)
+    count = chosen.shape[0] // len(picked)
+    for index, part in enumerate(picked):
+        part[...] = chosen[index * count : (index + 1) * count]
+
+
+def surroundings(prior, ozone, carbon, row_first, col_first):
     rows, cols = prior.shape
     tiles, per = rows // TILE, TILE // MARGIN
     above, below = edges(prior, "row", 0, MARGIN)
@@ -99,6 +106,14 @@
         filler = jnp.zeros((LANES - 2 * STEPS,), jnp.float32)
         rolled.append(jnp.concatenate([entry[STEPS:], filler, entry[:STEPS]]))
     col_weights = jnp.pad(jnp.stack(rolled), ((0, 5), (0, 0)))
+    return above, below, side, row_weights, col_weights
+
+
+def transport(prior, prepared, chooser, pieces):
+    rows, cols = prior.shape
+    tiles, per = rows // TILE, TILE // MARGIN
+    extent = TILE + 2 * MARGIN
+    count = chooser.shape[0] // pieces
     blocks = rows // MARGIN
     return pl.pallas_call(
         transport_kernel,
@@ -116,24 +131,490 @@
         ],
         out_specs=[
             pl.BlockSpec((TILE, cols), lambda i: (i, 0)),
-            pl.BlockSpec((TILE, chooser.shape[1]), lambda i: (i, 0)),
-        ],
+        ]
+        + [pl.BlockSpec((count, TILE), lambda i: (0, i))] * pieces,
         out_shape=[
             jax.ShapeDtypeStruct((rows, cols), jnp.float32),
-            jax.ShapeDtypeStruct((rows, chooser.shape[1]), jnp.float32),
-        ],
+        ]
+        + [jax.ShapeDtypeStruct((count, rows), jnp.float32)] * pieces,
         compiler_params=pltpu.CompilerParams(vmem_limit_bytes=60 << 20),
-    )(prior, prior, prior, above, below, side, row_weights, col_weights, chooser)
-
-
-def inverse_of(matrix):
-    factor = jnp.linalg.cholesky(matrix)
-    identity = jnp.eye(matrix.shape[0], dtype=jnp.float32)
-    return jax.scipy.linalg.cho_solve((factor, True), identity)
+    )(prior, prior, prior, *prepared, chooser)
+
+
+def plain(first_matrix, second_matrix):
+    return jnp.dot(first_matrix, second_matrix, preferred_element_type=jnp.float32)
+
+
+def rough(first_matrix, second_matrix):
+    return plain(first_matrix.astype(jnp.bfloat16), second_matrix.astype(jnp.bfloat16))
 
 
 def exact(first_matrix, second_matrix):
-    return jnp.dot(first_matrix, second_matrix, precision=HIGHEST)
+    return jnp.dot(
+        first_matrix, second_matrix, precision=HIGHEST, preferred_element_type=jnp.float32
+    )
+
+
+def halves(value):
+    coarse = value.astype(jnp.bfloat16)
+    return coarse, (value - coarse.astype(jnp.float32)).astype(jnp.bfloat16)
+
+
+def by_rows(count, step, write):
+    def body(index, carry):
+        write(pl.ds(pl.multiple_of(index * step, step), step))
+        return carry
+
+    lax.fori_loop(0, count // step, body, 0)
+
+
+def chunk(count):
+    return 128 if count % 128 == 0 else 16
+
+
+def below(rows, first):
+    return pl.ds(rows.start + first, rows.size)
+
+
+def unit_rows(rows, k):
+    down = lax.broadcasted_iota(jnp.int32, (rows.size, k), 0) + rows.start
+    return (down == lax.broadcasted_iota(jnp.int32, (rows.size, k), 1)).astype(jnp.float32)
+
+
+def cut(parts, value, rows=slice(None)):
+    for index in range(parts.shape[0]):
+        term = value.astype(jnp.bfloat16)
+        parts[index, rows, :] = term
+        value = value - term.astype(jnp.float32)
+
+
+def joined(left, right, rows, product=plain):
+    small = product(left[0, rows, :], right[2]) + product(left[2, rows, :], right[0])
+    small += product(left[1, rows, :], right[1])
+    small += product(left[0, rows, :], right[1]) + product(left[1, rows, :], right[0])
+    return small + product(left[0, rows, :], right[0])
+
+
+def whole_call(kernel, outs, scratch, *args, cost):
+    whole = pl.BlockSpec(memory_space=pltpu.VMEM)
+    return pl.pallas_call(
+        kernel,
+        in_specs=[whole] * len(args),
+        out_specs=[whole] * len(outs),
+        out_shape=[jax.ShapeDtypeStruct(*out) for out in outs],
+        scratch_shapes=[pltpu.VMEM(*entry) for entry in scratch],
+        cost_estimate=pl.CostEstimate(
+            flops=int(cost * 9e8), bytes_accessed=1 << 20, transcendentals=0
+        ),
+        compiler_params=pltpu.CompilerParams(vmem_limit_bytes=60 << 20),
+    )(*args)
+
+
+def assemble_kernel(slotted, place, g, parts):
+    cut(parts, slotted[...])
+
+    def write(rows):
+        picks = place[rows, :]
+        g[rows, :] = plain(picks, parts[0]) + plain(picks, parts[1]) + plain(picks, parts[2])
+
+    by_rows(g.shape[0], chunk(g.shape[0]), write)
+    g[...] = g[...].T
+
+
+def invert_kernel(block, variance, x, s, sp, xp, ep):
+    k = s.shape[0]
+    step = chunk(k)
+    cut(xp, block[...])
+
+    def innovation(rows):
+        s[rows, :] = unit_rows(rows, k) * variance[...] + joined(xp, xp, rows, across)
+
+    by_rows(k, step, innovation)
+    cut(sp, s[...])
+    bound = jnp.max(jnp.sum(jnp.abs(s[...]), axis=0))
+
+    def begin():
+        x[...] = (1.0 / bound) * unit_rows(pl.ds(0, k), k)
+        cut(xp, x[...])
+
+    def residual(precise):
+        def body(index, total):
+            rows = pl.ds(pl.multiple_of(index * step, step), step)
+            if precise:
+                left = unit_rows(rows, k) - joined(sp, xp, rows)
+                cut(ep, left, rows)
+            else:
+                left = unit_rows(rows, k) - plain(sp[0, rows, :], xp[0])
+                ep[0, rows, :] = left.astype(jnp.bfloat16)
+            return total + jnp.sum(left * left)
+
+        return lax.fori_loop(0, k // step, body, jnp.float32(0.0))
+
+    def improve(precise):
+        def write(rows):
+            value = plain(xp[0, rows, :], ep[0])
+            if precise:
+                value += plain(xp[0, rows, :], ep[1]) + plain(xp[1, rows, :], ep[0])
+            value += x[rows, :]
+            x[rows, :] = value
+            if precise:
+                cut(xp, value, rows)
+            else:
+                xp[0, rows, :] = value.astype(jnp.bfloat16)
+
+        by_rows(k, step, write)
+
+    begin()
+    first = residual(False)
+
+    def coarse_more(state):
+        index, norm = state
+        return (index < 14) & (norm > 0.25) & (norm <= 1.1 * first)
+
+    def coarse_step(state):
+        index, _ = state
+        improve(False)
+        return index + 1, residual(False)
+
+    lax.while_loop(coarse_more, coarse_step, (jnp.int32(0), first))
+    cut(xp, x[...])
+
+    def fine_more(state):
+        index, norm = state
+        return (index < 60) & jnp.logical_not(norm < 1e-7)
+
+    def fine_step(state):
+        index, norm = state
+
+        @pl.when((index == 0) | (norm < 0.8) | (index > 1))
+        def _():
+            @pl.when(index > 0)
+            def _():
+                improve(True)
+
+        @pl.when((index == 1) & jnp.logical_not(norm < 0.8))
+        def _():
+            begin()
+
+        return index + 1, residual(True)
+
+    lax.while_loop(fine_more, fine_step, (jnp.int32(0), jnp.float32(1.0)))
+    improve(True)
+
+
+def deflate_kernel(g, x0, carry, block, left, right):
+    k = x0.shape[0]
+    step = chunk(k)
+    cut(left, g[k:, :k])
+    cut(right, x0[...])
+
+    def carry_rows(rows):
+        carry[rows, :] = joined(left, right, rows)
+
+    by_rows(k, step, carry_rows)
+    cut(left, carry[...])
+    cut(right, g[:k, k:])
+
+    def block_rows(rows):
+        block[rows, :] = g[below(rows, k), k:] - joined(left, right, rows)
+
+    by_rows(k, step, block_rows)
+
+
+def gain_kernel(g, x0, x1, carry, spots, back, coarse_out, fine_out, hp, ap, xp, tp, part):
+    k = x0.shape[0]
+    step = chunk(k)
+    both = 2 * k
+    low, high = pl.ds(0, k), pl.ds(k, k)
+
+    def put(rows, columns, value):
+        coarse, fine = halves(value)
+        part[0, rows, columns] = coarse
+        part[1, rows, columns] = fine
+
+    cut(hp, x0[...])
+    cut(ap, g[:k, k:])
+
+    def h_rows(rows):
+        cut(xp, joined(hp, ap, rows), rows)
+
+    by_rows(k, step, h_rows)
+    for index in range(3):
+        hp[index] = xp[index]
+    cut(xp, x1[...])
+
+    def right_rows(rows):
+        put(rows, high, -joined(hp, xp, rows))
+        put(below(rows, k), high, x1[rows, :])
+
+    by_rows(k, step, right_rows)
+
+    def a_rows(rows):
+        value = joined(xp, ap, rows)
+        put(below(rows, k), low, -value)
+        cut(tp, value, rows)
+
+    cut(ap, carry[...])
+    by_rows(k, step, a_rows)
+
+    def left_rows(rows):
+        put(rows, low, x0[rows, :] + joined(hp, tp, rows))
+
+    by_rows(k, step, left_rows)
+
+    def slot_rows(rows):
+        picks = back[rows, :]
+        for index, out in ((0, coarse_out), (1, fine_out)):
+            moved = plain(picks, part[index]).astype(jnp.bfloat16)
+            out[rows, :] = plain(moved, spots[...]).astype(jnp.bfloat16)
+
+    by_rows(back.shape[0], chunk(back.shape[0]), slot_rows)
+
+
+def gain(slotted, place, spots, back, variance):
+    slots, both = slotted.shape
+    k = both // 2
+    square = ((k, k), jnp.float32)
+    terms = ((3, k, k), jnp.bfloat16)
+    (g,) = whole_call(
+        assemble_kernel,
+        [((both, both), jnp.float32)],
+        [((3, slots, both), jnp.bfloat16)],
+        slotted,
+        place,
+        cost=15,
+    )
+
+    def inverse(block, b):
+        scratch = [square, terms, terms, terms]
+        return whole_call(
+            invert_kernel, [square], scratch, block, variance[b : b + 1], cost=30
+        )[0]
+
+    x0 = inverse(g[:k, :k], 0)
+    carry, block = whole_call(deflate_kernel, [square, square], [terms, terms], g, x0, cost=8)
+    x1 = inverse(block, 1)
+    out = ((slots, spots.shape[1]), jnp.bfloat16)
+    return whole_call(
+        gain_kernel,
+        [out, out],
+        [terms] * 4 + [((2, both, both), jnp.bfloat16)],
+        g,
+        x0,
+        x1,
+        carry,
+        spots,
+        back,
+        cost=28,
+    )
+
+
+def crossing_kernel(known, slotted, send, recv, side_send, side_recv):
+    size = lax.axis_size("col")
+    half, side = known.shape[0] // 2, known.shape[1] // 2
+    row, col = lax.axis_index("row"), lax.axis_index("col")
+    core = row % 2
+    even = col % 2 == 0
+    ahead = jnp.where(
+        even,
+        jnp.where(col + 2 < size, col + 2, col + 1),
+        jnp.where(col > 1, col - 2, col - 1),
+    )
+    behind = jnp.where(
+        even,
+        jnp.where(col > 1, col - 2, col + 1),
+        jnp.where(col + 2 < size, col + 2, col - 1),
+    )
+    partner = row + 1 - 2 * core
+    mesh_ids = pl.DeviceIdType.MESH
+    barrier = pltpu.get_barrier_semaphore()
+    for device in ({"col": ahead}, {"col": behind}, {"row": partner}):
+        pl.semaphore_signal(barrier, inc=1, device_id=device, device_id_type=mesh_ids)
+    pl.semaphore_wait(barrier, 3)
+    columns = pl.ds(pl.multiple_of(core * side, side), side)
+
+    def slot(way, step):
+        return slotted.at[pl.ds((way * size + step) * half, half), columns]
+
+    def source(way, step):
+        if step == 0:
+            return known.at[pl.ds(way * half, half), columns]
+        return slot(way, step)
+
+    copies, sides = {}, []
+    for step in range(size):
+        for way, device in ((0, {"col": ahead}), (1, {"col": behind})):
+            if step:
+                copies[way, step - 1].wait_recv()
+            if step < size - 1:
+                copy = pltpu.make_async_remote_copy(
+                    src_ref=source(way, step),
+                    dst_ref=slot(way, step + 1),
+                    send_sem=send.at[way, step],
+                    recv_sem=recv.at[way, step],
+                    device_id=device,
+                    device_id_type=mesh_ids,
+                )
+                copy.start()
+                copies[way, step] = copy
+            copy = pltpu.make_async_remote_copy(
+                src_ref=source(way, step),
+                dst_ref=slot(way, step),
+                send_sem=side_send.at[way, step],
+                recv_sem=side_recv.at[way, step],
+                device_id={"row": partner},
+                device_id_type=mesh_ids,
+            )
+            copy.start()
+            sides.append(copy)
+            if step == 0:
+                slotted[pl.ds(way * size * half, half), columns] = known[
+                    pl.ds(way * half, half), columns
+                ]
+    for copy in copies.values():
+        copy.wait_send()
+    for copy in sides:
+        copy.wait()
+
+
+def crossing_gather(known):
+    size = lax.axis_size("col")
+    whole = pl.BlockSpec(memory_space=pltpu.VMEM)
+    sems = pltpu.SemaphoreType.DMA((2, size))
+    return pl.pallas_call(
+        crossing_kernel,
+        in_specs=[whole],
+        out_specs=whole,
+        out_shape=jax.ShapeDtypeStruct((known.shape[0] * size, known.shape[1]), known.dtype),
+        scratch_shapes=[sems] * 4,
+        compiler_params=pltpu.CompilerParams(collective_id=0, has_side_effects=True),
+    )(known)
+
+
+def weights_kernel(gain_coarse, gain_fine, *refs):
+    panels, (coarse_out, fine_out) = refs[:-2], refs[-2:]
+    coarse, fine = halves(jnp.concatenate([panel[...] for panel in panels], axis=0))
+
+    def write(rows):
+        value = plain(gain_coarse[rows, :], coarse)
+        value += plain(gain_coarse[rows, :], fine) + plain(gain_fine[rows, :], coarse)
+        coarse_out[rows, :], fine_out[rows, :] = halves(value)
+
+    by_rows(gain_coarse.shape[0], 16 * (gain_coarse.shape[0] // 64), write)
+
+
+def weights_of(gain_coarse, gain_fine, panels):
+    slots = gain_coarse.shape[0]
+    cols = panels[0].shape[1]
+    wide = min(256, cols)
+    held = pl.BlockSpec(gain_coarse.shape, lambda j: (0, 0), pipeline_mode=pl.Buffered(1))
+    out = jax.ShapeDtypeStruct((slots, cols), jnp.bfloat16)
+    return pl.pallas_call(
+        weights_kernel,
+        grid=(cols // wide,),
+        in_specs=[held, held]
+        + [pl.BlockSpec((p.shape[0], wide), lambda j: (0, j)) for p in panels],
+        out_specs=[pl.BlockSpec((slots, wide), lambda j: (0, j))] * 2,
+        out_shape=[out, out],
+        cost_estimate=pl.CostEstimate(
+            flops=6 * slots * gain_coarse.shape[1] * cols,
+            bytes_accessed=12 * slots * cols,
+            transcendentals=0,
+        ),
+        compiler_params=pltpu.CompilerParams(vmem_limit_bytes=60 << 20),
+    )(gain_coarse, gain_fine, *panels)
+
+
+def update_kernel(field, weights_coarse, weights_fine, *refs):
+    panels, out = refs[:-1], refs[-1]
+    panel = jnp.concatenate([part[...] for part in panels], axis=0).T
+    coarse, fine = halves(panel)
+    wide = min(512, out.shape[1])
+    for first in range(0, out.shape[1], wide):
+        columns = slice(first, first + wide)
+        value = plain(coarse, weights_coarse[:, columns])
+        value += plain(coarse, weights_fine[:, columns])
+        value += plain(fine, weights_coarse[:, columns])
+        out[:, columns] = field[:, columns] - value
+
+
+def update(field, weights_coarse, weights_fine, panels):
+    rows, cols = field.shape
+    tall = min(256, rows)
+    tile = pl.BlockSpec((tall, cols), lambda i: (i, 0))
+    held = pl.BlockSpec(weights_coarse.shape, lambda i: (0, 0), pipeline_mode=pl.Buffered(1))
+    return pl.pallas_call(
+        update_kernel,
+        grid=(rows // tall,),
+        in_specs=[tile, held, held]
+        + [pl.BlockSpec((p.shape[0], tall), lambda i: (0, i)) for p in panels],
+        out_specs=tile,
+        out_shape=jax.ShapeDtypeStruct(field.shape, jnp.float32),
+        compiler_params=pltpu.CompilerParams(vmem_limit_bytes=60 << 20),
+    )(field, weights_coarse, weights_fine, *panels)
+
+
+def capacity(total, parts):
+    mean = total / parts
+    need = math.ceil((mean + 3.0 * math.sqrt(mean * (1 - 1 / parts))) / 16) * 16
+    return min(need, total)
+
+
+def ring_of(size):
+    return list(range(0, size, 2)) + list(range(size - 1 - size % 2, 0, -2))
+
+
+def ring_gather(up_part, down_part, axis):
+    cycle = ring_of(lax.axis_size(axis))
+    ahead = [(cycle[i], cycle[(i + 1) % len(cycle)]) for i in range(len(cycle))]
+    behind = [(b, a) for a, b in ahead]
+    ups, downs = [up_part], [down_part]
+    for _ in range(len(cycle) - 1):
+        ups.append(lax.ppermute(ups[-1], axis, ahead))
+        downs.append(lax.ppermute(downs[-1], axis, behind))
+    return ups, downs
+
+
+def doubling_masks(size):
+    masks, reach = [0], size // 2
+    while reach:
+        masks += [mask ^ reach for mask in masks]
+        reach //= 2
+    return masks
+
+
+def doubling_gather(value, axis):
+    size = lax.axis_size(axis)
+    parts, reach = [value], size // 2
+    while reach:
+        pairs = [(i, i ^ reach) for i in range(size)]
+        parts += [lax.ppermute(part, axis, pairs) for part in parts]
+        reach //= 2
+    return parts
+
+
+def lookup(table, index):
+    return jnp.sum(
+        jnp.where(index[:, None] == jnp.arange(len(table))[None, :], jnp.array(table)[None, :], 0),
+        axis=1,
+    )
+
+
+def places(sites, extent):
+    owner = sites // extent
+    before = jnp.tril(jnp.ones((sites.size, sites.size), jnp.bool_), -1)
+    same = owner[:, None] == owner[None, :]
+    return owner, jnp.sum((same & before).astype(jnp.int32), axis=1)
+
+
+def local_cells(sites, owner, rank, me, extent, count, empty):
+    hit = (owner == me)[None, :] & (rank[None, :] == jnp.arange(count)[:, None])
+    cell = jnp.sum(jnp.where(hit, (sites - me * extent - empty)[None, :], 0), axis=1)
+    return cell + empty
+
+
+def one_hot(index, count):
+    return (index[:, None] == jnp.arange(count)[None, :]).astype(jnp.bfloat16)
 
 
 def pick_rows(matrix, sites, first_cell):
@@ -142,6 +623,69 @@
     owned = (offsets >= 0) & (offsets < count)
     picked = matrix[jnp.clip(offsets, 0, count - 1)]
     return jnp.where(owned[:, None], picked, 0.0)
+
+
+def balanced(prior, prepared, row_sites, col_sites, error_var, row_place, col_place):
+    rows, cols = prior.shape
+    across_rows, across_cols = lax.axis_size("row"), lax.axis_size("col")
+    my_row, my_col = lax.axis_index("row"), lax.axis_index("col")
+    total = row_sites.size
+    row_slots, col_slots = capacity(total, across_rows), capacity(total, across_cols)
+    row_owner, row_rank = row_place
+    col_owner, col_rank = col_place
+    half = col_slots // 2
+
+    my_rows = local_cells(row_sites, row_owner, row_rank, my_row, rows, row_slots, 0)
+    my_cols = local_cells(col_sites, col_owner, col_rank, my_col, cols, col_slots, -1)
+    chooser = one_hot(my_cols, cols)
+
+    masks = doubling_masks(across_rows)
+    order = [masks.index(mask) for mask in range(across_rows)]
+    row_slot = lookup(order, row_owner ^ my_row) * row_slots + row_rank
+    cycle = ring_of(across_cols)
+    spot = [cycle.index(c) for c in range(across_cols)]
+    here = lookup(spot, my_col[None])[0]
+    away = lookup(spot, col_owner) - here
+    up_step, down_step = (-away) % across_cols, away % across_cols
+    col_slot = jnp.where(
+        col_rank < half,
+        up_step * half + col_rank,
+        (across_cols + down_step) * half + col_rank - half,
+    )
+    spots = one_hot(row_slot, across_rows * row_slots)
+    place = one_hot(col_slot, across_cols * col_slots)
+
+    field, up_part, down_part = transport(prior, prepared, chooser, 2)
+    row_part = field[my_rows]
+    crossing = lax.dot_general(
+        chooser.astype(jnp.float32), row_part, (((1,), (1,)), ((), ())), precision=HIGHEST
+    )
+    pieces = doubling_gather(crossing, "row")
+    known = exact(jnp.concatenate(pieces, axis=1), spots.astype(jnp.float32).T)
+    slotted = crossing_gather(known)
+    panels = doubling_gather(row_part, "row")
+    up_panels, down_panels = ring_gather(up_part, down_part, "col")
+    gain_coarse, gain_fine = gain(slotted, place, spots, place.T, error_var)
+    weights = weights_of(gain_coarse, gain_fine, panels)
+    return update(field, *weights, up_panels + down_panels)
+
+
+def crowded(prior, prepared, row_sites, col_sites, error_var, row_place, col_place):
+    rows, cols = prior.shape
+    row_first = lax.axis_index("row") * rows
+    col_first = lax.axis_index("col") * cols
+    chooser = one_hot(col_sites - col_first, cols)
+    field, picked = transport(prior, prepared, chooser, 1)
+    row_part = pick_rows(field, row_sites, row_first)
+    crossing = lax.dot_general(
+        chooser.astype(jnp.float32), row_part, (((1,), (1,)), ((), ())), precision=HIGHEST
+    )
+    crossing = lax.psum(crossing, ("row", "col"))
+    row_panel = lax.psum(row_part, "row")
+    column_panel = lax.psum(picked, "col")
+    same = jnp.eye(row_sites.size, dtype=jnp.bfloat16)
+    weights = weights_of(*gain(crossing, same, same, same, error_var), [row_panel])
+    return update(field, *weights, [column_panel])
 
 
 def shards(
@@ -157,37 +701,21 @@
     error_var,
 ):
     rows, cols = prior.shape
-    row_first = lax.axis_index("row") * rows
-    col_first = lax.axis_index("col") * cols
-    batches, k = ozone_sites.shape
     row_sites = ozone_sites.reshape(-1)
     col_sites = carbon_sites.reshape(-1)
-    cells = col_first + lax.broadcasted_iota(jnp.int32, (cols, batches * k), 0)
-    chooser = (cells == col_sites[None, :]).astype(jnp.bfloat16)
-    field, picked = transport(
-        prior,
-        (ozone_courant, ozone_diffusion, ozone_wind),
-        (carbon_courant, carbon_diffusion, carbon_wind),
-        row_first,
-        col_first,
-        chooser,
-    )
-    crossing = lax.psum(pick_rows(picked, row_sites, row_first), ("row", "col"))
-    row_part = pick_rows(field, row_sites, row_first)
-    picked, row_part, crossing = lax.optimization_barrier((picked, row_part, crossing))
-    row_panel = lax.psum(row_part, "row")
-    column_panel = lax.psum(picked, "col")
-    g00, g01 = crossing[:k, :k], crossing[:k, k:]
-    g10, g11 = crossing[k:, :k], crossing[k:, k:]
-    inv0 = inverse_of(jnp.diag(error_var[0]) + exact(g00, g00.T))
-    carry = exact(g10, inv0)
-    block = g11 - exact(carry, g01)
-    inv1 = inverse_of(jnp.diag(error_var[1]) + exact(block, block.T))
-    r0, r1 = row_panel[:k], row_panel[k:]
-    w1 = exact(inv1, r1 - exact(carry, r0))
-    w0 = exact(inv0, r0 - exact(g01, w1))
-    weights = jnp.concatenate([w0, w1], axis=0)
-    return field - jnp.dot(column_panel, weights, precision=HIGH)
+    ozone = (ozone_courant, ozone_diffusion, ozone_wind)
+    carbon = (carbon_courant, carbon_diffusion, carbon_wind)
+    row_place = places(row_sites, rows)
+    col_place = places(col_sites, cols)
+    total = row_sites.size
+    fits = (jnp.max(row_place[1]) < capacity(total, lax.axis_size("row"))) & (
+        jnp.max(col_place[1]) < capacity(total, lax.axis_size("col"))
+    )
+    prepared = surroundings(
+        prior, ozone, carbon, lax.axis_index("row") * rows, lax.axis_index("col") * cols
+    )
+    given = (prior, prepared, row_sites, col_sites, error_var, row_place, col_place)
+    return lax.cond(fits, balanced, crowded, *given)
 
 
 def solution(mesh):

time: 1040 us -> 546 us (0.53)
  waiting for transfers between devices: 436 us -> 26 us
  Pallas kernels: 85 us -> 395 us
  other arithmetic: 266 us -> 16.3 us
  matrix products: 139 us -> 6.45 us
  local copies, waits for them, and re-layouts: 73 us -> 34.5 us
  starting transfers between devices: 16.3 us -> 38 us
    psum x3 -> x0, waiting for transfers between devices: 436 us -> none  [the longest x1 317 us: shards(): column_panel = lax.psum(picked, 'col')]
    pallas_call x0 -> x8, Pallas kernels: none -> 325 us  [the longest x5 153 us: whole_call(): pl.pallas_call(kernel, in_specs=[whole] * len(args), out_specs=[whole] *...]
    another operation x36 -> x2, other arithmetic: 244 us -> 0.09 us  [the longest x1 0.05 us: surroundings(): jnp.stack(coefficients(*ozone, row_first, MARGIN, MARGIN, rows), axis=1)]
    dot_general x9 -> x2, matrix products: 105 us -> 6.45 us  [the longest x1 4.66 us: exact(): jnp.dot(first_matrix, second_matrix, precision=HIGHEST, preferred_element...]
    another operation x40 -> x0, matrix products: 33.5 us -> none  [the longest x28 20.8 us: inverse_of(): return jax.scipy.linalg.cho_solve((factor, True), identity)]
    ppermute x0 -> x20, waiting for transfers between devices: none -> 25.3 us  [the longest x7 25 us: ring_gather(): ups.append(lax.ppermute(ups[-1], axis, ahead))]
    ppermute x0 -> x20, starting transfers between devices: none -> 22 us  [the longest x7 10.9 us: ring_gather(): ups.append(lax.ppermute(ups[-1], axis, ahead))]
    another operation x41 -> x9, local copies, waits for them, and re-layouts: 20.2 us -> 2.21 us  [the longest x27 19.2 us: inverse_of(): return jax.scipy.linalg.cho_solve((factor, True), identity)]
  transfers between devices with their start and end apart: 9 -> 26, of which waited for: 3 -> 4; matrix products, arithmetic and copies ran while one was open for 38% -> 10% of each run, Pallas kernels for 0% -> 46%
where the time goes in v1:
time: 546 us; the launch traced here: 540 us
  Pallas kernels  395 us (72%)
  starting transfers between devices  38 us (7%)
  local copies, waits for them, and re-layouts  34.5 us (6%)
  waiting for transfers between devices  26 us (5%)
  other arithmetic  16.3 us (3%)
  between operations  15.9 us (3%)
  loops' own time  8.19 us (2%)
  matrix products  6.45 us (1%)
    pallas_call x5, Pallas kernels, whole_call(): pl.pallas_call(kernel, in_specs=[whole] * len(args), out_specs=[whole] *...  153 us
    pallas_call x1, Pallas kernels, update(): pl.pallas_call(update_kernel, grid=(rows // tall,), in_specs=[tile, held,...  75.8 us
    pallas_call x1, Pallas kernels, transport(): pl.pallas_call(transport_kernel, grid=(tiles,), in_specs=[pl.BlockSpec((T...  70.4 us
    pallas_call x1, Pallas kernels, crossing_gather(): pl.pallas_call(crossing_kernel, in_specs=[whole], out_specs=whole, out_sh...  63.3 us
    pallas_call x1, Pallas kernels, weights_of(): pl.pallas_call(weights_kernel, grid=(cols // wide,), in_specs=[held, held...  32.5 us
    ppermute x7, waiting for transfers between devices, ring_gather(): ups.append(lax.ppermute(ups[-1], axis, ahead))  25 us
    ppermute x6, starting transfers between devices, edges(): return (lax.ppermute(last, axis, up), lax.ppermute(leading, axis, down))  16 us
    gather x1, local copies, waits for them, and re-layouts, balanced(): row_part = field[my_rows]  14.8 us
  transfers between devices with their start and end apart: 26, of which 4 were waited for; matrix products, arithmetic and copies ran while one was open for 10% of the time, Pallas kernels for 46%

profile of v1, /device:TPU:0, one launch (start us, length us, event | category | flops | bytes accessed | tf_op | source)
XLA Modules:
  0.0 540.3 jit_solution(11492024035895247226)
XLA Ops:
  6.5 0.9 fusion.47
  7.4 1.3 collective-permute-start.21
  8.7 3.0 collective-permute-start.20
  11.8 4.2 fusion.46
  16.0 2.3 copy.68
  18.4 1.3 collective-permute-start.22
  20.3 5.5 %collective-permute-start.23 = (f32[4096,2]{0,1:T(2,128)S(1)}, f32[4096,2]{0,1:T(2,128)S(1)}, u32[]{:S(2)}, u32[]{:S(2)}) collective-permute-start(f32[4096,2]{0,1:T(2,128)S(1)} %copy.69), channel_id=1, source_target_pairs={{0,1},{1,2},{2,3},{3,4},{4,5},{5,6},{6,7},{8,9},{9,10},{10,11},{11... | collective-permute-start | bytes 98312 | tf_op jit(solution)/shard_map/ppermute | solution.py:37
  27.4 2.1 convert_reduce_fusion
  32.3 1.3 collective-permute-start.25
  33.6 3.6 collective-permute-start.24
  37.2 0.7 collective-permute-done.24
  38.8 2.0 copy.64
  40.8 2.2 pad_maximum_fusion.1
  44.2 488.8 %conditional.1 = (f32[4096,2048]{1,0:T(8,128)}) conditional(s32[]{:T(128)} %convert_element_type.45, (s32[1024]{0:T(1024)S(1)}, f32[4096,2048]{1,0:T(8,128)}, f32[8,2048]{1,0:T(8,128)S(1)}, f32[8,2048]{1,0:T(8,128)S(1)}, f32[32,144,128]{2,1,0:T(8,128)S(1)}, /*index=5*/f32[32,144,8]{1,0,2:T(8,128)S(1)}, f32[8,2176]{1,0:T(8,128)S(1)}, ...), branch_computations={%region_4.8_spmd, %region_8.14_spmd} | conditional | flops 138572546048 | bytes 261433568 | solution.py:718
  52.7 1.1 fusion.11.chooser
  53.8 2.1 copy.67.row_weights
  56.0 70.4 %branch_1_fun.9 = (f32[4096,2048]{1,0:T(8,128)}, f32[80,4096]{1,0:T(8,128)}, f32[80,4096]{1,0:T(8,128)}) custom-call(f32[4096,2048]{1,0:T(8,128)} %get-tuple-element.114.main.prev.follow, f32[4096,2048]{1,0:T(8,128)} %get-tuple-element.114.main.prev.follow, f32[4096,2048]{1,0:T(8,128)} %get-tuple-element.114.main.prev.follow, ...), custom_call_target="tpu_custom_call" | custom-call | tf_op jit(solution)/shard_map/cond/branch_1_fun/pallas_call | solution.py:118
  126.4 1.6 collective-permute-start.6
  127.9 0.9 collective-permute-start.13
  129.3 14.8 %gather_fusion = f32[304,2048]{1,0:T(8,128)S(1)} fusion(f32[4096,2048]{1,0:T(8,128)} %get-tuple-element.128.field, s32[1024]{0:T(1024)S(1)} %pad_clamp_fusion), kind=kCustom, calls=%fused_computation.1 | custom fusion | bytes 4981952 | tf_op jit(solution)/shard_map/cond/branch_1_fun/gather | solution.py:659
  144.1 1.8 fusion.10
  145.9 1.4 collective-permute-start.1
  147.4 2.5 collective-permute-start
  151.5 2.7 fusion.8.back
  154.2 3.6 collective-permute-done.6.refs_1_
  157.8 1.5 collective-permute-start.7
  160.1 2.1 fusion.7.place
  162.2 2.0 fusion.5.spots
  165.1 1.9 collective-permute-start.3
  166.9 1.5 concatenate.18
  168.5 21.4 %collective-permute-done.7.refs_2_ = f32[80,4096]{1,0:T(8,128)} collective-permute-done((f32[80,4096]{1,0:T(8,128)}, f32[80,4096]{1,0:T(8,128)}, u32[]{:S(2)}, u32[]{:S(2)}) %collective-permute-start.7) | collective-permute-done | bytes 1310752 | tf_op jit(solution)/shard_map/cond/branch_1_fun/ppermute | solution.py:573
  189.8 1.2 collective-permute-start.8
  191.0 1.0 collective-permute-start.15
  192.1 4.7 fusion.6.known
  196.7 63.3 %branch_1_fun.10.slotted = f32[1280,1024]{1,0:T(8,128)} custom-call(f32[160,1024]{1,0:T(8,128)} %fusion.6.known), custom_call_target="tpu_custom_call" | custom-call | tf_op jit(solution)/shard_map/cond/branch_1_fun/pallas_call | solution.py:484
  260.0 17.5 %branch_1_fun.11.g = f32[1024,1024]{1,0:T(8,128)} custom-call(f32[1280,1024]{1,0:T(8,128)} %branch_1_fun.10.slotted, bf16[1024,1280]{1,0:T(8,128)(2,1)} %fusion.7.place), custom_call_target="tpu_custom_call" | custom-call | flops 13500000256 | bytes 1048576 | tf_op jit(solution)/shard_map/cond/branch_1_fun/pallas_call | solution.py:200
  277.5 2.3 slice.415.block
  279.7 2.2 collective-permute-start.9
  282.4 46.5 %branch_1_fun.12.x0 = f32[512,512]{1,0:T(8,128)} custom-call(f32[512,512]{1,0:T(8,128)} %slice.415.block, f32[1,512]{1,0:T(1,128)} %get-tuple-element.228.variance), custom_call_target="tpu_custom_call" | custom-call | flops 27000000512 | bytes 1048576 | tf_op jit(solution)/shard_map/cond/branch_1_fun/pallas_call | solution.py:200
  328.9 9.1 %branch_1_fun.13 = (f32[512,512]{1,0:T(8,128)}, f32[512,512]{1,0:T(8,128)}) custom-call(f32[1024,1024]{1,0:T(8,128)} %branch_1_fun.11.g, f32[512,512]{1,0:T(8,128)} %branch_1_fun.12.x0), custom_call_target="tpu_custom_call" | custom-call | flops 7200000000 | bytes 1048576 | tf_op jit(solution)/shard_map/cond/branch_1_fun/pallas_call | solution.py:200
  338.1 1.5 collective-permute-start.10
  339.6 0.8 collective-permute-start.17
  340.4 46.5 %branch_1_fun.14.x1 = f32[512,512]{1,0:T(8,128)} custom-call(f32[512,512]{1,0:T(8,128)} %get-tuple-element.138.block, f32[1,512]{1,0:T(1,128)} %get-tuple-element.227.variance), custom_call_target="tpu_custom_call" | custom-call | flops 27000000512 | bytes 1048576 | tf_op jit(solution)/shard_map/cond/branch_1_fun/pallas_call | solution.py:200
  386.9 1.5 collective-permute-start.11
  388.9 33.4 %branch_1_fun.15 = (bf16[1280,1216]{1,0:T(8,128)(2,1)}, bf16[1280,1216]{1,0:T(8,128)(2,1)}) custom-call(f32[1024,1024]{1,0:T(8,128)} %branch_1_fun.11.g, f32[512,512]{1,0:T(8,128)} %branch_1_fun.12.x0, f32[512,512]{1,0:T(8,128)} %branch_1_fun.14.x1, f32[512,512]{1,0:T(8,128)} %get-tuple-element.139.carry, bf16[1024,1216]{1,0:T(8,128)(2,1)} %fusion.5.spots, ...), custom_call_target="tpu_custom_call" | custom-call | flops 25200001024 | bytes 1048576 | tf_op jit(solution)/shard_map/cond/branch_1_fun/pallas_call | solution.py:200
  422.3 1.5 collective-permute-start.12
  424.4 32.5 %branch_1_fun.16 = (bf16[1280,2048]{1,0:T(8,128)(2,1)}, bf16[1280,2048]{1,0:T(8,128)(2,1)}) custom-call(bf16[1280,1216]{1,0:T(8,128)(2,1)} %get-tuple-element.140.gain_coarse, bf16[1280,1216]{1,0:T(8,128)(2,1)} %get-tuple-element.141.gain_fine, f32[304,2048]{1,0:T(8,128)} %copy-done, f32[304,2048]{1,0:T(8,128)} %collective-permute-done.3.refs_1_, ...), custom_call_target="tpu_custom_call" | custom-call | flops 19126026240 | bytes 31457280 | tf_op jit(solution)/shard_map/cond/branch_1_fun/pallas_call | solution.py:512
  456.8 75.8 %branch_1_fun.17 = f32[4096,2048]{1,0:T(8,128)} custom-call(f32[4096,2048]{1,0:T(8,128)} %get-tuple-element.128.field, bf16[1280,2048]{1,0:T(8,128)(2,1)} %get-tuple-element.142.weights_coarse, bf16[1280,2048]{1,0:T(8,128)(2,1)} %get-tuple-element.143.weights_fine, f32[80,4096]{1,0:T(8,128)} %get-tuple-element.144.refs_0_, ...), custom_call_target="tpu_custom_call" | custom-call | tf_op jit(solution)/shard_map/cond/branch_1_fun/pallas_call | solution.py:546
  (195 shorter events, 11.3 us)
Async XLA Ops:
  7.4 36.3 %collective-permute-start.21 = (f32[8,2048]{1,0:T(8,128)S(1)}, f32[8,2048]{1,0:T(8,128)S(1)}, u32[]{:S(2)}, u32[]{:S(2)}) collective-permute-start(f32[8,2048]{1,0:T(8,128)S(1)} %get-tuple-element.234), channel_id=1, source_target_pairs={{8,0},{16,8},{24,16},{9,1},{17,9},{25,17},{10,2},{18,10},{26,18},{... | collective-permute-start | bytes 196616 | tf_op jit(solution)/shard_map/ppermute | solution.py:37
  8.7 35.0 %collective-permute-start.20 = (f32[8,2048]{1,0:T(8,128)S(1)}, f32[8,2048]{1,0:T(8,128)S(1)}, u32[]{:S(2)}, u32[]{:S(2)}) collective-permute-start(f32[8,2048]{1,0:T(8,128)S(1)} %get-tuple-element.235), channel_id=1, source_target_pairs={{0,8},{8,16},{16,24},{1,9},{9,17},{17,25},{2,10},{10,18},{18,26},{... | collective-permute-start | bytes 196616 | tf_op jit(solution)/shard_map/ppermute | solution.py:37
  16.0 9.9 %copy-start.1 = (f32[16384]{0:T(1024)S(1)}, f32[16384]{0:T(1024)}, u32[]{:S(2)}) copy-start(f32[16384]{0:T(1024)} %param.20) | copy-start | bytes 196612
  16.0 9.9 %copy-start.2 = (f32[16384]{0:T(1024)S(1)}, f32[16384]{0:T(1024)}, u32[]{:S(2)}) copy-start(f32[16384]{0:T(1024)} %param.19) | copy-start | bytes 196612
  16.0 9.9 %copy-start.7 = (s32[16384]{0:T(1024)S(1)}, s32[16384]{0:T(1024)}, u32[]{:S(2)}) copy-start(s32[16384]{0:T(1024)} %param.21) | copy-start | bytes 196612
  16.0 10.3 %copy-start.17 = (s32[2,512]{1,0:T(2,128)S(1)}, s32[2,512]{1,0:T(2,128)}, u32[]{:S(2)}) copy-start(s32[2,512]{1,0:T(2,128)} %param.22) | copy-start | bytes 12292
  16.0 10.3 %copy-start.18 = (s32[2,512]{1,0:T(2,128)S(1)}, s32[2,512]{1,0:T(2,128)}, u32[]{:S(2)}) copy-start(s32[2,512]{1,0:T(2,128)} %param.23) | copy-start | bytes 12292
  16.0 10.4 %copy-start.3 = (f32[16384]{0:T(1024)S(1)}, f32[16384]{0:T(1024)}, u32[]{:S(2)}) copy-start(f32[16384]{0:T(1024)} %param.17) | copy-start | bytes 196612
  16.0 10.4 %copy-start.4 = (f32[16384]{0:T(1024)S(1)}, f32[16384]{0:T(1024)}, u32[]{:S(2)}) copy-start(f32[16384]{0:T(1024)} %param.16) | copy-start | bytes 196612
  16.0 10.4 %copy-start.8 = (s32[16384]{0:T(1024)S(1)}, s32[16384]{0:T(1024)}, u32[]{:S(2)}) copy-start(s32[16384]{0:T(1024)} %param.18) | copy-start | bytes 196612
  18.4 13.8 %collective-permute-start.22 = (f32[4096,2]{0,1:T(2,128)S(1)}, f32[4096,2]{0,1:T(2,128)S(1)}, u32[]{:S(2)}, u32[]{:S(2)}) collective-permute-start(f32[4096,2]{0,1:T(2,128)S(1)} %copy.68), channel_id=1, source_target_pairs={{1,0},{2,1},{3,2},{4,3},{5,4},{6,5},{7,6},{9,8},{10,9},{11,10},{12... | collective-permute-start | bytes 98312 | tf_op jit(solution)/shard_map/ppermute | solution.py:37
  20.3 11.9 %collective-permute-start.23 = (f32[4096,2]{0,1:T(2,128)S(1)}, f32[4096,2]{0,1:T(2,128)S(1)}, u32[]{:S(2)}, u32[]{:S(2)}) collective-permute-start(f32[4096,2]{0,1:T(2,128)S(1)} %copy.69), channel_id=1, source_target_pairs={{0,1},{1,2},{2,3},{3,4},{4,5},{5,6},{6,7},{8,9},{9,10},{10,11},{11... | collective-permute-start | bytes 98312 | tf_op jit(solution)/shard_map/ppermute | solution.py:37
  29.6 7.6 %copy-start.9 = (s32[1024]{0:T(1024)}, s32[1024]{0:T(1024)S(1)}, u32[]{:S(2)}) copy-start(s32[1024]{0:T(1024)S(1)} %get-tuple-element.215) | copy-start | bytes 12292
  29.6 7.6 %copy-start.11 = (s32[1024]{0:T(1024)}, s32[1024]{0:T(1024)S(1)}, u32[]{:S(2)}) copy-start(s32[1024]{0:T(1024)S(1)} %get-tuple-element.216) | copy-start | bytes 12292
  32.3 4.9 collective-permute-start.25
  33.6 4.4 collective-permute-start.24
  43.5 0.7 copy-start.10
  43.5 0.7 copy-start.12
  43.5 0.7 copy-start.14
  51.9 0.6 copy-start.15
  126.4 31.4 %collective-permute-start.6 = (f32[80,4096]{1,0:T(8,128)}, f32[80,4096]{1,0:T(8,128)}, u32[]{:S(2)}, u32[]{:S(2)}) collective-permute-start(f32[80,4096]{1,0:T(8,128)} %get-tuple-element.144.refs_0_), channel_id=1, source_target_pairs={{0,2},{2,4},{4,6},{6,7},{7,5},{5,3},{3,1},{1,0},{8,10},{10,12},{12... | collective-permute-start | bytes 3932168 | tf_op jit(solution)/shard_map/cond/branch_1_fun/ppermute | solution.py:573
  127.9 31.6 %collective-permute-start.13 = (f32[80,4096]{1,0:T(8,128)}, f32[80,4096]{1,0:T(8,128)}, u32[]{:S(2)}, u32[]{:S(2)}) collective-permute-start(f32[80,4096]{1,0:T(8,128)} %get-tuple-element.145.refs_8_), channel_id=1, source_target_pairs={{2,0},{4,2},{6,4},{7,6},{5,7},{3,5},{1,3},{0,1},{10,8},{12,10},{14... | collective-permute-start | bytes 3932168 | tf_op jit(solution)/shard_map/cond/branch_1_fun/ppermute | solution.py:574
  144.1 21.0 %copy-start = (f32[304,2048]{1,0:T(8,128)}, f32[304,2048]{1,0:T(8,128)S(1)}, u32[]{:S(2)}) copy-start(f32[304,2048]{1,0:T(8,128)S(1)} %gather_fusion) | copy-start | bytes 7471108 | tf_op jit(solution)/shard_map/cond
  144.1 5.9 %copy-start.20 = (s32[8]{0:T(128)S(1)}, s32[8]{0:T(128)}, u32[]{:S(2)}) copy-start(s32[8]{0:T(128)} %constant.140.clone.1) | copy-start | bytes 100 | tf_op jit(solution)/shard_map/cond
  144.1 6.6 %copy-start.19 = (s32[4]{0:T(128)S(1)}, s32[4]{0:T(128)}, u32[]{:S(2)}) copy-start(s32[4]{0:T(128)} %constant.139.clone.1) | copy-start | bytes 52 | tf_op jit(solution)/shard_map/cond
  145.9 19.1 %collective-permute-start.1 = (f32[160,304]{1,0:T(8,128)S(1)}, f32[160,304]{1,0:T(8,128)S(1)}, u32[]{:S(2)}, u32[]{:S(2)}) collective-permute-start(f32[160,304]{1,0:T(8,128)S(1)} %fusion.10), channel_id=1, source_target_pairs={{0,8},{8,0},{16,24},{24,16},{1,9},{9,1},{17,25},{25,17},{2,10},{10... | collective-permute-start | bytes 583688 | tf_op jit(solution)/shard_map/cond/branch_1_fun/ppermute | solution.py:591
  147.4 16.9 %collective-permute-start = (f32[160,304]{1,0:T(8,128)S(1)}, f32[160,304]{1,0:T(8,128)S(1)}, u32[]{:S(2)}, u32[]{:S(2)}) collective-permute-start(f32[160,304]{1,0:T(8,128)S(1)} %fusion.10), channel_id=1, source_target_pairs={{0,16},{8,24},{16,0},{24,8},{1,17},{9,25},{17,1},{25,9},{2,18},{10... | collective-permute-start | bytes 583688 | tf_op jit(solution)/shard_map/cond/branch_1_fun/ppermute | solution.py:591
  149.9 274.5 %collective-permute-start.4 = (f32[304,2048]{1,0:T(8,128)S(1)}, f32[304,2048]{1,0:T(8,128)}, u32[]{:S(2)}, u32[]{:S(2)}) collective-permute-start(f32[304,2048]{1,0:T(8,128)S(1)} %gather_fusion), channel_id=1, source_target_pairs={{0,8},{8,0},{16,24},{24,16},{1,9},{9,1},{17,25},{25,17},{2,10},{10... | collective-permute-start | bytes 7471112 | tf_op jit(solution)/shard_map/cond/branch_1_fun/ppermute | solution.py:591
  151.5 10.7 %copy-start.13 = (s32[1024]{0:T(1024)}, s32[1024]{0:T(1024)S(1)}, u32[]{:S(2)}) copy-start(s32[1024]{0:T(1024)S(1)} %get-tuple-element.231) | copy-start | bytes 12292 | tf_op jit(solution)/shard_map/cond
  154.2 10.3 %copy-start.16 = (f32[2,512]{1,0:T(2,128)S(1)}, f32[2,512]{1,0:T(2,128)}, u32[]{:S(2)}) copy-start(f32[2,512]{1,0:T(2,128)} %copy-done.15) | copy-start | bytes 12292 | tf_op jit(solution)/shard_map/cond
  157.8 32.1 %collective-permute-start.7 = (f32[80,4096]{1,0:T(8,128)}, f32[80,4096]{1,0:T(8,128)}, u32[]{:S(2)}, u32[]{:S(2)}) collective-permute-start(f32[80,4096]{1,0:T(8,128)} %collective-permute-done.6.refs_1_), channel_id=1, source_target_pairs={{0,2},{2,4},{4,6},{6,7},{7,5},{5,3},{3,1},{1,0},{8,10},{10,12},{12... | collective-permute-start | bytes 3932168 | tf_op jit(solution)/shard_map/cond/branch_1_fun/ppermute | solution.py:573
  159.5 31.5 %collective-permute-start.14 = (f32[80,4096]{1,0:T(8,128)}, f32[80,4096]{1,0:T(8,128)}, u32[]{:S(2)}, u32[]{:S(2)}) collective-permute-start(f32[80,4096]{1,0:T(8,128)} %collective-permute-done.13.refs_9_), channel_id=1, source_target_pairs={{2,0},{4,2},{6,4},{7,6},{5,7},{3,5},{1,3},{0,1},{10,8},{12,10},{14... | collective-permute-start | bytes 3932168 | tf_op jit(solution)/shard_map/cond/branch_1_fun/ppermute | solution.py:574
  164.2 2.7 copy-start.6
  164.2 2.7 collective-permute-start.2
  165.1 1.9 copy-start.5
  165.1 172.9 %collective-permute-start.3 = (f32[304,2048]{1,0:T(8,128)S(1)}, f32[304,2048]{1,0:T(8,128)}, u32[]{:S(2)}, u32[]{:S(2)}) collective-permute-start(f32[304,2048]{1,0:T(8,128)S(1)} %gather_fusion), channel_id=1, source_target_pairs={{0,16},{8,24},{16,0},{24,8},{1,17},{9,25},{17,1},{25,9},{2,18},{10... | collective-permute-start | bytes 7471112 | tf_op jit(solution)/shard_map/cond/branch_1_fun/ppermute | solution.py:591
  189.8 89.9 %collective-permute-start.8 = (f32[80,4096]{1,0:T(8,128)}, f32[80,4096]{1,0:T(8,128)}, u32[]{:S(2)}, u32[]{:S(2)}) collective-permute-start(f32[80,4096]{1,0:T(8,128)} %collective-permute-done.7.refs_2_), channel_id=1, source_target_pairs={{0,2},{2,4},{4,6},{6,7},{7,5},{5,3},{3,1},{1,0},{8,10},{10,12},{12... | collective-permute-start | bytes 3932168 | tf_op jit(solution)/shard_map/cond/branch_1_fun/ppermute | solution.py:573
  191.0 90.9 %collective-permute-start.15 = (f32[80,4096]{1,0:T(8,128)}, f32[80,4096]{1,0:T(8,128)}, u32[]{:S(2)}, u32[]{:S(2)}) collective-permute-start(f32[80,4096]{1,0:T(8,128)} %collective-permute-done.14.refs_10_), channel_id=1, source_target_pairs={{2,0},{4,2},{6,4},{7,6},{5,7},{3,5},{1,3},{0,1},{10,8},{12,10},{14... | collective-permute-start | bytes 3932168 | tf_op jit(solution)/shard_map/cond/branch_1_fun/ppermute | solution.py:574
  279.7 58.4 %collective-permute-start.9 = (f32[80,4096]{1,0:T(8,128)}, f32[80,4096]{1,0:T(8,128)}, u32[]{:S(2)}, u32[]{:S(2)}) collective-permute-start(f32[80,4096]{1,0:T(8,128)} %collective-permute-done.8.refs_3_), channel_id=1, source_target_pairs={{0,2},{2,4},{4,6},{6,7},{7,5},{5,3},{3,1},{1,0},{8,10},{10,12},{12... | collective-permute-start | bytes 3932168 | tf_op jit(solution)/shard_map/cond/branch_1_fun/ppermute | solution.py:573
  281.9 57.7 %collective-permute-start.16 = (f32[80,4096]{1,0:T(8,128)}, f32[80,4096]{1,0:T(8,128)}, u32[]{:S(2)}, u32[]{:S(2)}) collective-permute-start(f32[80,4096]{1,0:T(8,128)} %collective-permute-done.15.refs_11_), channel_id=1, source_target_pairs={{2,0},{4,2},{6,4},{7,6},{5,7},{3,5},{1,3},{0,1},{10,8},{12,10},{14... | collective-permute-start | bytes 3932168 | tf_op jit(solution)/shard_map/cond/branch_1_fun/ppermute | solution.py:574
  338.0 86.3 %collective-permute-start.5 = (f32[304,2048]{1,0:T(8,128)}, f32[304,2048]{1,0:T(8,128)}, u32[]{:S(2)}, u32[]{:S(2)}) collective-permute-start(f32[304,2048]{1,0:T(8,128)} %collective-permute-done.3.refs_1_), channel_id=1, source_target_pairs={{0,8},{8,0},{16,24},{24,16},{1,9},{9,1},{17,25},{25,17},{2,10},{10... | collective-permute-start | bytes 7471112 | tf_op jit(solution)/shard_map/cond/branch_1_fun/ppermute | solution.py:591
  338.1 48.8 %collective-permute-start.10 = (f32[80,4096]{1,0:T(8,128)}, f32[80,4096]{1,0:T(8,128)}, u32[]{:S(2)}, u32[]{:S(2)}) collective-permute-start(f32[80,4096]{1,0:T(8,128)} %collective-permute-done.9.refs_4_), channel_id=1, source_target_pairs={{0,2},{2,4},{4,6},{6,7},{7,5},{5,3},{3,1},{1,0},{8,10},{10,12},{12... | collective-permute-start | bytes 3932168 | tf_op jit(solution)/shard_map/cond/branch_1_fun/ppermute | solution.py:573
  339.6 48.8 %collective-permute-start.17 = (f32[80,4096]{1,0:T(8,128)}, f32[80,4096]{1,0:T(8,128)}, u32[]{:S(2)}, u32[]{:S(2)}) collective-permute-start(f32[80,4096]{1,0:T(8,128)} %collective-permute-done.16.refs_12_), channel_id=1, source_target_pairs={{2,0},{4,2},{6,4},{7,6},{5,7},{3,5},{1,3},{0,1},{10,8},{12,10},{14... | collective-permute-start | bytes 3932168 | tf_op jit(solution)/shard_map/cond/branch_1_fun/ppermute | solution.py:574
  386.9 35.4 %collective-permute-start.11 = (f32[80,4096]{1,0:T(8,128)}, f32[80,4096]{1,0:T(8,128)}, u32[]{:S(2)}, u32[]{:S(2)}) collective-permute-start(f32[80,4096]{1,0:T(8,128)} %collective-permute-done.10.refs_5_), channel_id=1, source_target_pairs={{0,2},{2,4},{4,6},{6,7},{7,5},{5,3},{3,1},{1,0},{8,10},{10,12},{12... | collective-permute-start | bytes 3932168 | tf_op jit(solution)/shard_map/cond/branch_1_fun/ppermute | solution.py:573
  388.4 35.4 %collective-permute-start.18 = (f32[80,4096]{1,0:T(8,128)}, f32[80,4096]{1,0:T(8,128)}, u32[]{:S(2)}, u32[]{:S(2)}) collective-permute-start(f32[80,4096]{1,0:T(8,128)} %collective-permute-done.17.refs_13_), channel_id=1, source_target_pairs={{2,0},{4,2},{6,4},{7,6},{5,7},{3,5},{1,3},{0,1},{10,8},{12,10},{14... | collective-permute-start | bytes 3932168 | tf_op jit(solution)/shard_map/cond/branch_1_fun/ppermute | solution.py:574
  422.3 34.5 %collective-permute-start.12 = (f32[80,4096]{1,0:T(8,128)}, f32[80,4096]{1,0:T(8,128)}, u32[]{:S(2)}, u32[]{:S(2)}) collective-permute-start(f32[80,4096]{1,0:T(8,128)} %collective-permute-done.11.refs_6_), channel_id=1, source_target_pairs={{0,2},{2,4},{4,6},{6,7},{7,5},{5,3},{3,1},{1,0},{8,10},{10,12},{12... | collective-permute-start | bytes 3932168 | tf_op jit(solution)/shard_map/cond/branch_1_fun/ppermute | solution.py:573
  423.8 33.0 %collective-permute-start.19 = (f32[80,4096]{1,0:T(8,128)}, f32[80,4096]{1,0:T(8,128)}, u32[]{:S(2)}, u32[]{:S(2)}) collective-permute-start(f32[80,4096]{1,0:T(8,128)} %collective-permute-done.18.refs_14_), channel_id=1, source_target_pairs={{2,0},{4,2},{6,4},{7,6},{5,7},{3,5},{1,3},{0,1},{10,8},{12,10},{14... | collective-permute-start | bytes 3932168 | tf_op jit(solution)/shard_map/cond/branch_1_fun/ppermute | solution.py:574

commit v2 on v1

--- a/solution.py
+++ b/solution.py
@@ -12,7 +12,8 @@
 LANES = 128
 TILE = 128
 HIGHEST = lax.Precision.HIGHEST
-HIGH = lax.Precision.HIGH
+LAST = 4
+SCALE = 1.5
 
 
 def coefficients(courant, diffusion, wind, first_cell, before, after, count):
@@ -204,7 +205,7 @@
         out_shape=[jax.ShapeDtypeStruct(*out) for out in outs],
         scratch_shapes=[pltpu.VMEM(*entry) for entry in scratch],
         cost_estimate=pl.CostEstimate(
-            flops=int(cost * 9e8), bytes_accessed=1 << 20, transcendentals=0
+            flops=int(cost * SCALE * 1e9), bytes_accessed=1 << 20, transcendentals=0
         ),
         compiler_params=pltpu.CompilerParams(vmem_limit_bytes=60 << 20),
     )(*args)
@@ -281,7 +282,7 @@
 
     def fine_more(state):
         index, norm = state
-        return (index < 60) & jnp.logical_not(norm < 1e-7)
+        return (index < 60) & jnp.logical_not(norm < 1e-5)
 
     def fine_step(state):
         index, norm = state
@@ -434,7 +435,7 @@
     columns = pl.ds(pl.multiple_of(core * side, side), side)
 
     def slot(way, step):
-        return slotted.at[pl.ds((way * size + step) * half, half), columns]
+        return slotted.at[pl.ds((2 * step + way) * half, half), columns]
 
     def source(way, step):
         if step == 0:
@@ -468,7 +469,7 @@
             copy.start()
             sides.append(copy)
             if step == 0:
-                slotted[pl.ds(way * size * half, half), columns] = known[
+                slotted[pl.ds(way * half, half), columns] = known[
                     pl.ds(way * half, half), columns
                 ]
     for copy in copies.values():
@@ -530,19 +531,24 @@
     panel = jnp.concatenate([part[...] for part in panels], axis=0).T
     coarse, fine = halves(panel)
     wide = min(512, out.shape[1])
-    for first in range(0, out.shape[1], wide):
-        columns = slice(first, first + wide)
+
+    def body(index, carry):
+        columns = pl.ds(pl.multiple_of(index * wide, wide), wide)
         value = plain(coarse, weights_coarse[:, columns])
         value += plain(coarse, weights_fine[:, columns])
         value += plain(fine, weights_coarse[:, columns])
         out[:, columns] = field[:, columns] - value
-
-
-def update(field, weights_coarse, weights_fine, panels):
+        return carry
+
+    lax.fori_loop(0, out.shape[1] // wide, body, 0)
+
+
+def update(field, weights_coarse, weights_fine, panels, piece):
     rows, cols = field.shape
     tall = min(256, rows)
     tile = pl.BlockSpec((tall, cols), lambda i: (i, 0))
-    held = pl.BlockSpec(weights_coarse.shape, lambda i: (0, 0), pipeline_mode=pl.Buffered(1))
+    slots = len(panels) * panels[0].shape[0]
+    held = pl.BlockSpec((slots, cols), lambda i: (piece, 0), pipeline_mode=pl.Buffered(1))
     return pl.pallas_call(
         update_kernel,
         grid=(rows // tall,),
@@ -550,6 +556,9 @@
         + [pl.BlockSpec((p.shape[0], tall), lambda i: (0, i)) for p in panels],
         out_specs=tile,
         out_shape=jax.ShapeDtypeStruct(field.shape, jnp.float32),
+        cost_estimate=pl.CostEstimate(
+            flops=8 * slots * rows * cols, bytes_accessed=8 * rows * cols, transcendentals=0
+        ),
         compiler_params=pltpu.CompilerParams(vmem_limit_bytes=60 << 20),
     )(field, weights_coarse, weights_fine, *panels)
 
@@ -564,7 +573,7 @@
     return list(range(0, size, 2)) + list(range(size - 1 - size % 2, 0, -2))
 
 
-def ring_gather(up_part, down_part, axis):
+def ring_gather(up_part, down_part, axis, after):
     cycle = ring_of(lax.axis_size(axis))
     ahead = [(cycle[i], cycle[(i + 1) % len(cycle)]) for i in range(len(cycle))]
     behind = [(b, a) for a, b in ahead]
@@ -572,7 +581,9 @@
     for _ in range(len(cycle) - 1):
         ups.append(lax.ppermute(ups[-1], axis, ahead))
         downs.append(lax.ppermute(downs[-1], axis, behind))
-    return ups, downs
+        if len(ups) == 2:
+            ups[1], downs[1], after = lax.optimization_barrier((ups[1], downs[1], after))
+    return [part for pair in zip(ups, downs) for part in pair], after
 
 
 def doubling_masks(size):
@@ -649,8 +660,8 @@
     up_step, down_step = (-away) % across_cols, away % across_cols
     col_slot = jnp.where(
         col_rank < half,
-        up_step * half + col_rank,
-        (across_cols + down_step) * half + col_rank - half,
+        2 * up_step * half + col_rank,
+        2 * down_step * half + col_rank,
     )
     spots = one_hot(row_slot, across_rows * row_slots)
     place = one_hot(col_slot, across_cols * col_slots)
@@ -662,30 +673,93 @@
     )
     pieces = doubling_gather(crossing, "row")
     known = exact(jnp.concatenate(pieces, axis=1), spots.astype(jnp.float32).T)
+    row_part, known = lax.optimization_barrier((row_part, known))
     slotted = crossing_gather(known)
     panels = doubling_gather(row_part, "row")
-    up_panels, down_panels = ring_gather(up_part, down_part, "col")
+    parts, slotted = ring_gather(up_part, down_part, "col", slotted)
     gain_coarse, gain_fine = gain(slotted, place, spots, place.T, error_var)
     weights = weights_of(gain_coarse, gain_fine, panels)
-    return update(field, *weights, up_panels + down_panels)
+    last = len(parts) // LAST
+    field = update(field, *weights, parts[:-last], 0)
+    return update(field, *weights, parts[-last:], LAST - 1)
+
+
+def added_up(value, axis):
+    size, reach = lax.axis_size(axis), 1
+    while reach < size:
+        pairs = [(i, i ^ reach) for i in range(size)]
+        value = value + lax.ppermute(value, axis, pairs)
+        reach *= 2
+    return value
+
+
+def product_kernel(left, right, out):
+    out[...] = exact(left[...], right[...])
+
+
+def product(left, right):
+    (rows, depth), cols = left.shape, right.shape[1]
+    tall, wide = min(128, rows), min(128, cols)
+    return pl.pallas_call(
+        product_kernel,
+        grid=(rows // tall, cols // wide),
+        in_specs=[
+            pl.BlockSpec((tall, depth), lambda i, j: (i, 0)),
+            pl.BlockSpec((depth, wide), lambda i, j: (0, j)),
+        ],
+        out_specs=pl.BlockSpec((tall, wide), lambda i, j: (i, j)),
+        out_shape=jax.ShapeDtypeStruct((rows, cols), jnp.float32),
+    )(left, right)
+
+
+def newton(matrix):
+    unit = jnp.eye(matrix.shape[0], dtype=jnp.float32)
+
+    def more(state):
+        index, _, norm = state
+        return (index < 60) & jnp.logical_not(norm < 1e-7)
+
+    def step(state):
+        index, inverse, _ = state
+        error = unit - product(matrix, inverse)
+        return index + 1, inverse + product(inverse, error), jnp.sum(error * error)
+
+    inverse = unit / jnp.max(jnp.sum(jnp.abs(matrix), axis=0))
+    return lax.while_loop(more, step, (jnp.int32(0), inverse, jnp.float32(1.0)))[1]
 
 
 def crowded(prior, prepared, row_sites, col_sites, error_var, row_place, col_place):
     rows, cols = prior.shape
     row_first = lax.axis_index("row") * rows
     col_first = lax.axis_index("col") * cols
+    k = error_var.shape[1]
     chooser = one_hot(col_sites - col_first, cols)
     field, picked = transport(prior, prepared, chooser, 1)
     row_part = pick_rows(field, row_sites, row_first)
-    crossing = lax.dot_general(
-        chooser.astype(jnp.float32), row_part, (((1,), (1,)), ((), ())), precision=HIGHEST
-    )
-    crossing = lax.psum(crossing, ("row", "col"))
-    row_panel = lax.psum(row_part, "row")
-    column_panel = lax.psum(picked, "col")
-    same = jnp.eye(row_sites.size, dtype=jnp.bfloat16)
-    weights = weights_of(*gain(crossing, same, same, same, error_var), [row_panel])
-    return update(field, *weights, [column_panel])
+    crossing = product(row_part, chooser.astype(jnp.float32).T)
+    crossing = added_up(added_up(crossing, "row"), "col")
+    row_panel = added_up(row_part, "row")
+    column_panel = added_up(picked, "col")
+
+    def body(b, state):
+        crossing, row_panel, column_panel, field = state
+        mine = b * k
+        block = lax.dynamic_slice(crossing, (mine, mine), (k, k))
+        variance = lax.dynamic_index_in_dim(error_var, b, 0, keepdims=False)
+        inverse = newton(jnp.diag(variance) + product(block, block.T))
+        picked_rows = lax.dynamic_slice_in_dim(row_panel, mine, k, axis=0)
+        picked_cols = lax.dynamic_slice_in_dim(column_panel, mine, k, axis=0).T
+        weights = product(inverse, picked_rows)
+        field = field - product(picked_cols, weights)
+        cross_rows = lax.dynamic_slice_in_dim(crossing, mine, k, axis=0)
+        cross_cols = lax.dynamic_slice_in_dim(crossing, mine, k, axis=1)
+        row_panel = row_panel - product(cross_cols, weights)
+        gains = product(inverse, cross_rows)
+        column_panel = column_panel - product(gains.T, picked_cols.T)
+        return crossing - product(cross_cols, gains), row_panel, column_panel, field
+
+    state = (crossing, row_panel, column_panel, field)
+    return lax.fori_loop(0, error_var.shape[0], body, state)[3]
 
 
 def shards(

time: 546 us -> 546 us (level)
  Pallas kernels: 395 us -> 420 us
  waiting for transfers between devices: 26 us -> 11.4 us
  between operations: 15.9 us -> 3.59 us
    pallas_call x1 -> x2, Pallas kernels: 75.8 us -> 120 us  [update(): pl.pallas_call(update_kernel, grid=(rows // tall,), in_specs=[tile, held,...]
    ppermute x7, waiting for transfers between devices: 25 us -> 9.72 us  [ring_gather(): ups.append(lax.ppermute(ups[-1], axis, ahead))]
    pallas_call x1, Pallas kernels: 63.3 us -> 53.9 us  [crossing_gather(): pl.pallas_call(crossing_kernel, in_specs=[whole], out_specs=whole, out_sh...]
    pallas_call x5, Pallas kernels: 153 us -> 144 us  [whole_call(): pl.pallas_call(kernel, in_specs=[whole] * len(args), out_specs=[whole] *...]
  transfers between devices with their start and end apart: 26 -> 26, of which waited for: 4 -> 3; matrix products, arithmetic and copies ran while one was open for 10% -> 6% of each run, Pallas kernels for 46% -> 57%
where the time goes in v2:
time: 546 us; the launch traced here: 538 us
  Pallas kernels  420 us (77%)
  starting transfers between devices  36.8 us (7%)
  local copies, waits for them, and re-layouts  33.9 us (6%)
  other arithmetic  17.5 us (3%)
  waiting for transfers between devices  11.4 us (2%)
  matrix products  7.56 us (1%)
  loops' own time  6.43 us (1%)
    pallas_call x5, Pallas kernels, whole_call(): pl.pallas_call(kernel, in_specs=[whole] * len(args), out_specs=[whole] *...  144 us
    pallas_call x2, Pallas kernels, update(): pl.pallas_call(update_kernel, grid=(rows // tall,), in_specs=[tile, held,...  120 us
    pallas_call x1, Pallas kernels, transport(): pl.pallas_call(transport_kernel, grid=(tiles,), in_specs=[pl.BlockSpec((T...  70.3 us
    pallas_call x1, Pallas kernels, crossing_gather(): pl.pallas_call(crossing_kernel, in_specs=[whole], out_specs=whole, out_sh...  53.9 us
    pallas_call x1, Pallas kernels, weights_of(): pl.pallas_call(weights_kernel, grid=(cols // wide,), in_specs=[held, held...  32.5 us
    ppermute x6, starting transfers between devices, edges(): return (lax.ppermute(last, axis, up), lax.ppermute(leading, axis, down))  16 us
    gather x1, local copies, waits for them, and re-layouts, balanced(): row_part = field[my_rows]  15.4 us
  transfers between devices with their start and end apart: 26, of which 3 were waited for; matrix products, arithmetic and copies ran while one was open for 6% of the time, Pallas kernels for 57%

profile of v2, /device:TPU:0, one launch (start us, length us, event | category | flops | bytes accessed | tf_op | source)
XLA Modules:
  0.0 537.6 jit_solution(9260811400282061552)
XLA Ops:
  0.0 0.9 fusion.46
  0.9 1.3 collective-permute-start.31
  2.2 3.0 collective-permute-start.30
  5.2 4.2 fusion.45
  9.5 2.3 copy.96
  11.8 1.3 collective-permute-start.32
  13.8 5.5 %collective-permute-start.33 = (f32[4096,2]{0,1:T(2,128)S(1)}, f32[4096,2]{0,1:T(2,128)S(1)}, u32[]{:S(2)}, u32[]{:S(2)}) collective-permute-start(f32[4096,2]{0,1:T(2,128)S(1)} %copy.97), channel_id=1, source_target_pairs={{0,1},{1,2},{2,3},{3,4},{4,5},{5,6},{6,7},{8,9},{9,10},{10,11},{11... | collective-permute-start | bytes 98312 | tf_op jit(solution)/shard_map/ppermute | solution.py:38
  20.9 2.1 convert_reduce_fusion
  25.9 1.3 collective-permute-start.35
  27.2 3.6 collective-permute-start.34
  32.5 2.0 copy.92
  34.5 2.2 pad_maximum_fusion.1
  37.4 498.8 %conditional.1 = (f32[4096,2048]{1,0:T(8,128)}) conditional(s32[]{:T(128)} %convert_element_type.50, (s32[1024]{0:T(1024)S(1)}, s32[1024]{0:T(1024)S(1)}, f32[4096,2048]{1,0:T(8,128)}, f32[8,2048]{1,0:T(8,128)S(1)}, f32[8,2048]{1,0:T(8,128)S(1)}, /*index=5*/f32[32,144,128]{2,1,0:T(8,128)S(1)}, f32[32,144,8]{1,0,2:T(8,128)S(1)}, ...), branch_computations={%region_4.12_spmd, %region_12.18_spmd} | conditional | flops 275123470336 | bytes 1123367424 | solution.py:792
  43.4 1.3 fusion.29
  44.9 0.7 select_reduce_fusion.2
  46.7 1.0 fusion.13.chooser
  47.7 2.2 copy.95.row_weights
  49.9 70.3 %branch_1_fun.10 = (f32[4096,2048]{1,0:T(8,128)}, f32[80,4096]{1,0:T(8,128)}, f32[80,4096]{1,0:T(8,128)}) custom-call(f32[4096,2048]{1,0:T(8,128)} %get-tuple-element.244.main.prev.follow, f32[4096,2048]{1,0:T(8,128)} %get-tuple-element.244.main.prev.follow, f32[4096,2048]{1,0:T(8,128)} %get-tuple-element.244.main.prev.follow, ...), custom_call_target="tpu_custom_call" | custom-call | tf_op jit(solution)/shard_map/cond/branch_1_fun/pallas_call | solution.py:119
  120.2 15.4 %gather_fusion = f32[304,2048]{1,0:T(8,128)} fusion(f32[4096,2048]{1,0:T(8,128)} %get-tuple-element.258.field, s32[1024]{0:T(1024)S(1)} %pad_clamp_fusion), kind=kCustom, calls=%fused_computation.1 | custom fusion | bytes 4981952 | tf_op jit(solution)/shard_map/cond/branch_1_fun/gather | solution.py:670
  135.6 3.5 fusion.12
  139.1 1.7 collective-permute-start.3
  140.8 2.2 collective-permute-start.2
  143.1 1.6 collective-permute-start
  144.7 1.0 collective-permute-start.1
  145.7 2.7 fusion.10.back
  148.4 2.0 fusion.9.place
  150.5 2.0 fusion.7.spots
  153.1 0.9 collective-permute-done.4
  154.3 4.1 fusion.8.known
  158.7 53.9 %branch_1_fun.11.slotted = f32[1280,1024]{1,0:T(8,128)} custom-call(f32[160,1024]{1,0:T(8,128)} %fusion.8.known), custom_call_target="tpu_custom_call" | custom-call | tf_op jit(solution)/shard_map/cond/branch_1_fun/pallas_call | solution.py:485
  212.6 2.1 collective-permute-start.8
  215.4 17.5 %branch_1_fun.12.g = f32[1024,1024]{1,0:T(8,128)} custom-call(f32[1280,1024]{1,0:T(8,128)} %branch_1_fun.11.slotted, bf16[1024,1280]{1,0:T(8,128)(2,1)} %fusion.9.place), custom_call_target="tpu_custom_call" | custom-call | flops 22499999744 | bytes 1048576 | tf_op jit(solution)/shard_map/cond/branch_1_fun/pallas_call | solution.py:201
  232.9 2.3 slice.405.block
  235.2 9.7 %collective-permute-done.8.refs_4_ = f32[80,4096]{1,0:T(8,128)S(1)} collective-permute-done((f32[80,4096]{1,0:T(8,128)}, f32[80,4096]{1,0:T(8,128)S(1)}, u32[]{:S(2)}, u32[]{:S(2)}) %collective-permute-start.8) | collective-permute-done | bytes 1310752 | tf_op jit(solution)/shard_map/cond/branch_1_fun/ppermute | solution.py:582
  244.9 1.1 collective-permute-start.10
  246.0 1.4 collective-permute-start.11
  247.4 42.1 %branch_1_fun.13.x0 = f32[512,512]{1,0:T(8,128)} custom-call(f32[512,512]{1,0:T(8,128)} %slice.405.block, f32[1,512]{1,0:T(1,128)} %get-tuple-element.443.variance), custom_call_target="tpu_custom_call" | custom-call | flops 44999999488 | bytes 1048576 | tf_op jit(solution)/shard_map/cond/branch_1_fun/pallas_call | solution.py:201
  289.4 9.1 %branch_1_fun.14 = (f32[512,512]{1,0:T(8,128)}, f32[512,512]{1,0:T(8,128)}) custom-call(f32[1024,1024]{1,0:T(8,128)} %branch_1_fun.12.g, f32[512,512]{1,0:T(8,128)} %branch_1_fun.13.x0), custom_call_target="tpu_custom_call" | custom-call | flops 12000000000 | bytes 1048576 | tf_op jit(solution)/shard_map/cond/branch_1_fun/pallas_call | solution.py:201
  299.2 1.4 collective-permute-start.13
  300.6 41.9 %branch_1_fun.15.x1 = f32[512,512]{1,0:T(8,128)} custom-call(f32[512,512]{1,0:T(8,128)} %get-tuple-element.272.block, f32[1,512]{1,0:T(1,128)} %get-tuple-element.442.variance), custom_call_target="tpu_custom_call" | custom-call | flops 44999999488 | bytes 1048576 | tf_op jit(solution)/shard_map/cond/branch_1_fun/pallas_call | solution.py:201
  343.1 1.4 collective-permute-start.15
  344.6 33.4 %branch_1_fun.16 = (bf16[1280,1216]{1,0:T(8,128)(2,1)}, bf16[1280,1216]{1,0:T(8,128)(2,1)}) custom-call(f32[1024,1024]{1,0:T(8,128)} %branch_1_fun.12.g, f32[512,512]{1,0:T(8,128)} %branch_1_fun.13.x0, f32[512,512]{1,0:T(8,128)} %branch_1_fun.15.x1, f32[512,512]{1,0:T(8,128)} %get-tuple-element.273.carry, bf16[1024,1216]{1,0:T(8,128)(2,1)} %fusion.7.spots, ...), custom_call_target="tpu_custom_call" | custom-call | flops 41999998976 | bytes 1048576 | tf_op jit(solution)/shard_map/cond/branch_1_fun/pallas_call | solution.py:201
  378.6 1.7 collective-permute-start.17
  380.3 32.5 %branch_1_fun.17 = (bf16[1280,2048]{1,0:T(8,128)(2,1)}, bf16[1280,2048]{1,0:T(8,128)(2,1)}) custom-call(bf16[1280,1216]{1,0:T(8,128)(2,1)} %get-tuple-element.274.gain_coarse, bf16[1280,1216]{1,0:T(8,128)(2,1)} %get-tuple-element.275.gain_fine, f32[304,2048]{1,0:T(8,128)} %gather_fusion, f32[304,2048]{1,0:T(8,128)} %collective-permute-done.5.refs_1_, ...), custom_call_target="tpu_custom_call" | custom-call | flops 19126026240 | bytes 31457280 | tf_op jit(solution)/shard_map/cond/branch_1_fun/pallas_call | solution.py:513
  413.5 1.4 collective-permute-start.19
  414.9 75.9 %branch_1_fun.18.field = f32[4096,2048]{1,0:T(8,128)} custom-call(f32[4096,2048]{1,0:T(8,128)} %get-tuple-element.258.field, bf16[1280,2048]{1,0:T(8,128)(2,1)} %get-tuple-element.277.weights_coarse, bf16[1280,2048]{1,0:T(8,128)(2,1)} %get-tuple-element.278.weights_fine, f32[80,4096]{1,0:T(8,128)} %get-tuple-element.259.refs_0_, ...), custom_call_target="tpu_custom_call" | custom-call | flops 64424509440 | bytes 67108864 | tf_op jit(solution)/shard_map/cond/branch_1_fun/pallas_call | solution.py:552
  490.8 1.1 copy-done.4
  491.9 44.0 %branch_1_fun.19 = f32[4096,2048]{1,0:T(8,128)} custom-call(f32[4096,2048]{1,0:T(8,128)} %branch_1_fun.18.field, bf16[1280,2048]{1,0:T(8,128)(2,1)} %get-tuple-element.277.weights_coarse, bf16[1280,2048]{1,0:T(8,128)(2,1)} %get-tuple-element.278.weights_fine, f32[80,4096]{1,0:T(8,128)} %copy-done.2, f32[80,4096]{1,0:T(8,128)} %copy-done.3, ...), custom_call_target="tpu_custom_call" | custom-call | flops 21474836480 | bytes 67108864 | tf_op jit(solution)/shard_map/cond/branch_1_fun/pallas_call | solution.py:552
  (200 shorter events, 11.5 us)
Async XLA Ops:
  0.9 36.5 %collective-permute-start.31 = (f32[8,2048]{1,0:T(8,128)S(1)}, f32[8,2048]{1,0:T(8,128)S(1)}, u32[]{:S(2)}, u32[]{:S(2)}) collective-permute-start(f32[8,2048]{1,0:T(8,128)S(1)} %get-tuple-element.448), channel_id=1, source_target_pairs={{8,0},{16,8},{24,16},{9,1},{17,9},{25,17},{10,2},{18,10},{26,18},{... | collective-permute-start | bytes 196616 | tf_op jit(solution)/shard_map/ppermute | solution.py:38
  2.2 35.2 %collective-permute-start.30 = (f32[8,2048]{1,0:T(8,128)S(1)}, f32[8,2048]{1,0:T(8,128)S(1)}, u32[]{:S(2)}, u32[]{:S(2)}) collective-permute-start(f32[8,2048]{1,0:T(8,128)S(1)} %get-tuple-element.449), channel_id=1, source_target_pairs={{0,8},{8,16},{16,24},{1,9},{9,17},{17,25},{2,10},{10,18},{18,26},{... | collective-permute-start | bytes 196616 | tf_op jit(solution)/shard_map/ppermute | solution.py:38
  9.4 9.9 %copy-start.5 = (f32[16384]{0:T(1024)S(1)}, f32[16384]{0:T(1024)}, u32[]{:S(2)}) copy-start(f32[16384]{0:T(1024)} %param.24) | copy-start | bytes 196612
  9.5 9.9 %copy-start.6 = (f32[16384]{0:T(1024)S(1)}, f32[16384]{0:T(1024)}, u32[]{:S(2)}) copy-start(f32[16384]{0:T(1024)} %param.23) | copy-start | bytes 196612
  9.5 9.9 %copy-start.9 = (s32[16384]{0:T(1024)S(1)}, s32[16384]{0:T(1024)}, u32[]{:S(2)}) copy-start(s32[16384]{0:T(1024)} %param.25) | copy-start | bytes 196612
  9.5 10.3 %copy-start.16 = (s32[2,512]{1,0:T(2,128)S(1)}, s32[2,512]{1,0:T(2,128)}, u32[]{:S(2)}) copy-start(s32[2,512]{1,0:T(2,128)} %param.26) | copy-start | bytes 12292
  9.5 10.3 %copy-start.17 = (s32[2,512]{1,0:T(2,128)S(1)}, s32[2,512]{1,0:T(2,128)}, u32[]{:S(2)}) copy-start(s32[2,512]{1,0:T(2,128)} %param.27) | copy-start | bytes 12292
  9.5 10.4 %copy-start.7 = (f32[16384]{0:T(1024)S(1)}, f32[16384]{0:T(1024)}, u32[]{:S(2)}) copy-start(f32[16384]{0:T(1024)} %param.21) | copy-start | bytes 196612
  9.5 10.4 %copy-start.8 = (f32[16384]{0:T(1024)S(1)}, f32[16384]{0:T(1024)}, u32[]{:S(2)}) copy-start(f32[16384]{0:T(1024)} %param.20) | copy-start | bytes 196612
  9.5 10.4 %copy-start.10 = (s32[16384]{0:T(1024)S(1)}, s32[16384]{0:T(1024)}, u32[]{:S(2)}) copy-start(s32[16384]{0:T(1024)} %param.22) | copy-start | bytes 196612
  11.8 14.0 %collective-permute-start.32 = (f32[4096,2]{0,1:T(2,128)S(1)}, f32[4096,2]{0,1:T(2,128)S(1)}, u32[]{:S(2)}, u32[]{:S(2)}) collective-permute-start(f32[4096,2]{0,1:T(2,128)S(1)} %copy.96), channel_id=1, source_target_pairs={{1,0},{2,1},{3,2},{4,3},{5,4},{6,5},{7,6},{9,8},{10,9},{11,10},{12... | collective-permute-start | bytes 98312 | tf_op jit(solution)/shard_map/ppermute | solution.py:38
  13.8 12.1 %collective-permute-start.33 = (f32[4096,2]{0,1:T(2,128)S(1)}, f32[4096,2]{0,1:T(2,128)S(1)}, u32[]{:S(2)}, u32[]{:S(2)}) collective-permute-start(f32[4096,2]{0,1:T(2,128)S(1)} %copy.97), channel_id=1, source_target_pairs={{0,1},{1,2},{2,3},{3,4},{4,5},{5,6},{6,7},{8,9},{9,10},{10,11},{11... | collective-permute-start | bytes 98312 | tf_op jit(solution)/shard_map/ppermute | solution.py:38
  23.0 7.8 %copy-start.12 = (s32[1024]{0:T(1024)}, s32[1024]{0:T(1024)S(1)}, u32[]{:S(2)}) copy-start(s32[1024]{0:T(1024)S(1)} %get-tuple-element.408) | copy-start | bytes 12292
  23.0 7.8 %copy-start.14 = (s32[1024]{0:T(1024)}, s32[1024]{0:T(1024)S(1)}, u32[]{:S(2)}) copy-start(s32[1024]{0:T(1024)S(1)} %get-tuple-element.409) | copy-start | bytes 12292
  25.9 4.9 collective-permute-start.35
  27.2 4.4 collective-permute-start.34
  36.7 0.8 copy-start.11
  36.7 0.8 copy-start.13
  135.6 14.8 %copy-start.18 = (s32[4]{0:T(128)S(1)}, s32[4]{0:T(128)}, u32[]{:S(2)}) copy-start(s32[4]{0:T(128)} %constant.211.clone.1) | copy-start | bytes 52 | tf_op jit(solution)/shard_map/cond
  139.1 13.9 %collective-permute-start.3 = (f32[160,304]{1,0:T(8,128)S(1)}, f32[160,304]{1,0:T(8,128)S(1)}, u32[]{:S(2)}, u32[]{:S(2)}) collective-permute-start(f32[160,304]{1,0:T(8,128)S(1)} %fusion.12), channel_id=1, source_target_pairs={{0,8},{8,0},{16,24},{24,16},{1,9},{9,1},{17,25},{25,17},{2,10},{10... | collective-permute-start | bytes 583688 | tf_op jit(solution)/shard_map/cond/branch_1_fun/ppermute | solution.py:602
  140.8 11.6 %collective-permute-start.2 = (f32[160,304]{1,0:T(8,128)S(1)}, f32[160,304]{1,0:T(8,128)S(1)}, u32[]{:S(2)}, u32[]{:S(2)}) collective-permute-start(f32[160,304]{1,0:T(8,128)S(1)} %fusion.12), channel_id=1, source_target_pairs={{0,16},{8,24},{16,0},{24,8},{1,17},{9,25},{17,1},{25,9},{2,18},{10... | collective-permute-start | bytes 583688 | tf_op jit(solution)/shard_map/cond/branch_1_fun/ppermute | solution.py:602
  143.1 69.5 %collective-permute-start = (f32[80,4096]{1,0:T(8,128)}, f32[80,4096]{1,0:T(8,128)}, u32[]{:S(2)}, u32[]{:S(2)}) collective-permute-start(f32[80,4096]{1,0:T(8,128)} %get-tuple-element.259.refs_0_), channel_id=1, source_target_pairs={{0,2},{2,4},{4,6},{6,7},{7,5},{5,3},{3,1},{1,0},{8,10},{10,12},{12... | collective-permute-start | bytes 3932168 | tf_op jit(solution)/shard_map/cond/branch_1_fun/ppermute | solution.py:582
  144.7 67.9 %collective-permute-start.1 = (f32[80,4096]{1,0:T(8,128)}, f32[80,4096]{1,0:T(8,128)}, u32[]{:S(2)}, u32[]{:S(2)}) collective-permute-start(f32[80,4096]{1,0:T(8,128)} %get-tuple-element.260.refs_1_), channel_id=1, source_target_pairs={{2,0},{4,2},{6,4},{7,6},{5,7},{3,5},{1,3},{0,1},{10,8},{12,10},{14... | collective-permute-start | bytes 3932168 | tf_op jit(solution)/shard_map/cond/branch_1_fun/ppermute | solution.py:583
  152.5 1.5 collective-permute-start.4
  158.4 221.9 %collective-permute-start.6 = (f32[304,2048]{1,0:T(8,128)}, f32[304,2048]{1,0:T(8,128)}, u32[]{:S(2)}, u32[]{:S(2)}) collective-permute-start(f32[304,2048]{1,0:T(8,128)} %gather_fusion), channel_id=1, source_target_pairs={{0,8},{8,0},{16,24},{24,16},{1,9},{9,1},{17,25},{25,17},{2,10},{10... | collective-permute-start | bytes 7471112 | tf_op jit(solution)/shard_map/cond/branch_1_fun/ppermute | solution.py:602
  158.5 183.9 %collective-permute-start.5 = (f32[304,2048]{1,0:T(8,128)}, f32[304,2048]{1,0:T(8,128)}, u32[]{:S(2)}, u32[]{:S(2)}) collective-permute-start(f32[304,2048]{1,0:T(8,128)} %gather_fusion), channel_id=1, source_target_pairs={{0,16},{8,24},{16,0},{24,8},{1,17},{9,25},{17,1},{25,9},{2,18},{10... | collective-permute-start | bytes 7471112 | tf_op jit(solution)/shard_map/cond/branch_1_fun/ppermute | solution.py:602
  212.6 32.3 %collective-permute-start.8 = (f32[80,4096]{1,0:T(8,128)}, f32[80,4096]{1,0:T(8,128)S(1)}, u32[]{:S(2)}, u32[]{:S(2)}) collective-permute-start(f32[80,4096]{1,0:T(8,128)} %collective-permute-done.refs_2_), channel_id=1, source_target_pairs={{0,2},{2,4},{4,6},{6,7},{7,5},{5,3},{3,1},{1,0},{8,10},{10,12},{12... | collective-permute-start | bytes 3932168 | tf_op jit(solution)/shard_map/cond/branch_1_fun/ppermute | solution.py:582
  214.7 31.3 %collective-permute-start.9 = (f32[80,4096]{1,0:T(8,128)}, f32[80,4096]{1,0:T(8,128)S(1)}, u32[]{:S(2)}, u32[]{:S(2)}) collective-permute-start(f32[80,4096]{1,0:T(8,128)} %collective-permute-done.1.refs_3_), channel_id=1, source_target_pairs={{2,0},{4,2},{6,4},{7,6},{5,7},{3,5},{1,3},{0,1},{10,8},{12,10},{14... | collective-permute-start | bytes 3932168 | tf_op jit(solution)/shard_map/cond/branch_1_fun/ppermute | solution.py:583
  244.9 44.5 %copy-start.19 = (f32[80,4096]{1,0:T(8,128)}, f32[80,4096]{1,0:T(8,128)S(1)}, u32[]{:S(2)}) copy-start(f32[80,4096]{1,0:T(8,128)S(1)} %collective-permute-done.8.refs_4_) | copy-start | bytes 3932164 | tf_op jit(solution)/shard_map/cond
  244.9 53.6 %collective-permute-start.10 = (f32[80,4096]{1,0:T(8,128)S(1)}, f32[80,4096]{1,0:T(8,128)S(1)}, u32[]{:S(2)}, u32[]{:S(2)}) collective-permute-start(f32[80,4096]{1,0:T(8,128)S(1)} %collective-permute-done.8.refs_4_), channel_id=1, source_target_pairs={{0,2},{2,4},{4,6},{6,7},{7,5},{5,3},{3,1},{1,0},{8,10},{10,12},{12... | collective-permute-start | bytes 3932168 | tf_op jit(solution)/shard_map/cond/branch_1_fun/ppermute | solution.py:582
  246.0 43.5 %copy-start.20 = (f32[80,4096]{1,0:T(8,128)}, f32[80,4096]{1,0:T(8,128)S(1)}, u32[]{:S(2)}) copy-start(f32[80,4096]{1,0:T(8,128)S(1)} %collective-permute-done.9.refs_5_) | copy-start | bytes 3932164 | tf_op jit(solution)/shard_map/cond
  246.0 53.2 %collective-permute-start.11 = (f32[80,4096]{1,0:T(8,128)S(1)}, f32[80,4096]{1,0:T(8,128)}, u32[]{:S(2)}, u32[]{:S(2)}) collective-permute-start(f32[80,4096]{1,0:T(8,128)S(1)} %collective-permute-done.9.refs_5_), channel_id=1, source_target_pairs={{2,0},{4,2},{6,4},{7,6},{5,7},{3,5},{1,3},{0,1},{10,8},{12,10},{14... | collective-permute-start | bytes 3932168 | tf_op jit(solution)/shard_map/cond/branch_1_fun/ppermute | solution.py:583
  298.5 43.9 %copy-start.21 = (f32[80,4096]{1,0:T(8,128)}, f32[80,4096]{1,0:T(8,128)S(1)}, u32[]{:S(2)}) copy-start(f32[80,4096]{1,0:T(8,128)S(1)} %collective-permute-done.10.refs_6_) | copy-start | bytes 3932164 | tf_op jit(solution)/shard_map/cond
  298.5 43.9 %collective-permute-start.12 = (f32[80,4096]{1,0:T(8,128)S(1)}, f32[80,4096]{1,0:T(8,128)S(1)}, u32[]{:S(2)}, u32[]{:S(2)}) collective-permute-start(f32[80,4096]{1,0:T(8,128)S(1)} %collective-permute-done.10.refs_6_), channel_id=1, source_target_pairs={{0,2},{2,4},{4,6},{6,7},{7,5},{5,3},{3,1},{1,0},{8,10},{10,12},{12... | collective-permute-start | bytes 3932168 | tf_op jit(solution)/shard_map/cond/branch_1_fun/ppermute | solution.py:582
  299.2 44.0 %collective-permute-start.13 = (f32[80,4096]{1,0:T(8,128)}, f32[80,4096]{1,0:T(8,128)S(1)}, u32[]{:S(2)}, u32[]{:S(2)}) collective-permute-start(f32[80,4096]{1,0:T(8,128)} %collective-permute-done.11.refs_7_), channel_id=1, source_target_pairs={{2,0},{4,2},{6,4},{7,6},{5,7},{3,5},{1,3},{0,1},{10,8},{12,10},{14... | collective-permute-start | bytes 3932168 | tf_op jit(solution)/shard_map/cond/branch_1_fun/ppermute | solution.py:583
  342.4 37.9 %collective-permute-start.7 = (f32[304,2048]{1,0:T(8,128)}, f32[304,2048]{1,0:T(8,128)}, u32[]{:S(2)}, u32[]{:S(2)}) collective-permute-start(f32[304,2048]{1,0:T(8,128)} %collective-permute-done.5.refs_1_), channel_id=1, source_target_pairs={{0,8},{8,0},{16,24},{24,16},{1,9},{9,1},{17,25},{25,17},{2,10},{10... | collective-permute-start | bytes 7471112 | tf_op jit(solution)/shard_map/cond/branch_1_fun/ppermute | solution.py:602
  342.4 35.5 %copy-start.22 = (f32[80,4096]{1,0:T(8,128)}, f32[80,4096]{1,0:T(8,128)S(1)}, u32[]{:S(2)}) copy-start(f32[80,4096]{1,0:T(8,128)S(1)} %collective-permute-done.12.refs_8_) | copy-start | bytes 3932164 | tf_op jit(solution)/shard_map/cond
  342.5 35.5 %collective-permute-start.14 = (f32[80,4096]{1,0:T(8,128)S(1)}, f32[80,4096]{1,0:T(8,128)S(1)}, u32[]{:S(2)}, u32[]{:S(2)}) collective-permute-start(f32[80,4096]{1,0:T(8,128)S(1)} %collective-permute-done.12.refs_8_), channel_id=1, source_target_pairs={{0,2},{2,4},{4,6},{6,7},{7,5},{5,3},{3,1},{1,0},{8,10},{10,12},{12... | collective-permute-start | bytes 3932168 | tf_op jit(solution)/shard_map/cond/branch_1_fun/ppermute | solution.py:582
  343.1 34.8 %copy-start.23 = (f32[80,4096]{1,0:T(8,128)}, f32[80,4096]{1,0:T(8,128)S(1)}, u32[]{:S(2)}) copy-start(f32[80,4096]{1,0:T(8,128)S(1)} %collective-permute-done.13.refs_9_) | copy-start | bytes 3932164 | tf_op jit(solution)/shard_map/cond
  343.1 35.5 %collective-permute-start.15 = (f32[80,4096]{1,0:T(8,128)S(1)}, f32[80,4096]{1,0:T(8,128)}, u32[]{:S(2)}, u32[]{:S(2)}) collective-permute-start(f32[80,4096]{1,0:T(8,128)S(1)} %collective-permute-done.13.refs_9_), channel_id=1, source_target_pairs={{2,0},{4,2},{6,4},{7,6},{5,7},{3,5},{1,3},{0,1},{10,8},{12,10},{14... | collective-permute-start | bytes 3932168 | tf_op jit(solution)/shard_map/cond/branch_1_fun/ppermute | solution.py:583
  377.9 34.9 %copy-start.24 = (f32[80,4096]{1,0:T(8,128)}, f32[80,4096]{1,0:T(8,128)S(1)}, u32[]{:S(2)}) copy-start(f32[80,4096]{1,0:T(8,128)S(1)} %collective-permute-done.14.refs_10_) | copy-start | bytes 3932164 | tf_op jit(solution)/shard_map/cond
  377.9 34.9 %collective-permute-start.16 = (f32[80,4096]{1,0:T(8,128)S(1)}, f32[80,4096]{1,0:T(8,128)S(1)}, u32[]{:S(2)}, u32[]{:S(2)}) collective-permute-start(f32[80,4096]{1,0:T(8,128)S(1)} %collective-permute-done.14.refs_10_), channel_id=1, source_target_pairs={{0,2},{2,4},{4,6},{6,7},{7,5},{5,3},{3,1},{1,0},{8,10},{10,12},{12... | collective-permute-start | bytes 3932168 | tf_op jit(solution)/shard_map/cond/branch_1_fun/ppermute | solution.py:582
  378.6 34.8 %collective-permute-start.17 = (f32[80,4096]{1,0:T(8,128)}, f32[80,4096]{1,0:T(8,128)S(1)}, u32[]{:S(2)}, u32[]{:S(2)}) collective-permute-start(f32[80,4096]{1,0:T(8,128)} %collective-permute-done.15.refs_11_), channel_id=1, source_target_pairs={{2,0},{4,2},{6,4},{7,6},{5,7},{3,5},{1,3},{0,1},{10,8},{12,10},{14... | collective-permute-start | bytes 3932168 | tf_op jit(solution)/shard_map/cond/branch_1_fun/ppermute | solution.py:583
  412.8 78.0 %copy-start.2 = (f32[80,4096]{1,0:T(8,128)}, f32[80,4096]{1,0:T(8,128)S(1)}, u32[]{:S(2)}) copy-start(f32[80,4096]{1,0:T(8,128)S(1)} %collective-permute-done.16.refs_0_) | copy-start | bytes 3932164 | tf_op jit(solution)/shard_map/cond
  412.8 78.0 %collective-permute-start.18 = (f32[80,4096]{1,0:T(8,128)S(1)}, f32[80,4096]{1,0:T(8,128)S(1)}, u32[]{:S(2)}, u32[]{:S(2)}) collective-permute-start(f32[80,4096]{1,0:T(8,128)S(1)} %collective-permute-done.16.refs_0_), channel_id=1, source_target_pairs={{0,2},{2,4},{4,6},{6,7},{7,5},{5,3},{3,1},{1,0},{8,10},{10,12},{12... | collective-permute-start | bytes 3932168 | tf_op jit(solution)/shard_map/cond/branch_1_fun/ppermute | solution.py:582
  413.5 77.3 %copy-start.3 = (f32[80,4096]{1,0:T(8,128)}, f32[80,4096]{1,0:T(8,128)S(1)}, u32[]{:S(2)}) copy-start(f32[80,4096]{1,0:T(8,128)S(1)} %collective-permute-done.17.refs_1_) | copy-start | bytes 3932164 | tf_op jit(solution)/shard_map/cond
  413.5 77.3 %collective-permute-start.19 = (f32[80,4096]{1,0:T(8,128)S(1)}, f32[80,4096]{1,0:T(8,128)}, u32[]{:S(2)}, u32[]{:S(2)}) collective-permute-start(f32[80,4096]{1,0:T(8,128)S(1)} %collective-permute-done.17.refs_1_), channel_id=1, source_target_pairs={{2,0},{4,2},{6,4},{7,6},{5,7},{3,5},{1,3},{0,1},{10,8},{12,10},{14... | collective-permute-start | bytes 3932168 | tf_op jit(solution)/shard_map/cond/branch_1_fun/ppermute | solution.py:583
  490.8 1.1 copy-start.4
  (1 other events, 0.8 us)

commit v3 on v2

--- a/solution.py
+++ b/solution.py
@@ -170,7 +170,7 @@
 
 
 def chunk(count):
-    return 128 if count % 128 == 0 else 16
+    return next(n for n in (512, 640, 256, 128, 16) if count % n == 0)
 
 
 def below(rows, first):
@@ -383,17 +383,17 @@
         [((3, slots, both), jnp.bfloat16)],
         slotted,
         place,
-        cost=15,
+        cost=17,
     )
 
     def inverse(block, b):
         scratch = [square, terms, terms, terms]
         return whole_call(
-            invert_kernel, [square], scratch, block, variance[b : b + 1], cost=30
+            invert_kernel, [square], scratch, block, variance[b : b + 1], cost=21
         )[0]
 
     x0 = inverse(g[:k, :k], 0)
-    carry, block = whole_call(deflate_kernel, [square, square], [terms, terms], g, x0, cost=8)
+    carry, block = whole_call(deflate_kernel, [square, square], [terms, terms], g, x0, cost=7)
     x1 = inverse(block, 1)
     out = ((slots, spots.shape[1]), jnp.bfloat16)
     return whole_call(
@@ -406,7 +406,7 @@
         carry,
         spots,
         back,
-        cost=28,
+        cost=26,
     )
 
 
@@ -501,7 +501,7 @@
         value += plain(gain_coarse[rows, :], fine) + plain(gain_fine[rows, :], coarse)
         coarse_out[rows, :], fine_out[rows, :] = halves(value)
 
-    by_rows(gain_coarse.shape[0], 16 * (gain_coarse.shape[0] // 64), write)
+    by_rows(gain_coarse.shape[0], gain_coarse.shape[0], write)
 
 
 def weights_of(gain_coarse, gain_fine, panels):
@@ -532,15 +532,12 @@
     coarse, fine = halves(panel)
     wide = min(512, out.shape[1])
 
-    def body(index, carry):
-        columns = pl.ds(pl.multiple_of(index * wide, wide), wide)
+    for index in range(out.shape[1] // wide):
+        columns = pl.ds(index * wide, wide)
         value = plain(coarse, weights_coarse[:, columns])
         value += plain(coarse, weights_fine[:, columns])
         value += plain(fine, weights_coarse[:, columns])
         out[:, columns] = field[:, columns] - value
-        return carry
-
-    lax.fori_loop(0, out.shape[1] // wide, body, 0)
 
 
 def update(field, weights_coarse, weights_fine, panels, piece):

time: 546 us -> 476 us (0.87)
  Pallas kernels: 420 us -> 348 us
    pallas_call x5, Pallas kernels: 144 us -> 98.8 us  [whole_call(): pl.pallas_call(kernel, in_specs=[whole] * len(args), out_specs=[whole] *...]
    pallas_call x2, Pallas kernels: 120 us -> 99.9 us  [update(): pl.pallas_call(update_kernel, grid=(rows // tall,), in_specs=[tile, held,...]
    ppermute x7, waiting for transfers between devices: 9.72 us -> 15.8 us  [ring_gather(): ups.append(lax.ppermute(ups[-1], axis, ahead))]
    pallas_call x1, Pallas kernels: 32.5 us -> 26.7 us  [weights_of(): pl.pallas_call(weights_kernel, grid=(cols // wide,), in_specs=[held, held...]
  transfers between devices with their start and end apart: 26 -> 26, of which waited for: 3 -> 5; matrix products, arithmetic and copies ran while one was open for 6% -> 7% of each run, Pallas kernels for 57% -> 51%
where the time goes in v3:
time: 476 us; the launch traced here: 471 us
  Pallas kernels  348 us (73%)
  starting transfers between devices  37 us (8%)
  local copies, waits for them, and re-layouts  36.4 us (8%)
  other arithmetic  17.5 us (4%)
  waiting for transfers between devices  16.8 us (4%)
  matrix products  6.52 us (1%)
  loops' own time  6.06 us (1%)
    pallas_call x2, Pallas kernels, update(): pl.pallas_call(update_kernel, grid=(rows // tall,), in_specs=[tile, held,...  99.9 us
    pallas_call x5, Pallas kernels, whole_call(): pl.pallas_call(kernel, in_specs=[whole] * len(args), out_specs=[whole] *...  98.8 us
    pallas_call x1, Pallas kernels, transport(): pl.pallas_call(transport_kernel, grid=(tiles,), in_specs=[pl.BlockSpec((T...  70.4 us
    pallas_call x1, Pallas kernels, crossing_gather(): pl.pallas_call(crossing_kernel, in_specs=[whole], out_specs=whole, out_sh...  52 us
    pallas_call x1, Pallas kernels, weights_of(): pl.pallas_call(weights_kernel, grid=(cols // wide,), in_specs=[held, held...  26.7 us
    ppermute x6, starting transfers between devices, edges(): return (lax.ppermute(last, axis, up), lax.ppermute(leading, axis, down))  16 us
    ppermute x7, waiting for transfers between devices, ring_gather(): ups.append(lax.ppermute(ups[-1], axis, ahead))  15.8 us
    gather x1, local copies, waits for them, and re-layouts, balanced(): row_part = field[my_rows]  14.8 us
  transfers between devices with their start and end apart: 26, of which 5 were waited for; matrix products, arithmetic and copies ran while one was open for 7% of the time, Pallas kernels for 51%

profile of v3, /device:TPU:0, one launch (start us, length us, event | category | flops | bytes accessed | tf_op | source)
XLA Modules:
  0.0 471.2 jit_solution(13704222605738587147)
XLA Ops:
  0.9 1.3 collective-permute-start.31
  2.2 3.0 collective-permute-start.30
  5.2 4.2 fusion.45
  9.5 2.3 copy.96
  11.8 1.3 collective-permute-start.32
  13.8 5.5 %collective-permute-start.33 = (f32[4096,2]{0,1:T(2,128)S(1)}, f32[4096,2]{0,1:T(2,128)S(1)}, u32[]{:S(2)}, u32[]{:S(2)}) collective-permute-start(f32[4096,2]{0,1:T(2,128)S(1)} %copy.97), channel_id=1, source_target_pairs={{0,1},{1,2},{2,3},{3,4},{4,5},{5,6},{6,7},{8,9},{9,10},{10,11},{11... | collective-permute-start | bytes 98312 | tf_op jit(solution)/shard_map/ppermute | solution.py:38
  20.9 2.1 convert_reduce_fusion
  25.8 1.3 collective-permute-start.35
  27.1 3.6 collective-permute-start.34
  32.3 2.0 copy.92
  34.3 2.2 pad_maximum_fusion.1
  37.3 432.8 %conditional.1 = (f32[4096,2048]{1,0:T(8,128)}) conditional(s32[]{:T(128)} %convert_element_type.50, (s32[1024]{0:T(1024)S(1)}, s32[1024]{0:T(1024)S(1)}, f32[4096,2048]{1,0:T(8,128)}, f32[8,2048]{1,0:T(8,128)S(1)}, f32[8,2048]{1,0:T(8,128)S(1)}, /*index=5*/f32[32,144,128]{2,1,0:T(8,128)S(1)}, f32[32,144,8]{1,0,2:T(8,128)S(1)}, ...), branch_computations={%region_4.12_spmd, %region_12.18_spmd} | conditional | flops 246623453184 | bytes 1123367424 | solution.py:789
  42.9 1.3 fusion.29
  46.2 1.0 fusion.13.chooser
  47.3 2.2 copy.95.row_weights
  49.4 70.4 %branch_1_fun.10 = (f32[4096,2048]{1,0:T(8,128)}, f32[80,4096]{1,0:T(8,128)}, f32[80,4096]{1,0:T(8,128)}) custom-call(f32[4096,2048]{1,0:T(8,128)} %get-tuple-element.244.main.prev.follow, f32[4096,2048]{1,0:T(8,128)} %get-tuple-element.244.main.prev.follow, f32[4096,2048]{1,0:T(8,128)} %get-tuple-element.244.main.prev.follow, ...), custom_call_target="tpu_custom_call" | custom-call | tf_op jit(solution)/shard_map/cond/branch_1_fun/pallas_call | solution.py:119
  119.8 14.8 %gather_fusion = f32[304,2048]{1,0:T(8,128)S(1)} fusion(f32[4096,2048]{1,0:T(8,128)} %get-tuple-element.258.field, s32[1024]{0:T(1024)S(1)} %pad_clamp_fusion), kind=kCustom, calls=%fused_computation.1 | custom fusion | bytes 4981952 | tf_op jit(solution)/shard_map/cond/branch_1_fun/gather | solution.py:667
  134.7 1.8 fusion.12
  136.5 1.7 collective-permute-start.3
  138.2 2.2 collective-permute-start.2
  140.4 1.6 collective-permute-start
  142.0 1.2 collective-permute-start.1
  143.2 2.7 fusion.10.back
  145.9 2.0 fusion.9.place
  148.0 2.0 fusion.7.spots
  151.6 1.5 concatenate.18
  153.2 4.7 %fusion.8.known = f32[160,1024]{1,0:T(8,128)} fusion(f32[160,1216]{1,0:T(8,128)S(1)} %concatenate.18, s32[1024]{0:T(1024)} %copy-done.18), kind=kOutput, calls=%fused_computation.29 | convolution fusion | flops 2391998464 | bytes 1437696 | tf_op jit(solution)/shard_map/cond/branch_1_fun/dot_general | solution.py:154
  158.2 52.0 %branch_1_fun.11.slotted = f32[1280,1024]{1,0:T(8,128)} custom-call(f32[160,1024]{1,0:T(8,128)} %fusion.8.known), custom_call_target="tpu_custom_call" | custom-call | tf_op jit(solution)/shard_map/cond/branch_1_fun/pallas_call | solution.py:485
  210.3 1.8 collective-permute-start.8
  212.0 1.1 collective-permute-start.9
  213.2 16.4 %branch_1_fun.12.g = f32[1024,1024]{1,0:T(8,128)} custom-call(f32[1280,1024]{1,0:T(8,128)} %branch_1_fun.11.slotted, bf16[1024,1280]{1,0:T(8,128)(2,1)} %fusion.9.place), custom_call_target="tpu_custom_call" | custom-call | flops 25500000256 | bytes 1048576 | tf_op jit(solution)/shard_map/cond/branch_1_fun/pallas_call | solution.py:201
  229.5 2.3 slice.405.block
  231.8 10.9 %collective-permute-done.8.refs_4_ = f32[80,4096]{1,0:T(8,128)} collective-permute-done((f32[80,4096]{1,0:T(8,128)}, f32[80,4096]{1,0:T(8,128)}, u32[]{:S(2)}, u32[]{:S(2)}) %collective-permute-start.8) | collective-permute-done | bytes 1310752 | tf_op jit(solution)/shard_map/cond/branch_1_fun/ppermute | solution.py:579
  243.4 1.7 collective-permute-start.11
  245.1 24.5 %branch_1_fun.13.x0 = f32[512,512]{1,0:T(8,128)} custom-call(f32[512,512]{1,0:T(8,128)} %slice.405.block, f32[1,512]{1,0:T(1,128)} %get-tuple-element.443.variance), custom_call_target="tpu_custom_call" | custom-call | flops 31499999232 | bytes 1048576 | tf_op jit(solution)/shard_map/cond/branch_1_fun/pallas_call | solution.py:201
  269.6 6.9 %branch_1_fun.14 = (f32[512,512]{1,0:T(8,128)}, f32[512,512]{1,0:T(8,128)}) custom-call(f32[1024,1024]{1,0:T(8,128)} %branch_1_fun.12.g, f32[512,512]{1,0:T(8,128)} %branch_1_fun.13.x0), custom_call_target="tpu_custom_call" | custom-call | flops 10499999744 | bytes 1048576 | tf_op jit(solution)/shard_map/cond/branch_1_fun/pallas_call | solution.py:201
  277.0 1.6 collective-permute-start.13
  278.6 24.6 %branch_1_fun.15.x1 = f32[512,512]{1,0:T(8,128)} custom-call(f32[512,512]{1,0:T(8,128)} %get-tuple-element.272.block, f32[1,512]{1,0:T(1,128)} %get-tuple-element.442.variance), custom_call_target="tpu_custom_call" | custom-call | flops 31499999232 | bytes 1048576 | tf_op jit(solution)/shard_map/cond/branch_1_fun/pallas_call | solution.py:201
  303.2 3.8 collective-permute-done.12.refs_8_
  307.3 1.9 collective-permute-start.15
  309.2 26.4 %branch_1_fun.16 = (bf16[1280,1216]{1,0:T(8,128)(2,1)}, bf16[1280,1216]{1,0:T(8,128)(2,1)}) custom-call(f32[1024,1024]{1,0:T(8,128)} %branch_1_fun.12.g, f32[512,512]{1,0:T(8,128)} %branch_1_fun.13.x0, f32[512,512]{1,0:T(8,128)} %branch_1_fun.15.x1, f32[512,512]{1,0:T(8,128)} %get-tuple-element.273.carry, bf16[1024,1216]{1,0:T(8,128)(2,1)} %fusion.7.spots, ...), custom_call_target="tpu_custom_call" | custom-call | flops 38999998464 | bytes 1048576 | tf_op jit(solution)/shard_map/cond/branch_1_fun/pallas_call | solution.py:201
  336.9 1.7 collective-permute-start.17
  338.7 26.7 %branch_1_fun.17 = (bf16[1280,2048]{1,0:T(8,128)(2,1)}, bf16[1280,2048]{1,0:T(8,128)(2,1)}) custom-call(bf16[1280,1216]{1,0:T(8,128)(2,1)} %get-tuple-element.274.gain_coarse, bf16[1280,1216]{1,0:T(8,128)(2,1)} %get-tuple-element.275.gain_fine, f32[304,2048]{1,0:T(8,128)} %copy-done.2, f32[304,2048]{1,0:T(8,128)} %collective-permute-done.5.refs_1_, ...), custom_call_target="tpu_custom_call" | custom-call | flops 19126026240 | bytes 31457280 | tf_op jit(solution)/shard_map/cond/branch_1_fun/pallas_call | solution.py:513
  365.8 2.0 collective-permute-start.19
  367.7 61.8 %branch_1_fun.18.field = f32[4096,2048]{1,0:T(8,128)} custom-call(f32[4096,2048]{1,0:T(8,128)} %get-tuple-element.258.field, bf16[1280,2048]{1,0:T(8,128)(2,1)} %get-tuple-element.277.weights_coarse, bf16[1280,2048]{1,0:T(8,128)(2,1)} %get-tuple-element.278.weights_fine, f32[80,4096]{1,0:T(8,128)} %get-tuple-element.259.refs_0_, ...), custom_call_target="tpu_custom_call" | custom-call | flops 64424509440 | bytes 67108864 | tf_op jit(solution)/shard_map/cond/branch_1_fun/pallas_call | solution.py:549
  429.5 1.0 copy-done.3
  430.6 1.1 copy-done.4
  431.6 38.1 %branch_1_fun.19 = f32[4096,2048]{1,0:T(8,128)} custom-call(f32[4096,2048]{1,0:T(8,128)} %branch_1_fun.18.field, bf16[1280,2048]{1,0:T(8,128)(2,1)} %get-tuple-element.277.weights_coarse, bf16[1280,2048]{1,0:T(8,128)(2,1)} %get-tuple-element.278.weights_fine, f32[80,4096]{1,0:T(8,128)} %collective-permute-done.16.refs_0_, ...), custom_call_target="tpu_custom_call" | custom-call | flops 21474836480 | bytes 67108864 | tf_op jit(solution)/shard_map/cond/branch_1_fun/pallas_call | solution.py:549
  (194 shorter events, 13.6 us)
Async XLA Ops:
  0.9 36.3 %collective-permute-start.31 = (f32[8,2048]{1,0:T(8,128)S(1)}, f32[8,2048]{1,0:T(8,128)S(1)}, u32[]{:S(2)}, u32[]{:S(2)}) collective-permute-start(f32[8,2048]{1,0:T(8,128)S(1)} %get-tuple-element.448), channel_id=1, source_target_pairs={{8,0},{16,8},{24,16},{9,1},{17,9},{25,17},{10,2},{18,10},{26,18},{... | collective-permute-start | bytes 196616 | tf_op jit(solution)/shard_map/ppermute | solution.py:38
  2.2 35.0 %collective-permute-start.30 = (f32[8,2048]{1,0:T(8,128)S(1)}, f32[8,2048]{1,0:T(8,128)S(1)}, u32[]{:S(2)}, u32[]{:S(2)}) collective-permute-start(f32[8,2048]{1,0:T(8,128)S(1)} %get-tuple-element.449), channel_id=1, source_target_pairs={{0,8},{8,16},{16,24},{1,9},{9,17},{17,25},{2,10},{10,18},{18,26},{... | collective-permute-start | bytes 196616 | tf_op jit(solution)/shard_map/ppermute | solution.py:38
  9.4 9.9 %copy-start.5 = (f32[16384]{0:T(1024)S(1)}, f32[16384]{0:T(1024)}, u32[]{:S(2)}) copy-start(f32[16384]{0:T(1024)} %param.24) | copy-start | bytes 196612
  9.5 9.9 %copy-start.6 = (f32[16384]{0:T(1024)S(1)}, f32[16384]{0:T(1024)}, u32[]{:S(2)}) copy-start(f32[16384]{0:T(1024)} %param.23) | copy-start | bytes 196612
  9.5 9.9 %copy-start.11 = (s32[16384]{0:T(1024)S(1)}, s32[16384]{0:T(1024)}, u32[]{:S(2)}) copy-start(s32[16384]{0:T(1024)} %param.25) | copy-start | bytes 196612
  9.5 10.3 %copy-start.19 = (s32[2,512]{1,0:T(2,128)S(1)}, s32[2,512]{1,0:T(2,128)}, u32[]{:S(2)}) copy-start(s32[2,512]{1,0:T(2,128)} %param.26) | copy-start | bytes 12292
  9.5 10.3 %copy-start.20 = (s32[2,512]{1,0:T(2,128)S(1)}, s32[2,512]{1,0:T(2,128)}, u32[]{:S(2)}) copy-start(s32[2,512]{1,0:T(2,128)} %param.27) | copy-start | bytes 12292
  9.5 10.4 %copy-start.7 = (f32[16384]{0:T(1024)S(1)}, f32[16384]{0:T(1024)}, u32[]{:S(2)}) copy-start(f32[16384]{0:T(1024)} %param.21) | copy-start | bytes 196612
  9.5 10.4 %copy-start.8 = (f32[16384]{0:T(1024)S(1)}, f32[16384]{0:T(1024)}, u32[]{:S(2)}) copy-start(f32[16384]{0:T(1024)} %param.20) | copy-start | bytes 196612
  9.5 10.4 %copy-start.12 = (s32[16384]{0:T(1024)S(1)}, s32[16384]{0:T(1024)}, u32[]{:S(2)}) copy-start(s32[16384]{0:T(1024)} %param.22) | copy-start | bytes 196612
  11.8 13.8 %collective-permute-start.32 = (f32[4096,2]{0,1:T(2,128)S(1)}, f32[4096,2]{0,1:T(2,128)S(1)}, u32[]{:S(2)}, u32[]{:S(2)}) collective-permute-start(f32[4096,2]{0,1:T(2,128)S(1)} %copy.96), channel_id=1, source_target_pairs={{1,0},{2,1},{3,2},{4,3},{5,4},{6,5},{7,6},{9,8},{10,9},{11,10},{12... | collective-permute-start | bytes 98312 | tf_op jit(solution)/shard_map/ppermute | solution.py:38
  13.8 11.9 %collective-permute-start.33 = (f32[4096,2]{0,1:T(2,128)S(1)}, f32[4096,2]{0,1:T(2,128)S(1)}, u32[]{:S(2)}, u32[]{:S(2)}) collective-permute-start(f32[4096,2]{0,1:T(2,128)S(1)} %copy.97), channel_id=1, source_target_pairs={{0,1},{1,2},{2,3},{3,4},{4,5},{5,6},{6,7},{8,9},{9,10},{10,11},{11... | collective-permute-start | bytes 98312 | tf_op jit(solution)/shard_map/ppermute | solution.py:38
  23.0 7.7 %copy-start.14 = (s32[1024]{0:T(1024)}, s32[1024]{0:T(1024)S(1)}, u32[]{:S(2)}) copy-start(s32[1024]{0:T(1024)S(1)} %get-tuple-element.408) | copy-start | bytes 12292
  23.0 7.7 %copy-start.16 = (s32[1024]{0:T(1024)}, s32[1024]{0:T(1024)S(1)}, u32[]{:S(2)}) copy-start(s32[1024]{0:T(1024)S(1)} %get-tuple-element.409) | copy-start | bytes 12292
  25.8 4.9 %collective-permute-start.35 = (f32[8,4]{0,1:T(4,128)S(1)}, f32[8,4]{0,1:T(4,128)S(1)}, u32[]{:S(2)}, u32[]{:S(2)}) collective-permute-start(f32[8,4]{0,1:T(4,128)S(1)} %get-tuple-element.456), channel_id=1, source_target_pairs={{8,0},{16,8},{24,16},{9,1},{17,9},{25,17},{10,2},{18,10},{26,18},{... | collective-permute-start | bytes 392 | tf_op jit(solution)/shard_map/ppermute | solution.py:38
  27.1 4.4 collective-permute-start.34
  36.5 0.8 copy-start.13
  36.5 0.8 copy-start.15
  36.5 0.8 copy-start.17
  134.6 23.4 %copy-start.2 = (f32[304,2048]{1,0:T(8,128)}, f32[304,2048]{1,0:T(8,128)S(1)}, u32[]{:S(2)}) copy-start(f32[304,2048]{1,0:T(8,128)S(1)} %gather_fusion) | copy-start | bytes 7471108 | tf_op jit(solution)/shard_map/cond
  134.6 13.3 %copy-start.21 = (s32[4]{0:T(128)S(1)}, s32[4]{0:T(128)}, u32[]{:S(2)}) copy-start(s32[4]{0:T(128)} %constant.211.clone.1) | copy-start | bytes 52 | tf_op jit(solution)/shard_map/cond
  136.5 14.2 %collective-permute-start.3 = (f32[160,304]{1,0:T(8,128)S(1)}, f32[160,304]{1,0:T(8,128)S(1)}, u32[]{:S(2)}, u32[]{:S(2)}) collective-permute-start(f32[160,304]{1,0:T(8,128)S(1)} %fusion.12), channel_id=1, source_target_pairs={{0,8},{8,0},{16,24},{24,16},{1,9},{9,1},{17,25},{25,17},{2,10},{10... | collective-permute-start | bytes 583688 | tf_op jit(solution)/shard_map/cond/branch_1_fun/ppermute | solution.py:599
  138.2 11.8 %collective-permute-start.2 = (f32[160,304]{1,0:T(8,128)S(1)}, f32[160,304]{1,0:T(8,128)S(1)}, u32[]{:S(2)}, u32[]{:S(2)}) collective-permute-start(f32[160,304]{1,0:T(8,128)S(1)} %fusion.12), channel_id=1, source_target_pairs={{0,16},{8,24},{16,0},{24,8},{1,17},{9,25},{17,1},{25,9},{2,18},{10... | collective-permute-start | bytes 583688 | tf_op jit(solution)/shard_map/cond/branch_1_fun/ppermute | solution.py:599
  140.4 69.8 %collective-permute-start = (f32[80,4096]{1,0:T(8,128)}, f32[80,4096]{1,0:T(8,128)}, u32[]{:S(2)}, u32[]{:S(2)}) collective-permute-start(f32[80,4096]{1,0:T(8,128)} %get-tuple-element.259.refs_0_), channel_id=1, source_target_pairs={{0,2},{2,4},{4,6},{6,7},{7,5},{5,3},{3,1},{1,0},{8,10},{10,12},{12... | collective-permute-start | bytes 3932168 | tf_op jit(solution)/shard_map/cond/branch_1_fun/ppermute | solution.py:579
  142.0 68.3 %collective-permute-start.1 = (f32[80,4096]{1,0:T(8,128)}, f32[80,4096]{1,0:T(8,128)}, u32[]{:S(2)}, u32[]{:S(2)}) collective-permute-start(f32[80,4096]{1,0:T(8,128)} %get-tuple-element.260.refs_1_), channel_id=1, source_target_pairs={{2,0},{4,2},{6,4},{7,6},{5,7},{3,5},{1,3},{0,1},{10,8},{12,10},{14... | collective-permute-start | bytes 3932168 | tf_op jit(solution)/shard_map/cond/branch_1_fun/ppermute | solution.py:580
  148.0 2.6 copy-start.18
  150.0 0.7 copy-start.10
  150.0 1.6 collective-permute-start.4
  150.7 0.7 copy-start.9
  157.9 180.8 %collective-permute-start.6 = (f32[304,2048]{1,0:T(8,128)S(1)}, f32[304,2048]{1,0:T(8,128)}, u32[]{:S(2)}, u32[]{:S(2)}) collective-permute-start(f32[304,2048]{1,0:T(8,128)S(1)} %gather_fusion), channel_id=1, source_target_pairs={{0,8},{8,0},{16,24},{24,16},{1,9},{9,1},{17,25},{25,17},{2,10},{10... | collective-permute-start | bytes 7471112 | tf_op jit(solution)/shard_map/cond/branch_1_fun/ppermute | solution.py:599
  158.1 145.1 %collective-permute-start.5 = (f32[304,2048]{1,0:T(8,128)S(1)}, f32[304,2048]{1,0:T(8,128)}, u32[]{:S(2)}, u32[]{:S(2)}) collective-permute-start(f32[304,2048]{1,0:T(8,128)S(1)} %gather_fusion), channel_id=1, source_target_pairs={{0,16},{8,24},{16,0},{24,8},{1,17},{9,25},{17,1},{25,9},{2,18},{10... | collective-permute-start | bytes 7471112 | tf_op jit(solution)/shard_map/cond/branch_1_fun/ppermute | solution.py:599
  210.3 32.4 %collective-permute-start.8 = (f32[80,4096]{1,0:T(8,128)}, f32[80,4096]{1,0:T(8,128)}, u32[]{:S(2)}, u32[]{:S(2)}) collective-permute-start(f32[80,4096]{1,0:T(8,128)} %collective-permute-done.refs_2_), channel_id=1, source_target_pairs={{0,2},{2,4},{4,6},{6,7},{7,5},{5,3},{3,1},{1,0},{8,10},{10,12},{12... | collective-permute-start | bytes 3932168 | tf_op jit(solution)/shard_map/cond/branch_1_fun/ppermute | solution.py:579
  212.0 31.4 %collective-permute-start.9 = (f32[80,4096]{1,0:T(8,128)}, f32[80,4096]{1,0:T(8,128)}, u32[]{:S(2)}, u32[]{:S(2)}) collective-permute-start(f32[80,4096]{1,0:T(8,128)} %collective-permute-done.1.refs_3_), channel_id=1, source_target_pairs={{2,0},{4,2},{6,4},{7,6},{5,7},{3,5},{1,3},{0,1},{10,8},{12,10},{14... | collective-permute-start | bytes 3932168 | tf_op jit(solution)/shard_map/cond/branch_1_fun/ppermute | solution.py:580
  242.7 33.8 %collective-permute-start.10 = (f32[80,4096]{1,0:T(8,128)}, f32[80,4096]{1,0:T(8,128)}, u32[]{:S(2)}, u32[]{:S(2)}) collective-permute-start(f32[80,4096]{1,0:T(8,128)} %collective-permute-done.8.refs_4_), channel_id=1, source_target_pairs={{0,2},{2,4},{4,6},{6,7},{7,5},{5,3},{3,1},{1,0},{8,10},{10,12},{12... | collective-permute-start | bytes 3932168 | tf_op jit(solution)/shard_map/cond/branch_1_fun/ppermute | solution.py:579
  243.4 33.6 %collective-permute-start.11 = (f32[80,4096]{1,0:T(8,128)}, f32[80,4096]{1,0:T(8,128)}, u32[]{:S(2)}, u32[]{:S(2)}) collective-permute-start(f32[80,4096]{1,0:T(8,128)} %collective-permute-done.9.refs_5_), channel_id=1, source_target_pairs={{2,0},{4,2},{6,4},{7,6},{5,7},{3,5},{1,3},{0,1},{10,8},{12,10},{14... | collective-permute-start | bytes 3932168 | tf_op jit(solution)/shard_map/cond/branch_1_fun/ppermute | solution.py:580
  276.5 30.5 %collective-permute-start.12 = (f32[80,4096]{1,0:T(8,128)}, f32[80,4096]{1,0:T(8,128)}, u32[]{:S(2)}, u32[]{:S(2)}) collective-permute-start(f32[80,4096]{1,0:T(8,128)} %collective-permute-done.10.refs_6_), channel_id=1, source_target_pairs={{0,2},{2,4},{4,6},{6,7},{7,5},{5,3},{3,1},{1,0},{8,10},{10,12},{12... | collective-permute-start | bytes 3932168 | tf_op jit(solution)/shard_map/cond/branch_1_fun/ppermute | solution.py:579
  277.0 30.3 %collective-permute-start.13 = (f32[80,4096]{1,0:T(8,128)}, f32[80,4096]{1,0:T(8,128)}, u32[]{:S(2)}, u32[]{:S(2)}) collective-permute-start(f32[80,4096]{1,0:T(8,128)} %collective-permute-done.11.refs_7_), channel_id=1, source_target_pairs={{2,0},{4,2},{6,4},{7,6},{5,7},{3,5},{1,3},{0,1},{10,8},{12,10},{14... | collective-permute-start | bytes 3932168 | tf_op jit(solution)/shard_map/cond/branch_1_fun/ppermute | solution.py:580
  303.2 35.5 %collective-permute-start.7 = (f32[304,2048]{1,0:T(8,128)}, f32[304,2048]{1,0:T(8,128)}, u32[]{:S(2)}, u32[]{:S(2)}) collective-permute-start(f32[304,2048]{1,0:T(8,128)} %collective-permute-done.5.refs_1_), channel_id=1, source_target_pairs={{0,8},{8,0},{16,24},{24,16},{1,9},{9,1},{17,25},{25,17},{2,10},{10... | collective-permute-start | bytes 7471112 | tf_op jit(solution)/shard_map/cond/branch_1_fun/ppermute | solution.py:599
  307.0 29.6 %collective-permute-start.14 = (f32[80,4096]{1,0:T(8,128)}, f32[80,4096]{1,0:T(8,128)}, u32[]{:S(2)}, u32[]{:S(2)}) collective-permute-start(f32[80,4096]{1,0:T(8,128)} %collective-permute-done.12.refs_8_), channel_id=1, source_target_pairs={{0,2},{2,4},{4,6},{6,7},{7,5},{5,3},{3,1},{1,0},{8,10},{10,12},{12... | collective-permute-start | bytes 3932168 | tf_op jit(solution)/shard_map/cond/branch_1_fun/ppermute | solution.py:579
  307.3 29.6 %collective-permute-start.15 = (f32[80,4096]{1,0:T(8,128)}, f32[80,4096]{1,0:T(8,128)}, u32[]{:S(2)}, u32[]{:S(2)}) collective-permute-start(f32[80,4096]{1,0:T(8,128)} %collective-permute-done.13.refs_9_), channel_id=1, source_target_pairs={{2,0},{4,2},{6,4},{7,6},{5,7},{3,5},{1,3},{0,1},{10,8},{12,10},{14... | collective-permute-start | bytes 3932168 | tf_op jit(solution)/shard_map/cond/branch_1_fun/ppermute | solution.py:580
  336.6 28.8 %collective-permute-start.16 = (f32[80,4096]{1,0:T(8,128)}, f32[80,4096]{1,0:T(8,128)}, u32[]{:S(2)}, u32[]{:S(2)}) collective-permute-start(f32[80,4096]{1,0:T(8,128)} %collective-permute-done.14.refs_10_), channel_id=1, source_target_pairs={{0,2},{2,4},{4,6},{6,7},{7,5},{5,3},{3,1},{1,0},{8,10},{10,12},{12... | collective-permute-start | bytes 3932168 | tf_op jit(solution)/shard_map/cond/branch_1_fun/ppermute | solution.py:579
  336.9 28.8 %collective-permute-start.17 = (f32[80,4096]{1,0:T(8,128)}, f32[80,4096]{1,0:T(8,128)}, u32[]{:S(2)}, u32[]{:S(2)}) collective-permute-start(f32[80,4096]{1,0:T(8,128)} %collective-permute-done.15.refs_11_), channel_id=1, source_target_pairs={{2,0},{4,2},{6,4},{7,6},{5,7},{3,5},{1,3},{0,1},{10,8},{12,10},{14... | collective-permute-start | bytes 3932168 | tf_op jit(solution)/shard_map/cond/branch_1_fun/ppermute | solution.py:580
  365.4 64.1 %collective-permute-start.18 = (f32[80,4096]{1,0:T(8,128)}, f32[80,4096]{1,0:T(8,128)S(1)}, u32[]{:S(2)}, u32[]{:S(2)}) collective-permute-start(f32[80,4096]{1,0:T(8,128)} %collective-permute-done.16.refs_0_), channel_id=1, source_target_pairs={{0,2},{2,4},{4,6},{6,7},{7,5},{5,3},{3,1},{1,0},{8,10},{10,12},{12... | collective-permute-start | bytes 3932168 | tf_op jit(solution)/shard_map/cond/branch_1_fun/ppermute | solution.py:579
  365.8 63.8 %collective-permute-start.19 = (f32[80,4096]{1,0:T(8,128)}, f32[80,4096]{1,0:T(8,128)S(1)}, u32[]{:S(2)}, u32[]{:S(2)}) collective-permute-start(f32[80,4096]{1,0:T(8,128)} %collective-permute-done.17.refs_1_), channel_id=1, source_target_pairs={{2,0},{4,2},{6,4},{7,6},{5,7},{3,5},{1,3},{0,1},{10,8},{12,10},{14... | collective-permute-start | bytes 3932168 | tf_op jit(solution)/shard_map/cond/branch_1_fun/ppermute | solution.py:580
  429.5 1.1 copy-start.3
  430.6 1.1 copy-start.4

commit v4 on v3

--- a/solution.py
+++ b/solution.py
@@ -7,7 +7,6 @@
 from jax.sharding import PartitionSpec as P
 
 STEPS = 2
-BATCHES = 2
 MARGIN = 8
 LANES = 128
 TILE = 128
@@ -87,7 +86,6 @@
         ],
         axis=1,
     )
-    extent = TILE + 2 * MARGIN
 
     def windows(values):
         parts = values.reshape((tiles * per + 2, MARGIN) + values.shape[1:])
@@ -103,7 +101,7 @@
     row_weights = jnp.pad(row_weights, ((0, 0), (0, 0), (0, 5)))
     trio = coefficients(*carbon, col_first, STEPS, STEPS, cols)
     rolled = []
-    for index, entry in enumerate(trio):
+    for entry in trio:
         filler = jnp.zeros((LANES - 2 * STEPS,), jnp.float32)
         rolled.append(jnp.concatenate([entry[STEPS:], filler, entry[:STEPS]]))
     col_weights = jnp.pad(jnp.stack(rolled), ((0, 5), (0, 0)))
@@ -146,10 +144,6 @@
     return jnp.dot(first_matrix, second_matrix, preferred_element_type=jnp.float32)
 
 
-def rough(first_matrix, second_matrix):
-    return plain(first_matrix.astype(jnp.bfloat16), second_matrix.astype(jnp.bfloat16))
-
-
 def exact(first_matrix, second_matrix):
     return jnp.dot(
         first_matrix, second_matrix, precision=HIGHEST, preferred_element_type=jnp.float32
@@ -325,7 +319,6 @@
 def gain_kernel(g, x0, x1, carry, spots, back, coarse_out, fine_out, hp, ap, xp, tp, part):
     k = x0.shape[0]
     step = chunk(k)
-    both = 2 * k
     low, high = pl.ds(0, k), pl.ds(k, k)
 
     def put(rows, columns, value):
@@ -575,7 +568,7 @@
     ahead = [(cycle[i], cycle[(i + 1) % len(cycle)]) for i in range(len(cycle))]
     behind = [(b, a) for a, b in ahead]
     ups, downs = [up_part], [down_part]
-    for _ in range(len(cycle) - 1):
+    for _ in range(1, len(cycle)):
         ups.append(lax.ppermute(ups[-1], axis, ahead))
         downs.append(lax.ppermute(downs[-1], axis, behind))
         if len(ups) == 2:
@@ -631,6 +624,61 @@
     owned = (offsets >= 0) & (offsets < count)
     picked = matrix[jnp.clip(offsets, 0, count - 1)]
     return jnp.where(owned[:, None], picked, 0.0)
+
+
+def pick_kernel(cells, chooser, field, picked, crossing, groups, sem):
+    count = picked.shape[0]
+
+    def fetch(index, carry):
+        group = pl.multiple_of(cells[index] // MARGIN * MARGIN, MARGIN)
+        spot = pl.multiple_of(index * MARGIN, MARGIN)
+        pltpu.make_async_copy(
+            field.at[pl.ds(group, MARGIN)], groups.at[pl.ds(spot, MARGIN)], sem
+        ).start()
+        return carry
+
+    lax.fori_loop(0, count, fetch, 0)
+    pltpu.make_async_copy(groups, groups, sem).wait()
+
+    def settle(index, carry):
+        spot = index * MARGIN + lax.rem(cells[index], MARGIN)
+        picked[pl.ds(index, 1), :] = groups[pl.ds(spot, 1), :]
+        return carry
+
+    lax.fori_loop(0, count, settle, 0, unroll=8)
+    value = picked[...]
+    total = jnp.zeros(crossing.shape, jnp.float32)
+    for _ in range(3):
+        term = value.astype(jnp.bfloat16)
+        total += across(chooser[...], term)
+        value = value - term.astype(jnp.float32)
+    crossing[...] = total
+
+
+def pick(field, cells, chooser):
+    count, cols = cells.size, field.shape[1]
+    held = pl.BlockSpec(memory_space=pltpu.VMEM)
+    return pl.pallas_call(
+        pick_kernel,
+        in_specs=[
+            pl.BlockSpec(memory_space=pltpu.SMEM),
+            held,
+            pl.BlockSpec(memory_space=pl.ANY),
+        ],
+        out_specs=[held, held],
+        out_shape=[
+            jax.ShapeDtypeStruct((count, cols), jnp.float32),
+            jax.ShapeDtypeStruct((chooser.shape[0], count), jnp.float32),
+        ],
+        scratch_shapes=[
+            pltpu.VMEM((count * MARGIN, cols), jnp.float32),
+            pltpu.SemaphoreType.DMA,
+        ],
+        cost_estimate=pl.CostEstimate(
+            flops=40 * 10**9, bytes_accessed=1 << 20, transcendentals=0
+        ),
+        compiler_params=pltpu.CompilerParams(vmem_limit_bytes=60 << 20),
+    )(cells, chooser, field)
 
 
 def balanced(prior, prepared, row_sites, col_sites, error_var, row_place, col_place):
@@ -664,10 +712,7 @@
     place = one_hot(col_slot, across_cols * col_slots)
 
     field, up_part, down_part = transport(prior, prepared, chooser, 2)
-    row_part = field[my_rows]
-    crossing = lax.dot_general(
-        chooser.astype(jnp.float32), row_part, (((1,), (1,)), ((), ())), precision=HIGHEST
-    )
+    row_part, crossing = pick(field, my_rows, chooser)
     pieces = doubling_gather(crossing, "row")
     known = exact(jnp.concatenate(pieces, axis=1), spots.astype(jnp.float32).T)
     row_part, known = lax.optimization_barrier((row_part, known))

time: 476 us -> 473 us (level)
  local copies, waits for them, and re-layouts: 36.4 us -> 18.5 us
  Pallas kernels: 348 us -> 359 us
    pallas_call x0 -> x1, Pallas kernels: none -> 15.3 us  [pick(): pl.pallas_call(pick_kernel, in_specs=[pl.BlockSpec(memory_space=pltpu.SME...]
    gather x1 -> x0, local copies, waits for them, and re-layouts: 14.8 us -> none  [balanced(): row_part = field[my_rows]]
    pallas_call x5, Pallas kernels: 98.8 us -> 92.4 us  [whole_call(): pl.pallas_call(kernel, in_specs=[whole] * len(args), out_specs=[whole] *...]
  transfers between devices with their start and end apart: 26 -> 26, of which waited for: 5 -> 7; matrix products, arithmetic and copies ran while one was open for 7% -> 7% of each run, Pallas kernels for 51% -> 50%
where the time goes in v4:
time: 473 us; the launch traced here: 467 us
  Pallas kernels  359 us (76%)
  starting transfers between devices  36.4 us (8%)
  waiting for transfers between devices  19.4 us (4%)
  local copies, waits for them, and re-layouts  18.5 us (4%)
  other arithmetic  17.9 us (4%)
  loops' own time  8.39 us (2%)
    pallas_call x2, Pallas kernels, update(): pl.pallas_call(update_kernel, grid=(rows // tall,), in_specs=[tile, held,...  100 us
    pallas_call x5, Pallas kernels, whole_call(): pl.pallas_call(kernel, in_specs=[whole] * len(args), out_specs=[whole] *...  92.4 us
    pallas_call x1, Pallas kernels, transport(): pl.pallas_call(transport_kernel, grid=(tiles,), in_specs=[pl.BlockSpec((T...  70.4 us
    pallas_call x1, Pallas kernels, crossing_gather(): pl.pallas_call(crossing_kernel, in_specs=[whole], out_specs=whole, out_sh...  54 us
    pallas_call x1, Pallas kernels, weights_of(): pl.pallas_call(weights_kernel, grid=(cols // wide,), in_specs=[held, held...  26.7 us
    ppermute x7, waiting for transfers between devices, ring_gather(): ups.append(lax.ppermute(ups[-1], axis, ahead))  17.6 us
    ppermute x6, starting transfers between devices, edges(): return (lax.ppermute(last, axis, up), lax.ppermute(leading, axis, down))  16 us
    pallas_call x1, Pallas kernels, pick(): pl.pallas_call(pick_kernel, in_specs=[pl.BlockSpec(memory_space=pltpu.SME...  15.3 us
  transfers between devices with their start and end apart: 26, of which 7 were waited for; matrix products, arithmetic and copies ran while one was open for 7% of the time, Pallas kernels for 50%

profile of v4, /device:TPU:0, one launch (start us, length us, event | category | flops | bytes accessed | tf_op | source)
XLA Modules:
  0.0 466.8 jit_solution(6112611173200738010)
XLA Ops:
  0.0 0.9 fusion.43
  0.9 1.3 collective-permute-start.31
  2.2 3.0 collective-permute-start.30
  5.2 4.2 fusion.42
  9.5 2.3 copy.87
  11.8 1.3 collective-permute-start.32
  13.8 5.5 %collective-permute-start.33 = (f32[4096,2]{0,1:T(2,128)S(1)}, f32[4096,2]{0,1:T(2,128)S(1)}, u32[]{:S(2)}, u32[]{:S(2)}) collective-permute-start(f32[4096,2]{0,1:T(2,128)S(1)} %copy.88), channel_id=1, source_target_pairs={{0,1},{1,2},{2,3},{3,4},{4,5},{5,6},{6,7},{8,9},{9,10},{10,11},{11... | collective-permute-start | bytes 98312 | tf_op jit(solution)/shard_map/ppermute | solution.py:37
  20.9 2.1 convert_reduce_fusion
  25.8 1.3 collective-permute-start.35
  27.1 3.6 collective-permute-start.34
  32.3 2.0 copy.83
  34.3 2.2 pad_maximum_fusion.1
  37.3 428.2 %conditional.1 = (f32[4096,2048]{1,0:T(8,128)}) conditional(s32[]{:T(128)} %convert_element_type.49, (s32[1024]{0:T(1024)S(1)}, s32[1024]{0:T(1024)S(1)}, f32[4096,2048]{1,0:T(8,128)}, f32[8,2048]{1,0:T(8,128)S(1)}, f32[8,2048]{1,0:T(8,128)S(1)}, /*index=5*/f32[32,144,128]{2,1,0:T(8,128)S(1)}, f32[32,144,8]{1,0,2:T(8,128)S(1)}, ...), branch_computations={%region_4.12_spmd, %region_12.18_spmd} | conditional | flops 285427761152 | bytes 1123367424 | solution.py:834
  45.2 1.3 fusion.21
  48.2 1.0 fusion.7.chooser
  49.2 2.1 copy.86.row_weights
  51.3 0.9 select_reduce_fusion.cells
  52.2 70.4 %branch_1_fun.11 = (f32[4096,2048]{1,0:T(8,128)}, f32[80,4096]{1,0:T(8,128)}, f32[80,4096]{1,0:T(8,128)}) custom-call(f32[4096,2048]{1,0:T(8,128)} %get-tuple-element.244.main.prev.follow, f32[4096,2048]{1,0:T(8,128)} %get-tuple-element.244.main.prev.follow, f32[4096,2048]{1,0:T(8,128)} %get-tuple-element.244.main.prev.follow, ...), custom_call_target="tpu_custom_call" | custom-call | tf_op jit(solution)/shard_map/cond/branch_1_fun/pallas_call | solution.py:117
  122.6 15.3 %branch_1_fun.12 = (f32[304,2048]{1,0:T(8,128)}, f32[160,304]{1,0:T(8,128)}) custom-call(s32[304]{0:T(512)} %select_reduce_fusion.cells, bf16[160,2048]{1,0:T(8,128)(2,1)} %fusion.7.chooser, f32[4096,2048]{1,0:T(8,128)} %get-tuple-element.258.field), custom_call_target="tpu_custom_call" | custom-call | flops 40000000000 | bytes 1048576 | tf_op jit(solution)/shard_map/cond/branch_1_fun/pallas_call | solution.py:661
  137.9 1.4 collective-permute-start.3
  139.3 2.8 collective-permute-start.2
  142.1 1.6 collective-permute-start
  144.5 2.7 fusion.5.back
  147.2 2.0 fusion.4.place
  149.3 2.0 fusion.2.spots
  151.8 0.9 collective-permute-done.4
  153.1 4.1 fusion.3.known
  157.4 54.0 %branch_1_fun.13.slotted = f32[1280,1024]{1,0:T(8,128)} custom-call(f32[160,1024]{1,0:T(8,128)} %fusion.3.known), custom_call_target="tpu_custom_call" | custom-call | tf_op jit(solution)/shard_map/cond/branch_1_fun/pallas_call | solution.py:478
  211.4 2.3 collective-permute-start.8
  214.3 16.4 %branch_1_fun.14.g = f32[1024,1024]{1,0:T(8,128)} custom-call(f32[1280,1024]{1,0:T(8,128)} %branch_1_fun.13.slotted, bf16[1024,1280]{1,0:T(8,128)(2,1)} %fusion.4.place), custom_call_target="tpu_custom_call" | custom-call | flops 25500000256 | bytes 1048576 | tf_op jit(solution)/shard_map/cond/branch_1_fun/pallas_call | solution.py:195
  230.6 2.3 slice.403.block
  232.9 10.6 %collective-permute-done.8.refs_4_ = f32[80,4096]{1,0:T(8,128)S(1)} collective-permute-done((f32[80,4096]{1,0:T(8,128)}, f32[80,4096]{1,0:T(8,128)S(1)}, u32[]{:S(2)}, u32[]{:S(2)}) %collective-permute-start.8) | collective-permute-done | bytes 1310752 | tf_op jit(solution)/shard_map/cond/branch_1_fun/ppermute | solution.py:572
  243.5 1.4 collective-permute-start.10
  245.6 21.4 %branch_1_fun.15.x0 = f32[512,512]{1,0:T(8,128)} custom-call(f32[512,512]{1,0:T(8,128)} %slice.403.block, f32[1,512]{1,0:T(1,128)} %get-tuple-element.433.variance), custom_call_target="tpu_custom_call" | custom-call | flops 31499999232 | bytes 1048576 | tf_op jit(solution)/shard_map/cond/branch_1_fun/pallas_call | solution.py:195
  266.9 6.9 %branch_1_fun.16 = (f32[512,512]{1,0:T(8,128)}, f32[512,512]{1,0:T(8,128)}) custom-call(f32[1024,1024]{1,0:T(8,128)} %branch_1_fun.14.g, f32[512,512]{1,0:T(8,128)} %branch_1_fun.15.x0), custom_call_target="tpu_custom_call" | custom-call | flops 10499999744 | bytes 1048576 | tf_op jit(solution)/shard_map/cond/branch_1_fun/pallas_call | solution.py:195
  274.1 1.1 collective-permute-start.12
  275.2 1.1 collective-permute-start.13
  276.4 21.4 %branch_1_fun.17.x1 = f32[512,512]{1,0:T(8,128)} custom-call(f32[512,512]{1,0:T(8,128)} %get-tuple-element.274.block, f32[1,512]{1,0:T(1,128)} %get-tuple-element.432.variance), custom_call_target="tpu_custom_call" | custom-call | flops 31499999232 | bytes 1048576 | tf_op jit(solution)/shard_map/cond/branch_1_fun/pallas_call | solution.py:195
  297.8 6.2 %collective-permute-done.12.refs_8_ = f32[80,4096]{1,0:T(8,128)S(1)} collective-permute-done((f32[80,4096]{1,0:T(8,128)S(1)}, f32[80,4096]{1,0:T(8,128)S(1)}, u32[]{:S(2)}, u32[]{:S(2)}) %collective-permute-start.12) | collective-permute-done | bytes 1310752 | tf_op jit(solution)/shard_map/cond/branch_1_fun/ppermute | solution.py:572
  304.0 0.8 collective-permute-start.14
  305.0 1.2 collective-permute-start.15
  306.2 26.4 %branch_1_fun.18 = (bf16[1280,1216]{1,0:T(8,128)(2,1)}, bf16[1280,1216]{1,0:T(8,128)(2,1)}) custom-call(f32[1024,1024]{1,0:T(8,128)} %branch_1_fun.14.g, f32[512,512]{1,0:T(8,128)} %branch_1_fun.15.x0, f32[512,512]{1,0:T(8,128)} %branch_1_fun.17.x1, f32[512,512]{1,0:T(8,128)} %get-tuple-element.275.carry, bf16[1024,1216]{1,0:T(8,128)(2,1)} %fusion.2.spots, ...), custom_call_target="tpu_custom_call" | custom-call | flops 38999998464 | bytes 1048576 | tf_op jit(solution)/shard_map/cond/branch_1_fun/pallas_call | solution.py:195
  333.6 1.4 collective-permute-start.17
  335.0 26.7 %branch_1_fun.19 = (bf16[1280,2048]{1,0:T(8,128)(2,1)}, bf16[1280,2048]{1,0:T(8,128)(2,1)}) custom-call(bf16[1280,1216]{1,0:T(8,128)(2,1)} %get-tuple-element.276.gain_coarse, bf16[1280,1216]{1,0:T(8,128)(2,1)} %get-tuple-element.277.gain_fine, f32[304,2048]{1,0:T(8,128)} %get-tuple-element.278.refs_0_, f32[304,2048]{1,0:T(8,128)} %collective-permute-done.5.refs_1_, ...), custom_call_target="tpu_custom_call" | custom-call | flops 19126026240 | bytes 31457280 | tf_op jit(solution)/shard_map/cond/branch_1_fun/pallas_call | solution.py:506
  362.5 1.6 collective-permute-start.19
  364.1 61.9 %branch_1_fun.20.field = f32[4096,2048]{1,0:T(8,128)} custom-call(f32[4096,2048]{1,0:T(8,128)} %get-tuple-element.258.field, bf16[1280,2048]{1,0:T(8,128)(2,1)} %get-tuple-element.279.weights_coarse, bf16[1280,2048]{1,0:T(8,128)(2,1)} %get-tuple-element.280.weights_fine, f32[80,4096]{1,0:T(8,128)} %get-tuple-element.259.refs_0_, ...), custom_call_target="tpu_custom_call" | custom-call | flops 64424509440 | bytes 67108864 | tf_op jit(solution)/shard_map/cond/branch_1_fun/pallas_call | solution.py:542
  426.0 1.0 copy-done.4
  427.1 38.1 %branch_1_fun.21 = f32[4096,2048]{1,0:T(8,128)} custom-call(f32[4096,2048]{1,0:T(8,128)} %branch_1_fun.20.field, bf16[1280,2048]{1,0:T(8,128)(2,1)} %get-tuple-element.279.weights_coarse, bf16[1280,2048]{1,0:T(8,128)(2,1)} %get-tuple-element.280.weights_fine, f32[80,4096]{1,0:T(8,128)} %copy-done.2, f32[80,4096]{1,0:T(8,128)} %copy-done.3, ...), custom_call_target="tpu_custom_call" | custom-call | flops 21474836480 | bytes 67108864 | tf_op jit(solution)/shard_map/cond/branch_1_fun/pallas_call | solution.py:542
  (199 shorter events, 12.7 us)
Async XLA Ops:
  0.9 36.3 %collective-permute-start.31 = (f32[8,2048]{1,0:T(8,128)S(1)}, f32[8,2048]{1,0:T(8,128)S(1)}, u32[]{:S(2)}, u32[]{:S(2)}) collective-permute-start(f32[8,2048]{1,0:T(8,128)S(1)} %get-tuple-element.438), channel_id=1, source_target_pairs={{8,0},{16,8},{24,16},{9,1},{17,9},{25,17},{10,2},{18,10},{26,18},{... | collective-permute-start | bytes 196616 | tf_op jit(solution)/shard_map/ppermute | solution.py:37
  2.2 35.0 %collective-permute-start.30 = (f32[8,2048]{1,0:T(8,128)S(1)}, f32[8,2048]{1,0:T(8,128)S(1)}, u32[]{:S(2)}, u32[]{:S(2)}) collective-permute-start(f32[8,2048]{1,0:T(8,128)S(1)} %get-tuple-element.439), channel_id=1, source_target_pairs={{0,8},{8,16},{16,24},{1,9},{9,17},{17,25},{2,10},{10,18},{18,26},{... | collective-permute-start | bytes 196616 | tf_op jit(solution)/shard_map/ppermute | solution.py:37
  9.4 9.9 %copy-start.5 = (f32[16384]{0:T(1024)S(1)}, f32[16384]{0:T(1024)}, u32[]{:S(2)}) copy-start(f32[16384]{0:T(1024)} %param.24) | copy-start | bytes 196612
  9.5 9.9 %copy-start.6 = (f32[16384]{0:T(1024)S(1)}, f32[16384]{0:T(1024)}, u32[]{:S(2)}) copy-start(f32[16384]{0:T(1024)} %param.23) | copy-start | bytes 196612
  9.5 9.9 %copy-start.10 = (s32[16384]{0:T(1024)S(1)}, s32[16384]{0:T(1024)}, u32[]{:S(2)}) copy-start(s32[16384]{0:T(1024)} %param.25) | copy-start | bytes 196612
  9.5 10.3 %copy-start.17 = (s32[2,512]{1,0:T(2,128)S(1)}, s32[2,512]{1,0:T(2,128)}, u32[]{:S(2)}) copy-start(s32[2,512]{1,0:T(2,128)} %param.26) | copy-start | bytes 12292
  9.5 10.3 %copy-start.18 = (s32[2,512]{1,0:T(2,128)S(1)}, s32[2,512]{1,0:T(2,128)}, u32[]{:S(2)}) copy-start(s32[2,512]{1,0:T(2,128)} %param.27) | copy-start | bytes 12292
  9.5 10.4 %copy-start.7 = (f32[16384]{0:T(1024)S(1)}, f32[16384]{0:T(1024)}, u32[]{:S(2)}) copy-start(f32[16384]{0:T(1024)} %param.21) | copy-start | bytes 196612
  9.5 10.4 %copy-start.8 = (f32[16384]{0:T(1024)S(1)}, f32[16384]{0:T(1024)}, u32[]{:S(2)}) copy-start(f32[16384]{0:T(1024)} %param.20) | copy-start | bytes 196612
  9.5 10.4 %copy-start.11 = (s32[16384]{0:T(1024)S(1)}, s32[16384]{0:T(1024)}, u32[]{:S(2)}) copy-start(s32[16384]{0:T(1024)} %param.22) | copy-start | bytes 196612
  11.8 13.8 %collective-permute-start.32 = (f32[4096,2]{0,1:T(2,128)S(1)}, f32[4096,2]{0,1:T(2,128)S(1)}, u32[]{:S(2)}, u32[]{:S(2)}) collective-permute-start(f32[4096,2]{0,1:T(2,128)S(1)} %copy.87), channel_id=1, source_target_pairs={{1,0},{2,1},{3,2},{4,3},{5,4},{6,5},{7,6},{9,8},{10,9},{11,10},{12... | collective-permute-start | bytes 98312 | tf_op jit(solution)/shard_map/ppermute | solution.py:37
  13.8 11.9 %collective-permute-start.33 = (f32[4096,2]{0,1:T(2,128)S(1)}, f32[4096,2]{0,1:T(2,128)S(1)}, u32[]{:S(2)}, u32[]{:S(2)}) collective-permute-start(f32[4096,2]{0,1:T(2,128)S(1)} %copy.88), channel_id=1, source_target_pairs={{0,1},{1,2},{2,3},{3,4},{4,5},{5,6},{6,7},{8,9},{9,10},{10,11},{11... | collective-permute-start | bytes 98312 | tf_op jit(solution)/shard_map/ppermute | solution.py:37
  23.0 7.7 %copy-start.13 = (s32[1024]{0:T(1024)}, s32[1024]{0:T(1024)S(1)}, u32[]{:S(2)}) copy-start(s32[1024]{0:T(1024)S(1)} %get-tuple-element.398) | copy-start | bytes 12292
  23.0 7.7 %copy-start.15 = (s32[1024]{0:T(1024)}, s32[1024]{0:T(1024)S(1)}, u32[]{:S(2)}) copy-start(s32[1024]{0:T(1024)S(1)} %get-tuple-element.399) | copy-start | bytes 12292
  25.8 4.9 %collective-permute-start.35 = (f32[8,4]{0,1:T(4,128)S(1)}, f32[8,4]{0,1:T(4,128)S(1)}, u32[]{:S(2)}, u32[]{:S(2)}) collective-permute-start(f32[8,4]{0,1:T(4,128)S(1)} %get-tuple-element.446), channel_id=1, source_target_pairs={{8,0},{16,8},{24,16},{9,1},{17,9},{25,17},{10,2},{18,10},{26,18},{... | collective-permute-start | bytes 392 | tf_op jit(solution)/shard_map/ppermute | solution.py:37
  27.1 4.4 collective-permute-start.34
  36.5 0.8 copy-start.12
  137.8 11.3 %copy-start.19 = (s32[4]{0:T(128)S(1)}, s32[4]{0:T(128)}, u32[]{:S(2)}) copy-start(s32[4]{0:T(128)} %constant.209.clone.1) | copy-start | bytes 52 | tf_op jit(solution)/shard_map/cond
  137.8 14.9 %copy-start.9 = (f32[160,304]{1,0:T(8,128)S(1)}, f32[160,304]{1,0:T(8,128)}, u32[]{:S(2)}) copy-start(f32[160,304]{1,0:T(8,128)} %get-tuple-element.267) | copy-start | bytes 583684 | tf_op jit(solution)/shard_map/cond
  137.9 14.0 %collective-permute-start.3 = (f32[160,304]{1,0:T(8,128)}, f32[160,304]{1,0:T(8,128)S(1)}, u32[]{:S(2)}, u32[]{:S(2)}) collective-permute-start(f32[160,304]{1,0:T(8,128)} %get-tuple-element.267), channel_id=1, source_target_pairs={{0,8},{8,0},{16,24},{24,16},{1,9},{9,1},{17,25},{25,17},{2,10},{10... | collective-permute-start | bytes 583688 | tf_op jit(solution)/shard_map/cond/branch_1_fun/ppermute | solution.py:592
  139.3 12.0 %collective-permute-start.2 = (f32[160,304]{1,0:T(8,128)}, f32[160,304]{1,0:T(8,128)S(1)}, u32[]{:S(2)}, u32[]{:S(2)}) collective-permute-start(f32[160,304]{1,0:T(8,128)} %get-tuple-element.267), channel_id=1, source_target_pairs={{0,16},{8,24},{16,0},{24,8},{1,17},{9,25},{17,1},{25,9},{2,18},{10... | collective-permute-start | bytes 583688 | tf_op jit(solution)/shard_map/cond/branch_1_fun/ppermute | solution.py:592
  142.1 69.3 %collective-permute-start = (f32[80,4096]{1,0:T(8,128)}, f32[80,4096]{1,0:T(8,128)}, u32[]{:S(2)}, u32[]{:S(2)}) collective-permute-start(f32[80,4096]{1,0:T(8,128)} %get-tuple-element.259.refs_0_), channel_id=1, source_target_pairs={{0,2},{2,4},{4,6},{6,7},{7,5},{5,3},{3,1},{1,0},{8,10},{10,12},{12... | collective-permute-start | bytes 3932168 | tf_op jit(solution)/shard_map/cond/branch_1_fun/ppermute | solution.py:572
  143.7 67.7 %collective-permute-start.1 = (f32[80,4096]{1,0:T(8,128)}, f32[80,4096]{1,0:T(8,128)}, u32[]{:S(2)}, u32[]{:S(2)}) collective-permute-start(f32[80,4096]{1,0:T(8,128)} %get-tuple-element.260.refs_1_), channel_id=1, source_target_pairs={{2,0},{4,2},{6,4},{7,6},{5,7},{3,5},{1,3},{0,1},{10,8},{12,10},{14... | collective-permute-start | bytes 3932168 | tf_op jit(solution)/shard_map/cond/branch_1_fun/ppermute | solution.py:573
  151.2 1.5 collective-permute-start.4
  157.2 177.9 %collective-permute-start.6 = (f32[304,2048]{1,0:T(8,128)}, f32[304,2048]{1,0:T(8,128)}, u32[]{:S(2)}, u32[]{:S(2)}) collective-permute-start(f32[304,2048]{1,0:T(8,128)} %get-tuple-element.278.refs_0_), channel_id=1, source_target_pairs={{0,8},{8,0},{16,24},{24,16},{1,9},{9,1},{17,25},{25,17},{2,10},{10... | collective-permute-start | bytes 7471112 | tf_op jit(solution)/shard_map/cond/branch_1_fun/ppermute | solution.py:592
  157.3 140.5 %collective-permute-start.5 = (f32[304,2048]{1,0:T(8,128)}, f32[304,2048]{1,0:T(8,128)}, u32[]{:S(2)}, u32[]{:S(2)}) collective-permute-start(f32[304,2048]{1,0:T(8,128)} %get-tuple-element.278.refs_0_), channel_id=1, source_target_pairs={{0,16},{8,24},{16,0},{24,8},{1,17},{9,25},{17,1},{25,9},{2,18},{10... | collective-permute-start | bytes 7471112 | tf_op jit(solution)/shard_map/cond/branch_1_fun/ppermute | solution.py:592
  211.4 32.1 %collective-permute-start.8 = (f32[80,4096]{1,0:T(8,128)}, f32[80,4096]{1,0:T(8,128)S(1)}, u32[]{:S(2)}, u32[]{:S(2)}) collective-permute-start(f32[80,4096]{1,0:T(8,128)} %collective-permute-done.refs_2_), channel_id=1, source_target_pairs={{0,2},{2,4},{4,6},{6,7},{7,5},{5,3},{3,1},{1,0},{8,10},{10,12},{12... | collective-permute-start | bytes 3932168 | tf_op jit(solution)/shard_map/cond/branch_1_fun/ppermute | solution.py:572
  213.7 31.3 %collective-permute-start.9 = (f32[80,4096]{1,0:T(8,128)}, f32[80,4096]{1,0:T(8,128)S(1)}, u32[]{:S(2)}, u32[]{:S(2)}) collective-permute-start(f32[80,4096]{1,0:T(8,128)} %collective-permute-done.1.refs_3_), channel_id=1, source_target_pairs={{2,0},{4,2},{6,4},{7,6},{5,7},{3,5},{1,3},{0,1},{10,8},{12,10},{14... | collective-permute-start | bytes 3932168 | tf_op jit(solution)/shard_map/cond/branch_1_fun/ppermute | solution.py:573
  243.5 23.4 %copy-start.20 = (f32[80,4096]{1,0:T(8,128)}, f32[80,4096]{1,0:T(8,128)S(1)}, u32[]{:S(2)}) copy-start(f32[80,4096]{1,0:T(8,128)S(1)} %collective-permute-done.8.refs_4_) | copy-start | bytes 3932164 | tf_op jit(solution)/shard_map/cond
  243.5 30.6 %collective-permute-start.10 = (f32[80,4096]{1,0:T(8,128)S(1)}, f32[80,4096]{1,0:T(8,128)S(1)}, u32[]{:S(2)}, u32[]{:S(2)}) collective-permute-start(f32[80,4096]{1,0:T(8,128)S(1)} %collective-permute-done.8.refs_4_), channel_id=1, source_target_pairs={{0,2},{2,4},{4,6},{6,7},{7,5},{5,3},{3,1},{1,0},{8,10},{10,12},{12... | collective-permute-start | bytes 3932168 | tf_op jit(solution)/shard_map/cond/branch_1_fun/ppermute | solution.py:572
  244.9 22.0 %copy-start.21 = (f32[80,4096]{1,0:T(8,128)}, f32[80,4096]{1,0:T(8,128)S(1)}, u32[]{:S(2)}) copy-start(f32[80,4096]{1,0:T(8,128)S(1)} %collective-permute-done.9.refs_5_) | copy-start | bytes 3932164 | tf_op jit(solution)/shard_map/cond
  244.9 30.3 %collective-permute-start.11 = (f32[80,4096]{1,0:T(8,128)S(1)}, f32[80,4096]{1,0:T(8,128)}, u32[]{:S(2)}, u32[]{:S(2)}) collective-permute-start(f32[80,4096]{1,0:T(8,128)S(1)} %collective-permute-done.9.refs_5_), channel_id=1, source_target_pairs={{2,0},{4,2},{6,4},{7,6},{5,7},{3,5},{1,3},{0,1},{10,8},{12,10},{14... | collective-permute-start | bytes 3932168 | tf_op jit(solution)/shard_map/cond/branch_1_fun/ppermute | solution.py:573
  274.1 23.6 %copy-start.22 = (f32[80,4096]{1,0:T(8,128)}, f32[80,4096]{1,0:T(8,128)S(1)}, u32[]{:S(2)}) copy-start(f32[80,4096]{1,0:T(8,128)S(1)} %collective-permute-done.10.refs_6_) | copy-start | bytes 3932164 | tf_op jit(solution)/shard_map/cond
  274.1 29.9 %collective-permute-start.12 = (f32[80,4096]{1,0:T(8,128)S(1)}, f32[80,4096]{1,0:T(8,128)S(1)}, u32[]{:S(2)}, u32[]{:S(2)}) collective-permute-start(f32[80,4096]{1,0:T(8,128)S(1)} %collective-permute-done.10.refs_6_), channel_id=1, source_target_pairs={{0,2},{2,4},{4,6},{6,7},{7,5},{5,3},{3,1},{1,0},{8,10},{10,12},{12... | collective-permute-start | bytes 3932168 | tf_op jit(solution)/shard_map/cond/branch_1_fun/ppermute | solution.py:572
  275.2 29.8 %collective-permute-start.13 = (f32[80,4096]{1,0:T(8,128)}, f32[80,4096]{1,0:T(8,128)S(1)}, u32[]{:S(2)}, u32[]{:S(2)}) collective-permute-start(f32[80,4096]{1,0:T(8,128)} %collective-permute-done.11.refs_7_), channel_id=1, source_target_pairs={{2,0},{4,2},{6,4},{7,6},{5,7},{3,5},{1,3},{0,1},{10,8},{12,10},{14... | collective-permute-start | bytes 3932168 | tf_op jit(solution)/shard_map/cond/branch_1_fun/ppermute | solution.py:573
  297.7 37.3 %collective-permute-start.7 = (f32[304,2048]{1,0:T(8,128)}, f32[304,2048]{1,0:T(8,128)}, u32[]{:S(2)}, u32[]{:S(2)}) collective-permute-start(f32[304,2048]{1,0:T(8,128)} %collective-permute-done.5.refs_1_), channel_id=1, source_target_pairs={{0,8},{8,0},{16,24},{24,16},{1,9},{9,1},{17,25},{25,17},{2,10},{10... | collective-permute-start | bytes 7471112 | tf_op jit(solution)/shard_map/cond/branch_1_fun/ppermute | solution.py:592
  304.0 28.6 %copy-start.23 = (f32[80,4096]{1,0:T(8,128)}, f32[80,4096]{1,0:T(8,128)S(1)}, u32[]{:S(2)}) copy-start(f32[80,4096]{1,0:T(8,128)S(1)} %collective-permute-done.12.refs_8_) | copy-start | bytes 3932164 | tf_op jit(solution)/shard_map/cond
  304.0 29.0 %collective-permute-start.14 = (f32[80,4096]{1,0:T(8,128)S(1)}, f32[80,4096]{1,0:T(8,128)S(1)}, u32[]{:S(2)}, u32[]{:S(2)}) collective-permute-start(f32[80,4096]{1,0:T(8,128)S(1)} %collective-permute-done.12.refs_8_), channel_id=1, source_target_pairs={{0,2},{2,4},{4,6},{6,7},{7,5},{5,3},{3,1},{1,0},{8,10},{10,12},{12... | collective-permute-start | bytes 3932168 | tf_op jit(solution)/shard_map/cond/branch_1_fun/ppermute | solution.py:572
  305.0 27.6 %copy-start.24 = (f32[80,4096]{1,0:T(8,128)}, f32[80,4096]{1,0:T(8,128)S(1)}, u32[]{:S(2)}) copy-start(f32[80,4096]{1,0:T(8,128)S(1)} %collective-permute-done.13.refs_9_) | copy-start | bytes 3932164 | tf_op jit(solution)/shard_map/cond
  305.0 28.7 %collective-permute-start.15 = (f32[80,4096]{1,0:T(8,128)S(1)}, f32[80,4096]{1,0:T(8,128)}, u32[]{:S(2)}, u32[]{:S(2)}) collective-permute-start(f32[80,4096]{1,0:T(8,128)S(1)} %collective-permute-done.13.refs_9_), channel_id=1, source_target_pairs={{2,0},{4,2},{6,4},{7,6},{5,7},{3,5},{1,3},{0,1},{10,8},{12,10},{14... | collective-permute-start | bytes 3932168 | tf_op jit(solution)/shard_map/cond/branch_1_fun/ppermute | solution.py:573
  333.0 28.8 %copy-start.25 = (f32[80,4096]{1,0:T(8,128)}, f32[80,4096]{1,0:T(8,128)S(1)}, u32[]{:S(2)}) copy-start(f32[80,4096]{1,0:T(8,128)S(1)} %collective-permute-done.14.refs_10_) | copy-start | bytes 3932164 | tf_op jit(solution)/shard_map/cond
  333.0 28.8 %collective-permute-start.16 = (f32[80,4096]{1,0:T(8,128)S(1)}, f32[80,4096]{1,0:T(8,128)S(1)}, u32[]{:S(2)}, u32[]{:S(2)}) collective-permute-start(f32[80,4096]{1,0:T(8,128)S(1)} %collective-permute-done.14.refs_10_), channel_id=1, source_target_pairs={{0,2},{2,4},{4,6},{6,7},{7,5},{5,3},{3,1},{1,0},{8,10},{10,12},{12... | collective-permute-start | bytes 3932168 | tf_op jit(solution)/shard_map/cond/branch_1_fun/ppermute | solution.py:572
  333.6 28.9 %collective-permute-start.17 = (f32[80,4096]{1,0:T(8,128)}, f32[80,4096]{1,0:T(8,128)S(1)}, u32[]{:S(2)}, u32[]{:S(2)}) collective-permute-start(f32[80,4096]{1,0:T(8,128)} %collective-permute-done.15.refs_11_), channel_id=1, source_target_pairs={{2,0},{4,2},{6,4},{7,6},{5,7},{3,5},{1,3},{0,1},{10,8},{12,10},{14... | collective-permute-start | bytes 3932168 | tf_op jit(solution)/shard_map/cond/branch_1_fun/ppermute | solution.py:573
  361.8 64.2 %copy-start.2 = (f32[80,4096]{1,0:T(8,128)}, f32[80,4096]{1,0:T(8,128)S(1)}, u32[]{:S(2)}) copy-start(f32[80,4096]{1,0:T(8,128)S(1)} %collective-permute-done.16.refs_0_) | copy-start | bytes 3932164 | tf_op jit(solution)/shard_map/cond
  361.8 64.2 %collective-permute-start.18 = (f32[80,4096]{1,0:T(8,128)S(1)}, f32[80,4096]{1,0:T(8,128)S(1)}, u32[]{:S(2)}, u32[]{:S(2)}) collective-permute-start(f32[80,4096]{1,0:T(8,128)S(1)} %collective-permute-done.16.refs_0_), channel_id=1, source_target_pairs={{0,2},{2,4},{4,6},{6,7},{7,5},{5,3},{3,1},{1,0},{8,10},{10,12},{12... | collective-permute-start | bytes 3932168 | tf_op jit(solution)/shard_map/cond/branch_1_fun/ppermute | solution.py:572
  362.5 63.5 %copy-start.3 = (f32[80,4096]{1,0:T(8,128)}, f32[80,4096]{1,0:T(8,128)S(1)}, u32[]{:S(2)}) copy-start(f32[80,4096]{1,0:T(8,128)S(1)} %collective-permute-done.17.refs_1_) | copy-start | bytes 3932164 | tf_op jit(solution)/shard_map/cond
  362.5 63.5 %collective-permute-start.19 = (f32[80,4096]{1,0:T(8,128)S(1)}, f32[80,4096]{1,0:T(8,128)}, u32[]{:S(2)}, u32[]{:S(2)}) collective-permute-start(f32[80,4096]{1,0:T(8,128)S(1)} %collective-permute-done.17.refs_1_), channel_id=1, source_target_pairs={{2,0},{4,2},{6,4},{7,6},{5,7},{3,5},{1,3},{0,1},{10,8},{12,10},{14... | collective-permute-start | bytes 3932168 | tf_op jit(solution)/shard_map/cond/branch_1_fun/ppermute | solution.py:573
  426.0 1.1 copy-start.4
  (2 other events, 1.5 us)

commit v5 on v4

--- a/solution.py
+++ b/solution.py
@@ -358,9 +358,9 @@
 
     def slot_rows(rows):
         picks = back[rows, :]
-        for index, out in ((0, coarse_out), (1, fine_out)):
-            moved = plain(picks, part[index]).astype(jnp.bfloat16)
-            out[rows, :] = plain(moved, spots[...]).astype(jnp.bfloat16)
+        coarse, fine = halves(plain(picks, part[0]) + plain(picks, part[1]))
+        moved = plain(coarse, spots[...]) + plain(fine, spots[...])
+        coarse_out[rows, :], fine_out[rows, :] = halves(moved)
 
     by_rows(back.shape[0], chunk(back.shape[0]), slot_rows)
 
@@ -604,12 +604,18 @@
 def places(sites, extent):
     owner = sites // extent
     before = jnp.tril(jnp.ones((sites.size, sites.size), jnp.bool_), -1)
-    same = owner[:, None] == owner[None, :]
-    return owner, jnp.sum((same & before).astype(jnp.int32), axis=1)
-
-
-def local_cells(sites, owner, rank, me, extent, count, empty):
-    hit = (owner == me)[None, :] & (rank[None, :] == jnp.arange(count)[:, None])
+    again = (sites[:, None] == sites[None, :]) & before
+    fresh = jnp.logical_not(jnp.any(again, axis=1))
+    counts = (owner[:, None] == owner[None, :]) & before & fresh[None, :]
+    rank = jnp.sum(counts.astype(jnp.int32), axis=1)
+    same = sites[:, None] == sites[None, :]
+    shared = jnp.sum(jnp.where(same & fresh[None, :], rank[None, :], 0), axis=1)
+    return owner, shared, fresh
+
+
+def local_cells(sites, place, me, extent, count, empty):
+    owner, rank, fresh = place
+    hit = (fresh & (owner == me))[None, :] & (rank[None, :] == jnp.arange(count)[:, None])
     cell = jnp.sum(jnp.where(hit, (sites - me * extent - empty)[None, :], 0), axis=1)
     return cell + empty
 
@@ -687,12 +693,12 @@
     my_row, my_col = lax.axis_index("row"), lax.axis_index("col")
     total = row_sites.size
     row_slots, col_slots = capacity(total, across_rows), capacity(total, across_cols)
-    row_owner, row_rank = row_place
-    col_owner, col_rank = col_place
+    row_owner, row_rank, _ = row_place
+    col_owner, col_rank, _ = col_place
     half = col_slots // 2
 
-    my_rows = local_cells(row_sites, row_owner, row_rank, my_row, rows, row_slots, 0)
-    my_cols = local_cells(col_sites, col_owner, col_rank, my_col, cols, col_slots, -1)
+    my_rows = local_cells(row_sites, row_place, my_row, rows, row_slots, 0)
+    my_cols = local_cells(col_sites, col_place, my_col, cols, col_slots, -1)
     chooser = one_hot(my_cols, cols)
 
     masks = doubling_masks(across_rows)
@@ -741,7 +747,7 @@
 
 def product(left, right):
     (rows, depth), cols = left.shape, right.shape[1]
-    tall, wide = min(128, rows), min(128, cols)
+    tall, wide = min(256, rows), min(256, cols)
     return pl.pallas_call(
         product_kernel,
         grid=(rows // tall, cols // wide),

time: 473 us -> 483 us (1.021)
  other arithmetic: 17.9 us -> 22.8 us
  transfers between devices with their start and end apart: 26 -> 26, of which waited for: 7 -> 6; matrix products, arithmetic and copies ran while one was open for 7% -> 8% of each run, Pallas kernels for 50% -> 50%
where the time goes in v5:
time: 483 us; the launch traced here: 475 us
  Pallas kernels  362 us (75%)
  starting transfers between devices  36.2 us (7%)
  other arithmetic  22.8 us (5%)
  local copies, waits for them, and re-layouts  19.1 us (4%)
  waiting for transfers between devices  19 us (4%)
  loops' own time  8.33 us (2%)
    pallas_call x2, Pallas kernels, update(): pl.pallas_call(update_kernel, grid=(rows // tall,), in_specs=[tile, held,...  100 us
    pallas_call x5, Pallas kernels, whole_call(): pl.pallas_call(kernel, in_specs=[whole] * len(args), out_specs=[whole] *...  94.8 us
    pallas_call x1, Pallas kernels, transport(): pl.pallas_call(transport_kernel, grid=(tiles,), in_specs=[pl.BlockSpec((T...  70.4 us
    pallas_call x1, Pallas kernels, crossing_gather(): pl.pallas_call(crossing_kernel, in_specs=[whole], out_specs=whole, out_sh...  53.9 us
    pallas_call x1, Pallas kernels, weights_of(): pl.pallas_call(weights_kernel, grid=(cols // wide,), in_specs=[held, held...  26.8 us
    ppermute x7, waiting for transfers between devices, ring_gather(): ups.append(lax.ppermute(ups[-1], axis, ahead))  17.2 us
    ppermute x6, starting transfers between devices, edges(): return (lax.ppermute(last, axis, up), lax.ppermute(leading, axis, down))  16 us
    pallas_call x1, Pallas kernels, pick(): pl.pallas_call(pick_kernel, in_specs=[pl.BlockSpec(memory_space=pltpu.SME...  15.9 us
  transfers between devices with their start and end apart: 26, of which 6 were waited for; matrix products, arithmetic and copies ran while one was open for 8% of the time, Pallas kernels for 50%

profile of v5, /device:TPU:0, one launch (start us, length us, event | category | flops | bytes accessed | tf_op | source)
XLA Modules:
  0.0 474.7 jit_solution(3539230228207202341)
XLA Ops:
  0.9 1.3 collective-permute-start.31
  2.2 3.0 collective-permute-start.30
  5.2 4.2 fusion.46
  9.5 2.3 copy.87
  11.8 1.3 collective-permute-start.32
  13.7 5.5 %collective-permute-start.33 = (f32[4096,2]{0,1:T(2,128)S(1)}, f32[4096,2]{0,1:T(2,128)S(1)}, u32[]{:S(2)}, u32[]{:S(2)}) collective-permute-start(f32[4096,2]{0,1:T(2,128)S(1)} %copy.88), channel_id=1, source_target_pairs={{0,1},{1,2},{2,3},{3,4},{4,5},{5,6},{6,7},{8,9},{9,10},{10,11},{11... | collective-permute-start | bytes 98312 | tf_op jit(solution)/shard_map/ppermute | solution.py:37
  20.2 2.2 fusion.30
  23.6 2.6 convert_reduce_fusion
  26.2 2.1 select_reduce_fusion.4
  31.2 1.3 collective-permute-start.35
  32.5 3.6 collective-permute-start.34
  37.7 2.0 copy.83
  39.7 2.2 pad_maximum_fusion.1
  42.8 430.6 %conditional.1 = (f32[4096,2048]{1,0:T(8,128)}) conditional(s32[]{:T(128)} %convert_element_type.49, (s32[1024]{0:T(1024)S(1)}, s32[1024]{0:T(1024)S(1)}, f32[4096,2048]{1,0:T(8,128)}, f32[8,2048]{1,0:T(8,128)S(1)}, f32[8,2048]{1,0:T(8,128)S(1)}, /*index=5*/f32[32,144,128]{2,1,0:T(8,128)S(1)}, f32[32,144,8]{1,0,2:T(8,128)S(1)}, ...), branch_computations={%region_8.16_spmd, %region_16.22_spmd} | conditional | flops 285427761152 | bytes 1123367424 | solution.py:840
  50.6 1.3 fusion.21
  52.9 1.0 fusion.7.chooser
  53.9 2.2 copy.86.row_weights
  56.8 0.9 select_reduce_fusion.cells
  57.7 70.4 %branch_1_fun.11 = (f32[4096,2048]{1,0:T(8,128)}, f32[80,4096]{1,0:T(8,128)}, f32[80,4096]{1,0:T(8,128)}) custom-call(f32[4096,2048]{1,0:T(8,128)} %get-tuple-element.250.main.prev.follow, f32[4096,2048]{1,0:T(8,128)} %get-tuple-element.250.main.prev.follow, f32[4096,2048]{1,0:T(8,128)} %get-tuple-element.250.main.prev.follow, ...), custom_call_target="tpu_custom_call" | custom-call | tf_op jit(solution)/shard_map/cond/branch_1_fun/pallas_call | solution.py:117
  128.0 15.9 %branch_1_fun.12 = (f32[304,2048]{1,0:T(8,128)}, f32[160,304]{1,0:T(8,128)}) custom-call(s32[304]{0:T(512)} %select_reduce_fusion.cells, bf16[160,2048]{1,0:T(8,128)(2,1)} %fusion.7.chooser, f32[4096,2048]{1,0:T(8,128)} %get-tuple-element.265.field), custom_call_target="tpu_custom_call" | custom-call | flops 40000000000 | bytes 1048576 | tf_op jit(solution)/shard_map/cond/branch_1_fun/pallas_call | solution.py:667
  143.9 1.3 collective-permute-start.3
  145.2 2.6 collective-permute-start.2
  147.9 1.6 collective-permute-start
  150.3 2.7 fusion.5.back
  153.0 2.0 fusion.4.place
  155.1 2.0 fusion.2.spots
  157.7 0.9 collective-permute-done.4
  158.9 4.1 fusion.3.known
  163.3 53.9 %branch_1_fun.13.slotted = f32[1280,1024]{1,0:T(8,128)} custom-call(f32[160,1024]{1,0:T(8,128)} %fusion.3.known), custom_call_target="tpu_custom_call" | custom-call | tf_op jit(solution)/shard_map/cond/branch_1_fun/pallas_call | solution.py:478
  217.2 2.3 collective-permute-start.8
  220.1 16.4 %branch_1_fun.14.g = f32[1024,1024]{1,0:T(8,128)} custom-call(f32[1280,1024]{1,0:T(8,128)} %branch_1_fun.13.slotted, bf16[1024,1280]{1,0:T(8,128)(2,1)} %fusion.4.place), custom_call_target="tpu_custom_call" | custom-call | flops 25500000256 | bytes 1048576 | tf_op jit(solution)/shard_map/cond/branch_1_fun/pallas_call | solution.py:195
  236.4 2.3 slice.403.block
  238.7 10.6 %collective-permute-done.8.refs_4_ = f32[80,4096]{1,0:T(8,128)S(1)} collective-permute-done((f32[80,4096]{1,0:T(8,128)}, f32[80,4096]{1,0:T(8,128)S(1)}, u32[]{:S(2)}, u32[]{:S(2)}) %collective-permute-start.8) | collective-permute-done | bytes 1310752 | tf_op jit(solution)/shard_map/cond/branch_1_fun/ppermute | solution.py:572
  249.3 1.4 collective-permute-start.10
  251.4 21.4 %branch_1_fun.15.x0 = f32[512,512]{1,0:T(8,128)} custom-call(f32[512,512]{1,0:T(8,128)} %slice.403.block, f32[1,512]{1,0:T(1,128)} %get-tuple-element.447.variance), custom_call_target="tpu_custom_call" | custom-call | flops 31499999232 | bytes 1048576 | tf_op jit(solution)/shard_map/cond/branch_1_fun/pallas_call | solution.py:195
  272.7 6.9 %branch_1_fun.16 = (f32[512,512]{1,0:T(8,128)}, f32[512,512]{1,0:T(8,128)}) custom-call(f32[1024,1024]{1,0:T(8,128)} %branch_1_fun.14.g, f32[512,512]{1,0:T(8,128)} %branch_1_fun.15.x0), custom_call_target="tpu_custom_call" | custom-call | flops 10499999744 | bytes 1048576 | tf_op jit(solution)/shard_map/cond/branch_1_fun/pallas_call | solution.py:195
  279.9 1.1 collective-permute-start.12
  281.0 1.1 collective-permute-start.13
  282.2 21.4 %branch_1_fun.17.x1 = f32[512,512]{1,0:T(8,128)} custom-call(f32[512,512]{1,0:T(8,128)} %get-tuple-element.282.block, f32[1,512]{1,0:T(1,128)} %get-tuple-element.446.variance), custom_call_target="tpu_custom_call" | custom-call | flops 31499999232 | bytes 1048576 | tf_op jit(solution)/shard_map/cond/branch_1_fun/pallas_call | solution.py:195
  303.6 6.2 %collective-permute-done.12.refs_8_ = f32[80,4096]{1,0:T(8,128)S(1)} collective-permute-done((f32[80,4096]{1,0:T(8,128)S(1)}, f32[80,4096]{1,0:T(8,128)S(1)}, u32[]{:S(2)}, u32[]{:S(2)}) %collective-permute-start.12) | collective-permute-done | bytes 1310752 | tf_op jit(solution)/shard_map/cond/branch_1_fun/ppermute | solution.py:572
  310.8 1.1 collective-permute-start.15
  311.9 28.8 %branch_1_fun.18 = (bf16[1280,1216]{1,0:T(8,128)(2,1)}, bf16[1280,1216]{1,0:T(8,128)(2,1)}) custom-call(f32[1024,1024]{1,0:T(8,128)} %branch_1_fun.14.g, f32[512,512]{1,0:T(8,128)} %branch_1_fun.15.x0, f32[512,512]{1,0:T(8,128)} %branch_1_fun.17.x1, f32[512,512]{1,0:T(8,128)} %get-tuple-element.283.carry, bf16[1024,1216]{1,0:T(8,128)(2,1)} %fusion.2.spots, ...), custom_call_target="tpu_custom_call" | custom-call | flops 38999998464 | bytes 1048576 | tf_op jit(solution)/shard_map/cond/branch_1_fun/pallas_call | solution.py:195
  341.7 1.4 collective-permute-start.17
  343.1 26.8 %branch_1_fun.19 = (bf16[1280,2048]{1,0:T(8,128)(2,1)}, bf16[1280,2048]{1,0:T(8,128)(2,1)}) custom-call(bf16[1280,1216]{1,0:T(8,128)(2,1)} %get-tuple-element.284.gain_coarse, bf16[1280,1216]{1,0:T(8,128)(2,1)} %get-tuple-element.285.gain_fine, f32[304,2048]{1,0:T(8,128)} %get-tuple-element.286.refs_0_, f32[304,2048]{1,0:T(8,128)} %collective-permute-done.5.refs_1_, ...), custom_call_target="tpu_custom_call" | custom-call | flops 19126026240 | bytes 31457280 | tf_op jit(solution)/shard_map/cond/branch_1_fun/pallas_call | solution.py:506
  370.8 1.2 collective-permute-start.19
  372.0 61.9 %branch_1_fun.20.field = f32[4096,2048]{1,0:T(8,128)} custom-call(f32[4096,2048]{1,0:T(8,128)} %get-tuple-element.265.field, bf16[1280,2048]{1,0:T(8,128)(2,1)} %get-tuple-element.287.weights_coarse, bf16[1280,2048]{1,0:T(8,128)(2,1)} %get-tuple-element.288.weights_fine, f32[80,4096]{1,0:T(8,128)} %get-tuple-element.266.refs_0_, ...), custom_call_target="tpu_custom_call" | custom-call | flops 64424509440 | bytes 67108864 | tf_op jit(solution)/shard_map/cond/branch_1_fun/pallas_call | solution.py:542
  433.9 1.1 copy-done.4
  435.0 38.1 %branch_1_fun.21 = f32[4096,2048]{1,0:T(8,128)} custom-call(f32[4096,2048]{1,0:T(8,128)} %branch_1_fun.20.field, bf16[1280,2048]{1,0:T(8,128)(2,1)} %get-tuple-element.287.weights_coarse, bf16[1280,2048]{1,0:T(8,128)(2,1)} %get-tuple-element.288.weights_fine, f32[80,4096]{1,0:T(8,128)} %copy-done.2, f32[80,4096]{1,0:T(8,128)} %copy-done.3, ...), custom_call_target="tpu_custom_call" | custom-call | flops 21474836480 | bytes 67108864 | tf_op jit(solution)/shard_map/cond/branch_1_fun/pallas_call | solution.py:542
  (212 shorter events, 15.1 us)
Async XLA Ops:
  0.9 41.8 %collective-permute-start.31 = (f32[8,2048]{1,0:T(8,128)S(1)}, f32[8,2048]{1,0:T(8,128)S(1)}, u32[]{:S(2)}, u32[]{:S(2)}) collective-permute-start(f32[8,2048]{1,0:T(8,128)S(1)} %get-tuple-element.452), channel_id=1, source_target_pairs={{8,0},{16,8},{24,16},{9,1},{17,9},{25,17},{10,2},{18,10},{26,18},{... | collective-permute-start | bytes 196616 | tf_op jit(solution)/shard_map/ppermute | solution.py:37
  2.2 40.5 %collective-permute-start.30 = (f32[8,2048]{1,0:T(8,128)S(1)}, f32[8,2048]{1,0:T(8,128)S(1)}, u32[]{:S(2)}, u32[]{:S(2)}) collective-permute-start(f32[8,2048]{1,0:T(8,128)S(1)} %get-tuple-element.453), channel_id=1, source_target_pairs={{0,8},{8,16},{16,24},{1,9},{9,17},{17,25},{2,10},{10,18},{18,26},{... | collective-permute-start | bytes 196616 | tf_op jit(solution)/shard_map/ppermute | solution.py:37
  9.4 9.9 %copy-start.19 = (s32[2,512]{1,0:T(2,128)S(1)}, s32[2,512]{1,0:T(2,128)}, u32[]{:S(2)}) copy-start(s32[2,512]{1,0:T(2,128)} %param.26) | copy-start | bytes 12292
  9.5 9.9 %copy-start.20 = (s32[2,512]{1,0:T(2,128)S(1)}, s32[2,512]{1,0:T(2,128)}, u32[]{:S(2)}) copy-start(s32[2,512]{1,0:T(2,128)} %param.27) | copy-start | bytes 12292
  9.5 9.9 %copy-start.5 = (f32[16384]{0:T(1024)S(1)}, f32[16384]{0:T(1024)}, u32[]{:S(2)}) copy-start(f32[16384]{0:T(1024)} %param.24) | copy-start | bytes 196612
  9.5 9.9 %copy-start.6 = (f32[16384]{0:T(1024)S(1)}, f32[16384]{0:T(1024)}, u32[]{:S(2)}) copy-start(f32[16384]{0:T(1024)} %param.23) | copy-start | bytes 196612
  9.5 10.0 %copy-start.10 = (s32[16384]{0:T(1024)S(1)}, s32[16384]{0:T(1024)}, u32[]{:S(2)}) copy-start(s32[16384]{0:T(1024)} %param.25) | copy-start | bytes 196612
  9.5 10.4 %copy-start.7 = (f32[16384]{0:T(1024)S(1)}, f32[16384]{0:T(1024)}, u32[]{:S(2)}) copy-start(f32[16384]{0:T(1024)} %param.21) | copy-start | bytes 196612
  9.5 10.4 %copy-start.8 = (f32[16384]{0:T(1024)S(1)}, f32[16384]{0:T(1024)}, u32[]{:S(2)}) copy-start(f32[16384]{0:T(1024)} %param.20) | copy-start | bytes 196612
  9.5 10.4 %copy-start.11 = (s32[16384]{0:T(1024)S(1)}, s32[16384]{0:T(1024)}, u32[]{:S(2)}) copy-start(s32[16384]{0:T(1024)} %param.22) | copy-start | bytes 196612
  11.8 19.3 %collective-permute-start.32 = (f32[4096,2]{0,1:T(2,128)S(1)}, f32[4096,2]{0,1:T(2,128)S(1)}, u32[]{:S(2)}, u32[]{:S(2)}) collective-permute-start(f32[4096,2]{0,1:T(2,128)S(1)} %copy.87), channel_id=1, source_target_pairs={{1,0},{2,1},{3,2},{4,3},{5,4},{6,5},{7,6},{9,8},{10,9},{11,10},{12... | collective-permute-start | bytes 98312 | tf_op jit(solution)/shard_map/ppermute | solution.py:37
  13.7 17.4 %collective-permute-start.33 = (f32[4096,2]{0,1:T(2,128)S(1)}, f32[4096,2]{0,1:T(2,128)S(1)}, u32[]{:S(2)}, u32[]{:S(2)}) collective-permute-start(f32[4096,2]{0,1:T(2,128)S(1)} %copy.88), channel_id=1, source_target_pairs={{0,1},{1,2},{2,3},{3,4},{4,5},{5,6},{6,7},{8,9},{9,10},{10,11},{11... | collective-permute-start | bytes 98312 | tf_op jit(solution)/shard_map/ppermute | solution.py:37
  28.4 7.8 %copy-start.12 = (s32[1024]{0:T(1024)}, s32[1024]{0:T(1024)S(1)}, u32[]{:S(2)}) copy-start(s32[1024]{0:T(1024)S(1)} %get-tuple-element.468) | copy-start | bytes 12292
  28.4 7.8 %copy-start.14 = (s32[1024]{0:T(1024)}, s32[1024]{0:T(1024)S(1)}, u32[]{:S(2)}) copy-start(s32[1024]{0:T(1024)S(1)} %get-tuple-element.469) | copy-start | bytes 12292
  31.2 4.9 %collective-permute-start.35 = (f32[8,4]{0,1:T(4,128)S(1)}, f32[8,4]{0,1:T(4,128)S(1)}, u32[]{:S(2)}, u32[]{:S(2)}) collective-permute-start(f32[8,4]{0,1:T(4,128)S(1)} %get-tuple-element.460), channel_id=1, source_target_pairs={{8,0},{16,8},{24,16},{9,1},{17,9},{25,17},{10,2},{18,10},{26,18},{... | collective-permute-start | bytes 392 | tf_op jit(solution)/shard_map/ppermute | solution.py:37
  32.5 4.4 collective-permute-start.34
  41.9 0.8 copy-start.13
  143.9 11.1 %copy-start.23 = (s32[4]{0:T(128)S(1)}, s32[4]{0:T(128)}, u32[]{:S(2)}) copy-start(s32[4]{0:T(128)} %constant.211.clone.1) | copy-start | bytes 52 | tf_op jit(solution)/shard_map/cond
  143.9 14.7 %copy-start.9 = (f32[160,304]{1,0:T(8,128)S(1)}, f32[160,304]{1,0:T(8,128)}, u32[]{:S(2)}) copy-start(f32[160,304]{1,0:T(8,128)} %get-tuple-element.275) | copy-start | bytes 583684 | tf_op jit(solution)/shard_map/cond
  143.9 13.7 %collective-permute-start.3 = (f32[160,304]{1,0:T(8,128)}, f32[160,304]{1,0:T(8,128)S(1)}, u32[]{:S(2)}, u32[]{:S(2)}) collective-permute-start(f32[160,304]{1,0:T(8,128)} %get-tuple-element.275), channel_id=1, source_target_pairs={{0,8},{8,0},{16,24},{24,16},{1,9},{9,1},{17,25},{25,17},{2,10},{10... | collective-permute-start | bytes 583688 | tf_op jit(solution)/shard_map/cond/branch_1_fun/ppermute | solution.py:592
  145.2 11.8 %collective-permute-start.2 = (f32[160,304]{1,0:T(8,128)}, f32[160,304]{1,0:T(8,128)S(1)}, u32[]{:S(2)}, u32[]{:S(2)}) collective-permute-start(f32[160,304]{1,0:T(8,128)} %get-tuple-element.275), channel_id=1, source_target_pairs={{0,16},{8,24},{16,0},{24,8},{1,17},{9,25},{17,1},{25,9},{2,18},{10... | collective-permute-start | bytes 583688 | tf_op jit(solution)/shard_map/cond/branch_1_fun/ppermute | solution.py:592
  147.9 69.3 %collective-permute-start = (f32[80,4096]{1,0:T(8,128)}, f32[80,4096]{1,0:T(8,128)}, u32[]{:S(2)}, u32[]{:S(2)}) collective-permute-start(f32[80,4096]{1,0:T(8,128)} %get-tuple-element.266.refs_0_), channel_id=1, source_target_pairs={{0,2},{2,4},{4,6},{6,7},{7,5},{5,3},{3,1},{1,0},{8,10},{10,12},{12... | collective-permute-start | bytes 3932168 | tf_op jit(solution)/shard_map/cond/branch_1_fun/ppermute | solution.py:572
  149.5 67.7 %collective-permute-start.1 = (f32[80,4096]{1,0:T(8,128)}, f32[80,4096]{1,0:T(8,128)}, u32[]{:S(2)}, u32[]{:S(2)}) collective-permute-start(f32[80,4096]{1,0:T(8,128)} %get-tuple-element.267.refs_1_), channel_id=1, source_target_pairs={{2,0},{4,2},{6,4},{7,6},{5,7},{3,5},{1,3},{0,1},{10,8},{12,10},{14... | collective-permute-start | bytes 3932168 | tf_op jit(solution)/shard_map/cond/branch_1_fun/ppermute | solution.py:573
  157.1 1.5 collective-permute-start.4
  163.0 180.1 %collective-permute-start.6 = (f32[304,2048]{1,0:T(8,128)}, f32[304,2048]{1,0:T(8,128)}, u32[]{:S(2)}, u32[]{:S(2)}) collective-permute-start(f32[304,2048]{1,0:T(8,128)} %get-tuple-element.286.refs_0_), channel_id=1, source_target_pairs={{0,8},{8,0},{16,24},{24,16},{1,9},{9,1},{17,25},{25,17},{2,10},{10... | collective-permute-start | bytes 7471112 | tf_op jit(solution)/shard_map/cond/branch_1_fun/ppermute | solution.py:592
  163.1 140.4 %collective-permute-start.5 = (f32[304,2048]{1,0:T(8,128)}, f32[304,2048]{1,0:T(8,128)}, u32[]{:S(2)}, u32[]{:S(2)}) collective-permute-start(f32[304,2048]{1,0:T(8,128)} %get-tuple-element.286.refs_0_), channel_id=1, source_target_pairs={{0,16},{8,24},{16,0},{24,8},{1,17},{9,25},{17,1},{25,9},{2,18},{10... | collective-permute-start | bytes 7471112 | tf_op jit(solution)/shard_map/cond/branch_1_fun/ppermute | solution.py:592
  217.2 32.1 %collective-permute-start.8 = (f32[80,4096]{1,0:T(8,128)}, f32[80,4096]{1,0:T(8,128)S(1)}, u32[]{:S(2)}, u32[]{:S(2)}) collective-permute-start(f32[80,4096]{1,0:T(8,128)} %collective-permute-done.refs_2_), channel_id=1, source_target_pairs={{0,2},{2,4},{4,6},{6,7},{7,5},{5,3},{3,1},{1,0},{8,10},{10,12},{12... | collective-permute-start | bytes 3932168 | tf_op jit(solution)/shard_map/cond/branch_1_fun/ppermute | solution.py:572
  219.5 31.3 %collective-permute-start.9 = (f32[80,4096]{1,0:T(8,128)}, f32[80,4096]{1,0:T(8,128)S(1)}, u32[]{:S(2)}, u32[]{:S(2)}) collective-permute-start(f32[80,4096]{1,0:T(8,128)} %collective-permute-done.1.refs_3_), channel_id=1, source_target_pairs={{2,0},{4,2},{6,4},{7,6},{5,7},{3,5},{1,3},{0,1},{10,8},{12,10},{14... | collective-permute-start | bytes 3932168 | tf_op jit(solution)/shard_map/cond/branch_1_fun/ppermute | solution.py:573
  249.3 23.4 %copy-start.24 = (f32[80,4096]{1,0:T(8,128)}, f32[80,4096]{1,0:T(8,128)S(1)}, u32[]{:S(2)}) copy-start(f32[80,4096]{1,0:T(8,128)S(1)} %collective-permute-done.8.refs_4_) | copy-start | bytes 3932164 | tf_op jit(solution)/shard_map/cond
  249.3 30.6 %collective-permute-start.10 = (f32[80,4096]{1,0:T(8,128)S(1)}, f32[80,4096]{1,0:T(8,128)S(1)}, u32[]{:S(2)}, u32[]{:S(2)}) collective-permute-start(f32[80,4096]{1,0:T(8,128)S(1)} %collective-permute-done.8.refs_4_), channel_id=1, source_target_pairs={{0,2},{2,4},{4,6},{6,7},{7,5},{5,3},{3,1},{1,0},{8,10},{10,12},{12... | collective-permute-start | bytes 3932168 | tf_op jit(solution)/shard_map/cond/branch_1_fun/ppermute | solution.py:572
  250.7 22.0 %copy-start.25 = (f32[80,4096]{1,0:T(8,128)}, f32[80,4096]{1,0:T(8,128)S(1)}, u32[]{:S(2)}) copy-start(f32[80,4096]{1,0:T(8,128)S(1)} %collective-permute-done.9.refs_5_) | copy-start | bytes 3932164 | tf_op jit(solution)/shard_map/cond
  250.7 30.3 %collective-permute-start.11 = (f32[80,4096]{1,0:T(8,128)S(1)}, f32[80,4096]{1,0:T(8,128)}, u32[]{:S(2)}, u32[]{:S(2)}) collective-permute-start(f32[80,4096]{1,0:T(8,128)S(1)} %collective-permute-done.9.refs_5_), channel_id=1, source_target_pairs={{2,0},{4,2},{6,4},{7,6},{5,7},{3,5},{1,3},{0,1},{10,8},{12,10},{14... | collective-permute-start | bytes 3932168 | tf_op jit(solution)/shard_map/cond/branch_1_fun/ppermute | solution.py:573
  279.9 23.6 %copy-start.26 = (f32[80,4096]{1,0:T(8,128)}, f32[80,4096]{1,0:T(8,128)S(1)}, u32[]{:S(2)}) copy-start(f32[80,4096]{1,0:T(8,128)S(1)} %collective-permute-done.10.refs_6_) | copy-start | bytes 3932164 | tf_op jit(solution)/shard_map/cond
  279.9 29.9 %collective-permute-start.12 = (f32[80,4096]{1,0:T(8,128)S(1)}, f32[80,4096]{1,0:T(8,128)S(1)}, u32[]{:S(2)}, u32[]{:S(2)}) collective-permute-start(f32[80,4096]{1,0:T(8,128)S(1)} %collective-permute-done.10.refs_6_), channel_id=1, source_target_pairs={{0,2},{2,4},{4,6},{6,7},{7,5},{5,3},{3,1},{1,0},{8,10},{10,12},{12... | collective-permute-start | bytes 3932168 | tf_op jit(solution)/shard_map/cond/branch_1_fun/ppermute | solution.py:572
  281.0 29.8 %collective-permute-start.13 = (f32[80,4096]{1,0:T(8,128)}, f32[80,4096]{1,0:T(8,128)S(1)}, u32[]{:S(2)}, u32[]{:S(2)}) collective-permute-start(f32[80,4096]{1,0:T(8,128)} %collective-permute-done.11.refs_7_), channel_id=1, source_target_pairs={{2,0},{4,2},{6,4},{7,6},{5,7},{3,5},{1,3},{0,1},{10,8},{12,10},{14... | collective-permute-start | bytes 3932168 | tf_op jit(solution)/shard_map/cond/branch_1_fun/ppermute | solution.py:573
  303.6 39.6 %collective-permute-start.7 = (f32[304,2048]{1,0:T(8,128)}, f32[304,2048]{1,0:T(8,128)}, u32[]{:S(2)}, u32[]{:S(2)}) collective-permute-start(f32[304,2048]{1,0:T(8,128)} %collective-permute-done.5.refs_1_), channel_id=1, source_target_pairs={{0,8},{8,0},{16,24},{24,16},{1,9},{9,1},{17,25},{25,17},{2,10},{10... | collective-permute-start | bytes 7471112 | tf_op jit(solution)/shard_map/cond/branch_1_fun/ppermute | solution.py:592
  309.8 31.0 %copy-start.27 = (f32[80,4096]{1,0:T(8,128)}, f32[80,4096]{1,0:T(8,128)S(1)}, u32[]{:S(2)}) copy-start(f32[80,4096]{1,0:T(8,128)S(1)} %collective-permute-done.12.refs_8_) | copy-start | bytes 3932164 | tf_op jit(solution)/shard_map/cond
  309.8 31.0 %collective-permute-start.14 = (f32[80,4096]{1,0:T(8,128)S(1)}, f32[80,4096]{1,0:T(8,128)S(1)}, u32[]{:S(2)}, u32[]{:S(2)}) collective-permute-start(f32[80,4096]{1,0:T(8,128)S(1)} %collective-permute-done.12.refs_8_), channel_id=1, source_target_pairs={{0,2},{2,4},{4,6},{6,7},{7,5},{5,3},{3,1},{1,0},{8,10},{10,12},{12... | collective-permute-start | bytes 3932168 | tf_op jit(solution)/shard_map/cond/branch_1_fun/ppermute | solution.py:572
  310.8 30.0 %copy-start.28 = (f32[80,4096]{1,0:T(8,128)}, f32[80,4096]{1,0:T(8,128)S(1)}, u32[]{:S(2)}) copy-start(f32[80,4096]{1,0:T(8,128)S(1)} %collective-permute-done.13.refs_9_) | copy-start | bytes 3932164 | tf_op jit(solution)/shard_map/cond
  310.8 30.9 %collective-permute-start.15 = (f32[80,4096]{1,0:T(8,128)S(1)}, f32[80,4096]{1,0:T(8,128)}, u32[]{:S(2)}, u32[]{:S(2)}) collective-permute-start(f32[80,4096]{1,0:T(8,128)S(1)} %collective-permute-done.13.refs_9_), channel_id=1, source_target_pairs={{2,0},{4,2},{6,4},{7,6},{5,7},{3,5},{1,3},{0,1},{10,8},{12,10},{14... | collective-permute-start | bytes 3932168 | tf_op jit(solution)/shard_map/cond/branch_1_fun/ppermute | solution.py:573
  340.8 29.1 %copy-start.29 = (f32[80,4096]{1,0:T(8,128)}, f32[80,4096]{1,0:T(8,128)S(1)}, u32[]{:S(2)}) copy-start(f32[80,4096]{1,0:T(8,128)S(1)} %collective-permute-done.14.refs_10_) | copy-start | bytes 3932164 | tf_op jit(solution)/shard_map/cond
  340.8 29.1 %collective-permute-start.16 = (f32[80,4096]{1,0:T(8,128)S(1)}, f32[80,4096]{1,0:T(8,128)S(1)}, u32[]{:S(2)}, u32[]{:S(2)}) collective-permute-start(f32[80,4096]{1,0:T(8,128)S(1)} %collective-permute-done.14.refs_10_), channel_id=1, source_target_pairs={{0,2},{2,4},{4,6},{6,7},{7,5},{5,3},{3,1},{1,0},{8,10},{10,12},{12... | collective-permute-start | bytes 3932168 | tf_op jit(solution)/shard_map/cond/branch_1_fun/ppermute | solution.py:572
  341.7 29.1 %collective-permute-start.17 = (f32[80,4096]{1,0:T(8,128)}, f32[80,4096]{1,0:T(8,128)S(1)}, u32[]{:S(2)}, u32[]{:S(2)}) collective-permute-start(f32[80,4096]{1,0:T(8,128)} %collective-permute-done.15.refs_11_), channel_id=1, source_target_pairs={{2,0},{4,2},{6,4},{7,6},{5,7},{3,5},{1,3},{0,1},{10,8},{12,10},{14... | collective-permute-start | bytes 3932168 | tf_op jit(solution)/shard_map/cond/branch_1_fun/ppermute | solution.py:573
  369.9 64.0 %copy-start.2 = (f32[80,4096]{1,0:T(8,128)}, f32[80,4096]{1,0:T(8,128)S(1)}, u32[]{:S(2)}) copy-start(f32[80,4096]{1,0:T(8,128)S(1)} %collective-permute-done.16.refs_0_) | copy-start | bytes 3932164 | tf_op jit(solution)/shard_map/cond
  369.9 64.0 %collective-permute-start.18 = (f32[80,4096]{1,0:T(8,128)S(1)}, f32[80,4096]{1,0:T(8,128)S(1)}, u32[]{:S(2)}, u32[]{:S(2)}) collective-permute-start(f32[80,4096]{1,0:T(8,128)S(1)} %collective-permute-done.16.refs_0_), channel_id=1, source_target_pairs={{0,2},{2,4},{4,6},{6,7},{7,5},{5,3},{3,1},{1,0},{8,10},{10,12},{12... | collective-permute-start | bytes 3932168 | tf_op jit(solution)/shard_map/cond/branch_1_fun/ppermute | solution.py:572
  370.8 63.1 %copy-start.3 = (f32[80,4096]{1,0:T(8,128)}, f32[80,4096]{1,0:T(8,128)S(1)}, u32[]{:S(2)}) copy-start(f32[80,4096]{1,0:T(8,128)S(1)} %collective-permute-done.17.refs_1_) | copy-start | bytes 3932164 | tf_op jit(solution)/shard_map/cond
  370.8 63.1 %collective-permute-start.19 = (f32[80,4096]{1,0:T(8,128)S(1)}, f32[80,4096]{1,0:T(8,128)}, u32[]{:S(2)}, u32[]{:S(2)}) collective-permute-start(f32[80,4096]{1,0:T(8,128)S(1)} %collective-permute-done.17.refs_1_), channel_id=1, source_target_pairs={{2,0},{4,2},{6,4},{7,6},{5,7},{3,5},{1,3},{0,1},{10,8},{12,10},{14... | collective-permute-start | bytes 3932168 | tf_op jit(solution)/shard_map/cond/branch_1_fun/ppermute | solution.py:573
  433.9 1.1 copy-start.4
  (6 other events, 4.3 us)

commit v6 on v5

--- a/solution.py
+++ b/solution.py
@@ -9,7 +9,7 @@
 STEPS = 2
 MARGIN = 8
 LANES = 128
-TILE = 128
+TILE = 256
 HIGHEST = lax.Precision.HIGHEST
 LAST = 4
 SCALE = 1.5
@@ -219,7 +219,7 @@
 def invert_kernel(block, variance, x, s, sp, xp, ep):
     k = s.shape[0]
     step = chunk(k)
-    cut(xp, block[...])
+    cut(xp, block[:k, :k])
 
     def innovation(rows):
         s[rows, :] = unit_rows(rows, k) * variance[...] + joined(xp, xp, rows, across)
@@ -385,7 +385,7 @@
             invert_kernel, [square], scratch, block, variance[b : b + 1], cost=21
         )[0]
 
-    x0 = inverse(g[:k, :k], 0)
+    x0 = inverse(g, 0)
     carry, block = whole_call(deflate_kernel, [square, square], [terms, terms], g, x0, cost=7)
     x1 = inverse(block, 1)
     out = ((slots, spots.shape[1]), jnp.bfloat16)

time: 483 us -> 479 us (level)
  transfers between devices with their start and end apart: 26 -> 26, of which waited for: 6 -> 5; matrix products, arithmetic and copies ran while one was open for 8% -> 7% of each run, Pallas kernels for 50% -> 50%
where the time goes in v6:
time: 479 us; the launch traced here: 472 us
  Pallas kernels  358 us (75%)
  starting transfers between devices  36.2 us (8%)
  other arithmetic  23 us (5%)
  waiting for transfers between devices  21.4 us (4%)
  local copies, waits for them, and re-layouts  16.5 us (3%)
  loops' own time  9.27 us (2%)
    pallas_call x2, Pallas kernels, update(): pl.pallas_call(update_kernel, grid=(rows // tall,), in_specs=[tile, held,...  100 us
    pallas_call x5, Pallas kernels, whole_call(): pl.pallas_call(kernel, in_specs=[whole] * len(args), out_specs=[whole] *...  95.8 us
    pallas_call x1, Pallas kernels, transport(): pl.pallas_call(transport_kernel, grid=(tiles,), in_specs=[pl.BlockSpec((T...  66 us
    pallas_call x1, Pallas kernels, crossing_gather(): pl.pallas_call(crossing_kernel, in_specs=[whole], out_specs=whole, out_sh...  53.9 us
    pallas_call x1, Pallas kernels, weights_of(): pl.pallas_call(weights_kernel, grid=(cols // wide,), in_specs=[held, held...  26.7 us
    ppermute x7, waiting for transfers between devices, ring_gather(): ups.append(lax.ppermute(ups[-1], axis, ahead))  19.5 us
    ppermute x6, starting transfers between devices, edges(): return (lax.ppermute(last, axis, up), lax.ppermute(leading, axis, down))  16 us
    pallas_call x1, Pallas kernels, pick(): pl.pallas_call(pick_kernel, in_specs=[pl.BlockSpec(memory_space=pltpu.SME...  15.8 us
  transfers between devices with their start and end apart: 26, of which 5 were waited for; matrix products, arithmetic and copies ran while one was open for 7% of the time, Pallas kernels for 50%

profile of v6, /device:TPU:0, one launch (start us, length us, event | category | flops | bytes accessed | tf_op | source)
XLA Modules:
  0.0 472.0 jit_solution(1177623506981145990)
XLA Ops:
  0.9 1.3 collective-permute-start.31
  2.2 3.0 collective-permute-start.30
  5.2 4.2 fusion.46
  9.5 2.3 copy.55
  11.8 1.3 collective-permute-start.32
  13.7 5.5 %collective-permute-start.33 = (f32[4096,2]{0,1:T(2,128)S(1)}, f32[4096,2]{0,1:T(2,128)S(1)}, u32[]{:S(2)}, u32[]{:S(2)}) collective-permute-start(f32[4096,2]{0,1:T(2,128)S(1)} %copy.56), channel_id=1, source_target_pairs={{0,1},{1,2},{2,3},{3,4},{4,5},{5,6},{6,7},{8,9},{9,10},{10,11},{11... | collective-permute-start | bytes 98312 | tf_op jit(solution)/shard_map/ppermute | solution.py:37
  20.2 2.2 fusion.30
  23.6 2.6 convert_reduce_fusion
  26.1 2.1 select_reduce_fusion.4
  31.1 1.3 collective-permute-start.35
  32.4 3.6 collective-permute-start.34
  37.6 2.0 copy.51
  39.6 2.2 pad_maximum_fusion.1
  42.5 428.2 %conditional.1 = (f32[4096,2048]{1,0:T(8,128)}) conditional(s32[]{:T(128)} %convert_element_type.49, (s32[1024]{0:T(1024)S(1)}, s32[1024]{0:T(1024)S(1)}, f32[4096,2048]{1,0:T(8,128)}, f32[8,2048]{1,0:T(8,128)S(1)}, f32[8,2048]{1,0:T(8,128)S(1)}, /*index=5*/f32[16,272,128]{2,1,0:T(8,128)S(1)}, f32[16,272,8]{1,0,2:T(8,128)S(1)}, ...), branch_computations={%region_8.16_spmd, %region_16.22_spmd} | conditional | flops 285427761152 | bytes 1123351040 | solution.py:840
  51.4 1.3 fusion.21
  53.6 1.0 fusion.7.chooser
  54.7 2.1 copy.54.row_weights
  57.4 0.9 select_reduce_fusion.cells
  58.3 66.0 %branch_1_fun.11 = (f32[4096,2048]{1,0:T(8,128)}, f32[80,4096]{1,0:T(8,128)}, f32[80,4096]{1,0:T(8,128)}) custom-call(f32[4096,2048]{1,0:T(8,128)} %get-tuple-element.250.main.prev.follow, f32[4096,2048]{1,0:T(8,128)} %get-tuple-element.250.main.prev.follow, f32[4096,2048]{1,0:T(8,128)} %get-tuple-element.250.main.prev.follow, ...), custom_call_target="tpu_custom_call" | custom-call | tf_op jit(solution)/shard_map/cond/branch_1_fun/pallas_call | solution.py:117
  124.3 15.8 %branch_1_fun.12 = (f32[304,2048]{1,0:T(8,128)}, f32[160,304]{1,0:T(8,128)}) custom-call(s32[304]{0:T(512)} %select_reduce_fusion.cells, bf16[160,2048]{1,0:T(8,128)(2,1)} %fusion.7.chooser, f32[4096,2048]{1,0:T(8,128)} %get-tuple-element.265.field), custom_call_target="tpu_custom_call" | custom-call | flops 40000000000 | bytes 1048576 | tf_op jit(solution)/shard_map/cond/branch_1_fun/pallas_call | solution.py:667
  140.2 1.3 collective-permute-start.3
  141.5 2.6 collective-permute-start.2
  144.1 1.6 collective-permute-start
  146.6 2.7 fusion.5.back
  149.3 2.0 fusion.4.place
  151.3 2.0 fusion.2.spots
  155.2 4.1 fusion.3.known
  159.5 53.9 %branch_1_fun.13.slotted = f32[1280,1024]{1,0:T(8,128)} custom-call(f32[160,1024]{1,0:T(8,128)} %fusion.3.known), custom_call_target="tpu_custom_call" | custom-call | tf_op jit(solution)/shard_map/cond/branch_1_fun/pallas_call | solution.py:478
  213.5 2.4 collective-permute-start.8
  216.3 16.4 %branch_1_fun.14.block.g = f32[1024,1024]{1,0:T(8,128)} custom-call(f32[1280,1024]{1,0:T(8,128)} %branch_1_fun.13.slotted, bf16[1024,1280]{1,0:T(8,128)(2,1)} %fusion.4.place), custom_call_target="tpu_custom_call" | custom-call | flops 25500000256 | bytes 1048576 | tf_op jit(solution)/shard_map/cond/branch_1_fun/pallas_call | solution.py:195
  232.7 13.1 %collective-permute-done.8.refs_4_ = f32[80,4096]{1,0:T(8,128)S(1)} collective-permute-done((f32[80,4096]{1,0:T(8,128)}, f32[80,4096]{1,0:T(8,128)S(1)}, u32[]{:S(2)}, u32[]{:S(2)}) %collective-permute-start.8) | collective-permute-done | bytes 1310752 | tf_op jit(solution)/shard_map/cond/branch_1_fun/ppermute | solution.py:572
  245.8 1.4 collective-permute-start.10
  247.8 22.3 %branch_1_fun.15.x0 = f32[512,512]{1,0:T(8,128)} custom-call(f32[1024,1024]{1,0:T(8,128)} %branch_1_fun.14.block.g, f32[1,512]{1,0:T(1,128)} %get-tuple-element.447.variance), custom_call_target="tpu_custom_call" | custom-call | flops 31499999232 | bytes 1048576 | tf_op jit(solution)/shard_map/cond/branch_1_fun/pallas_call | solution.py:195
  270.1 6.9 %branch_1_fun.16 = (f32[512,512]{1,0:T(8,128)}, f32[512,512]{1,0:T(8,128)}) custom-call(f32[1024,1024]{1,0:T(8,128)} %branch_1_fun.14.block.g, f32[512,512]{1,0:T(8,128)} %branch_1_fun.15.x0), custom_call_target="tpu_custom_call" | custom-call | flops 10499999744 | bytes 1048576 | tf_op jit(solution)/shard_map/cond/branch_1_fun/pallas_call | solution.py:195
  277.0 1.4 collective-permute-start.12
  279.3 21.4 %branch_1_fun.17.x1 = f32[512,512]{1,0:T(8,128)} custom-call(f32[512,512]{1,0:T(8,128)} %get-tuple-element.282.block, f32[1,512]{1,0:T(1,128)} %get-tuple-element.446.variance), custom_call_target="tpu_custom_call" | custom-call | flops 31499999232 | bytes 1048576 | tf_op jit(solution)/shard_map/cond/branch_1_fun/pallas_call | solution.py:195
  300.7 6.4 %collective-permute-done.12.refs_8_ = f32[80,4096]{1,0:T(8,128)S(1)} collective-permute-done((f32[80,4096]{1,0:T(8,128)S(1)}, f32[80,4096]{1,0:T(8,128)S(1)}, u32[]{:S(2)}, u32[]{:S(2)}) %collective-permute-start.12) | collective-permute-done | bytes 1310752 | tf_op jit(solution)/shard_map/cond/branch_1_fun/ppermute | solution.py:572
  307.1 1.0 collective-permute-start.14
  308.2 1.1 collective-permute-start.15
  309.3 28.8 %branch_1_fun.18 = (bf16[1280,1216]{1,0:T(8,128)(2,1)}, bf16[1280,1216]{1,0:T(8,128)(2,1)}) custom-call(f32[1024,1024]{1,0:T(8,128)} %branch_1_fun.14.block.g, f32[512,512]{1,0:T(8,128)} %branch_1_fun.15.x0, f32[512,512]{1,0:T(8,128)} %branch_1_fun.17.x1, f32[512,512]{1,0:T(8,128)} %get-tuple-element.283.carry, bf16[1024,1216]{1,0:T(8,128)(2,1)} %fusion.2.spots, ...), custom_call_target="tpu_custom_call" | custom-call | flops 38999998464 | bytes 1048576 | tf_op jit(solution)/shard_map/cond/branch_1_fun/pallas_call | solution.py:195
  338.1 1.0 collective-permute-start.16
  339.2 1.3 collective-permute-start.17
  340.5 26.7 %branch_1_fun.19 = (bf16[1280,2048]{1,0:T(8,128)(2,1)}, bf16[1280,2048]{1,0:T(8,128)(2,1)}) custom-call(bf16[1280,1216]{1,0:T(8,128)(2,1)} %get-tuple-element.284.gain_coarse, bf16[1280,1216]{1,0:T(8,128)(2,1)} %get-tuple-element.285.gain_fine, f32[304,2048]{1,0:T(8,128)} %get-tuple-element.286.refs_0_, f32[304,2048]{1,0:T(8,128)} %collective-permute-done.5.refs_1_, ...), custom_call_target="tpu_custom_call" | custom-call | flops 19126026240 | bytes 31457280 | tf_op jit(solution)/shard_map/cond/branch_1_fun/pallas_call | solution.py:506
  367.2 1.0 collective-permute-start.18
  368.3 1.1 collective-permute-start.19
  369.3 61.9 %branch_1_fun.20.field = f32[4096,2048]{1,0:T(8,128)} custom-call(f32[4096,2048]{1,0:T(8,128)} %get-tuple-element.265.field, bf16[1280,2048]{1,0:T(8,128)(2,1)} %get-tuple-element.287.weights_coarse, bf16[1280,2048]{1,0:T(8,128)(2,1)} %get-tuple-element.288.weights_fine, f32[80,4096]{1,0:T(8,128)} %get-tuple-element.266.refs_0_, ...), custom_call_target="tpu_custom_call" | custom-call | flops 64424509440 | bytes 67108864 | tf_op jit(solution)/shard_map/cond/branch_1_fun/pallas_call | solution.py:542
  431.3 1.1 copy-done.4
  432.3 38.1 %branch_1_fun.21 = f32[4096,2048]{1,0:T(8,128)} custom-call(f32[4096,2048]{1,0:T(8,128)} %branch_1_fun.20.field, bf16[1280,2048]{1,0:T(8,128)(2,1)} %get-tuple-element.287.weights_coarse, bf16[1280,2048]{1,0:T(8,128)(2,1)} %get-tuple-element.288.weights_fine, f32[80,4096]{1,0:T(8,128)} %copy-done.2, f32[80,4096]{1,0:T(8,128)} %copy-done.3, ...), custom_call_target="tpu_custom_call" | custom-call | flops 21474836480 | bytes 67108864 | tf_op jit(solution)/shard_map/cond/branch_1_fun/pallas_call | solution.py:542
  (179 shorter events, 13.8 us)
Async XLA Ops:
  0.9 41.5 %collective-permute-start.31 = (f32[8,2048]{1,0:T(8,128)S(1)}, f32[8,2048]{1,0:T(8,128)S(1)}, u32[]{:S(2)}, u32[]{:S(2)}) collective-permute-start(f32[8,2048]{1,0:T(8,128)S(1)} %get-tuple-element.452), channel_id=1, source_target_pairs={{8,0},{16,8},{24,16},{9,1},{17,9},{25,17},{10,2},{18,10},{26,18},{... | collective-permute-start | bytes 196616 | tf_op jit(solution)/shard_map/ppermute | solution.py:37
  2.2 40.2 %collective-permute-start.30 = (f32[8,2048]{1,0:T(8,128)S(1)}, f32[8,2048]{1,0:T(8,128)S(1)}, u32[]{:S(2)}, u32[]{:S(2)}) collective-permute-start(f32[8,2048]{1,0:T(8,128)S(1)} %get-tuple-element.453), channel_id=1, source_target_pairs={{0,8},{8,16},{16,24},{1,9},{9,17},{17,25},{2,10},{10,18},{18,26},{... | collective-permute-start | bytes 196616 | tf_op jit(solution)/shard_map/ppermute | solution.py:37
  9.4 9.9 %copy-start.19 = (s32[2,512]{1,0:T(2,128)S(1)}, s32[2,512]{1,0:T(2,128)}, u32[]{:S(2)}) copy-start(s32[2,512]{1,0:T(2,128)} %param.26) | copy-start | bytes 12292
  9.5 9.9 %copy-start.20 = (s32[2,512]{1,0:T(2,128)S(1)}, s32[2,512]{1,0:T(2,128)}, u32[]{:S(2)}) copy-start(s32[2,512]{1,0:T(2,128)} %param.27) | copy-start | bytes 12292
  9.5 9.9 %copy-start.5 = (f32[16384]{0:T(1024)S(1)}, f32[16384]{0:T(1024)}, u32[]{:S(2)}) copy-start(f32[16384]{0:T(1024)} %param.24) | copy-start | bytes 196612
  9.5 9.9 %copy-start.6 = (f32[16384]{0:T(1024)S(1)}, f32[16384]{0:T(1024)}, u32[]{:S(2)}) copy-start(f32[16384]{0:T(1024)} %param.23) | copy-start | bytes 196612
  9.5 10.0 %copy-start.10 = (s32[16384]{0:T(1024)S(1)}, s32[16384]{0:T(1024)}, u32[]{:S(2)}) copy-start(s32[16384]{0:T(1024)} %param.25) | copy-start | bytes 196612
  9.5 10.4 %copy-start.7 = (f32[16384]{0:T(1024)S(1)}, f32[16384]{0:T(1024)}, u32[]{:S(2)}) copy-start(f32[16384]{0:T(1024)} %param.21) | copy-start | bytes 196612
  9.5 10.4 %copy-start.8 = (f32[16384]{0:T(1024)S(1)}, f32[16384]{0:T(1024)}, u32[]{:S(2)}) copy-start(f32[16384]{0:T(1024)} %param.20) | copy-start | bytes 196612
  9.5 10.4 %copy-start.11 = (s32[16384]{0:T(1024)S(1)}, s32[16384]{0:T(1024)}, u32[]{:S(2)}) copy-start(s32[16384]{0:T(1024)} %param.22) | copy-start | bytes 196612
  11.8 19.2 %collective-permute-start.32 = (f32[4096,2]{0,1:T(2,128)S(1)}, f32[4096,2]{0,1:T(2,128)S(1)}, u32[]{:S(2)}, u32[]{:S(2)}) collective-permute-start(f32[4096,2]{0,1:T(2,128)S(1)} %copy.55), channel_id=1, source_target_pairs={{1,0},{2,1},{3,2},{4,3},{5,4},{6,5},{7,6},{9,8},{10,9},{11,10},{12... | collective-permute-start | bytes 98312 | tf_op jit(solution)/shard_map/ppermute | solution.py:37
  13.7 17.3 %collective-permute-start.33 = (f32[4096,2]{0,1:T(2,128)S(1)}, f32[4096,2]{0,1:T(2,128)S(1)}, u32[]{:S(2)}, u32[]{:S(2)}) collective-permute-start(f32[4096,2]{0,1:T(2,128)S(1)} %copy.56), channel_id=1, source_target_pairs={{0,1},{1,2},{2,3},{3,4},{4,5},{5,6},{6,7},{8,9},{9,10},{10,11},{11... | collective-permute-start | bytes 98312 | tf_op jit(solution)/shard_map/ppermute | solution.py:37
  28.3 7.8 %copy-start.12 = (s32[1024]{0:T(1024)}, s32[1024]{0:T(1024)S(1)}, u32[]{:S(2)}) copy-start(s32[1024]{0:T(1024)S(1)} %get-tuple-element.468) | copy-start | bytes 12292
  28.3 7.8 %copy-start.14 = (s32[1024]{0:T(1024)}, s32[1024]{0:T(1024)S(1)}, u32[]{:S(2)}) copy-start(s32[1024]{0:T(1024)S(1)} %get-tuple-element.469) | copy-start | bytes 12292
  31.1 4.9 %collective-permute-start.35 = (f32[8,4]{0,1:T(4,128)S(1)}, f32[8,4]{0,1:T(4,128)S(1)}, u32[]{:S(2)}, u32[]{:S(2)}) collective-permute-start(f32[8,4]{0,1:T(4,128)S(1)} %get-tuple-element.460), channel_id=1, source_target_pairs={{8,0},{16,8},{24,16},{9,1},{17,9},{25,17},{10,2},{18,10},{26,18},{... | collective-permute-start | bytes 392 | tf_op jit(solution)/shard_map/ppermute | solution.py:37
  32.4 4.4 collective-permute-start.34
  41.8 0.7 copy-start.16
  140.2 11.1 %copy-start.23 = (s32[4]{0:T(128)S(1)}, s32[4]{0:T(128)}, u32[]{:S(2)}) copy-start(s32[4]{0:T(128)} %constant.211.clone.1) | copy-start | bytes 52 | tf_op jit(solution)/shard_map/cond
  140.2 14.7 %copy-start.9 = (f32[160,304]{1,0:T(8,128)S(1)}, f32[160,304]{1,0:T(8,128)}, u32[]{:S(2)}) copy-start(f32[160,304]{1,0:T(8,128)} %get-tuple-element.275) | copy-start | bytes 583684 | tf_op jit(solution)/shard_map/cond
  140.2 13.8 %collective-permute-start.3 = (f32[160,304]{1,0:T(8,128)}, f32[160,304]{1,0:T(8,128)S(1)}, u32[]{:S(2)}, u32[]{:S(2)}) collective-permute-start(f32[160,304]{1,0:T(8,128)} %get-tuple-element.275), channel_id=1, source_target_pairs={{0,8},{8,0},{16,24},{24,16},{1,9},{9,1},{17,25},{25,17},{2,10},{10... | collective-permute-start | bytes 583688 | tf_op jit(solution)/shard_map/cond/branch_1_fun/ppermute | solution.py:592
  141.5 11.8 %collective-permute-start.2 = (f32[160,304]{1,0:T(8,128)}, f32[160,304]{1,0:T(8,128)S(1)}, u32[]{:S(2)}, u32[]{:S(2)}) collective-permute-start(f32[160,304]{1,0:T(8,128)} %get-tuple-element.275), channel_id=1, source_target_pairs={{0,16},{8,24},{16,0},{24,8},{1,17},{9,25},{17,1},{25,9},{2,18},{10... | collective-permute-start | bytes 583688 | tf_op jit(solution)/shard_map/cond/branch_1_fun/ppermute | solution.py:592
  144.1 69.3 %collective-permute-start = (f32[80,4096]{1,0:T(8,128)}, f32[80,4096]{1,0:T(8,128)}, u32[]{:S(2)}, u32[]{:S(2)}) collective-permute-start(f32[80,4096]{1,0:T(8,128)} %get-tuple-element.266.refs_0_), channel_id=1, source_target_pairs={{0,2},{2,4},{4,6},{6,7},{7,5},{5,3},{3,1},{1,0},{8,10},{10,12},{12... | collective-permute-start | bytes 3932168 | tf_op jit(solution)/shard_map/cond/branch_1_fun/ppermute | solution.py:572
  145.7 67.7 %collective-permute-start.1 = (f32[80,4096]{1,0:T(8,128)}, f32[80,4096]{1,0:T(8,128)}, u32[]{:S(2)}, u32[]{:S(2)}) collective-permute-start(f32[80,4096]{1,0:T(8,128)} %get-tuple-element.267.refs_1_), channel_id=1, source_target_pairs={{2,0},{4,2},{6,4},{7,6},{5,7},{3,5},{1,3},{0,1},{10,8},{12,10},{14... | collective-permute-start | bytes 3932168 | tf_op jit(solution)/shard_map/cond/branch_1_fun/ppermute | solution.py:573
  153.4 1.5 collective-permute-start.4
  159.3 181.2 %collective-permute-start.6 = (f32[304,2048]{1,0:T(8,128)}, f32[304,2048]{1,0:T(8,128)}, u32[]{:S(2)}, u32[]{:S(2)}) collective-permute-start(f32[304,2048]{1,0:T(8,128)} %get-tuple-element.286.refs_0_), channel_id=1, source_target_pairs={{0,8},{8,0},{16,24},{24,16},{1,9},{9,1},{17,25},{25,17},{2,10},{10... | collective-permute-start | bytes 7471112 | tf_op jit(solution)/shard_map/cond/branch_1_fun/ppermute | solution.py:592
  159.4 141.3 %collective-permute-start.5 = (f32[304,2048]{1,0:T(8,128)}, f32[304,2048]{1,0:T(8,128)}, u32[]{:S(2)}, u32[]{:S(2)}) collective-permute-start(f32[304,2048]{1,0:T(8,128)} %get-tuple-element.286.refs_0_), channel_id=1, source_target_pairs={{0,16},{8,24},{16,0},{24,8},{1,17},{9,25},{17,1},{25,9},{2,18},{10... | collective-permute-start | bytes 7471112 | tf_op jit(solution)/shard_map/cond/branch_1_fun/ppermute | solution.py:592
  213.5 32.3 %collective-permute-start.8 = (f32[80,4096]{1,0:T(8,128)}, f32[80,4096]{1,0:T(8,128)S(1)}, u32[]{:S(2)}, u32[]{:S(2)}) collective-permute-start(f32[80,4096]{1,0:T(8,128)} %collective-permute-done.refs_2_), channel_id=1, source_target_pairs={{0,2},{2,4},{4,6},{6,7},{7,5},{5,3},{3,1},{1,0},{8,10},{10,12},{12... | collective-permute-start | bytes 3932168 | tf_op jit(solution)/shard_map/cond/branch_1_fun/ppermute | solution.py:572
  215.9 31.3 %collective-permute-start.9 = (f32[80,4096]{1,0:T(8,128)}, f32[80,4096]{1,0:T(8,128)S(1)}, u32[]{:S(2)}, u32[]{:S(2)}) collective-permute-start(f32[80,4096]{1,0:T(8,128)} %collective-permute-done.1.refs_3_), channel_id=1, source_target_pairs={{2,0},{4,2},{6,4},{7,6},{5,7},{3,5},{1,3},{0,1},{10,8},{12,10},{14... | collective-permute-start | bytes 3932168 | tf_op jit(solution)/shard_map/cond/branch_1_fun/ppermute | solution.py:573
  245.8 24.4 %copy-start.24 = (f32[80,4096]{1,0:T(8,128)}, f32[80,4096]{1,0:T(8,128)S(1)}, u32[]{:S(2)}) copy-start(f32[80,4096]{1,0:T(8,128)S(1)} %collective-permute-done.8.refs_4_) | copy-start | bytes 3932164 | tf_op jit(solution)/shard_map/cond
  245.8 31.3 %collective-permute-start.10 = (f32[80,4096]{1,0:T(8,128)S(1)}, f32[80,4096]{1,0:T(8,128)S(1)}, u32[]{:S(2)}, u32[]{:S(2)}) collective-permute-start(f32[80,4096]{1,0:T(8,128)S(1)} %collective-permute-done.8.refs_4_), channel_id=1, source_target_pairs={{0,2},{2,4},{4,6},{6,7},{7,5},{5,3},{3,1},{1,0},{8,10},{10,12},{12... | collective-permute-start | bytes 3932168 | tf_op jit(solution)/shard_map/cond/branch_1_fun/ppermute | solution.py:572
  247.2 23.0 %copy-start.25 = (f32[80,4096]{1,0:T(8,128)}, f32[80,4096]{1,0:T(8,128)S(1)}, u32[]{:S(2)}) copy-start(f32[80,4096]{1,0:T(8,128)S(1)} %collective-permute-done.9.refs_5_) | copy-start | bytes 3932164 | tf_op jit(solution)/shard_map/cond
  247.2 31.3 %collective-permute-start.11 = (f32[80,4096]{1,0:T(8,128)S(1)}, f32[80,4096]{1,0:T(8,128)}, u32[]{:S(2)}, u32[]{:S(2)}) collective-permute-start(f32[80,4096]{1,0:T(8,128)S(1)} %collective-permute-done.9.refs_5_), channel_id=1, source_target_pairs={{2,0},{4,2},{6,4},{7,6},{5,7},{3,5},{1,3},{0,1},{10,8},{12,10},{14... | collective-permute-start | bytes 3932168 | tf_op jit(solution)/shard_map/cond/branch_1_fun/ppermute | solution.py:573
  277.0 23.7 %copy-start.26 = (f32[80,4096]{1,0:T(8,128)}, f32[80,4096]{1,0:T(8,128)S(1)}, u32[]{:S(2)}) copy-start(f32[80,4096]{1,0:T(8,128)S(1)} %collective-permute-done.10.refs_6_) | copy-start | bytes 3932164 | tf_op jit(solution)/shard_map/cond
  277.0 30.1 %collective-permute-start.12 = (f32[80,4096]{1,0:T(8,128)S(1)}, f32[80,4096]{1,0:T(8,128)S(1)}, u32[]{:S(2)}, u32[]{:S(2)}) collective-permute-start(f32[80,4096]{1,0:T(8,128)S(1)} %collective-permute-done.10.refs_6_), channel_id=1, source_target_pairs={{0,2},{2,4},{4,6},{6,7},{7,5},{5,3},{3,1},{1,0},{8,10},{10,12},{12... | collective-permute-start | bytes 3932168 | tf_op jit(solution)/shard_map/cond/branch_1_fun/ppermute | solution.py:572
  278.4 29.8 %collective-permute-start.13 = (f32[80,4096]{1,0:T(8,128)}, f32[80,4096]{1,0:T(8,128)S(1)}, u32[]{:S(2)}, u32[]{:S(2)}) collective-permute-start(f32[80,4096]{1,0:T(8,128)} %collective-permute-done.11.refs_7_), channel_id=1, source_target_pairs={{2,0},{4,2},{6,4},{7,6},{5,7},{3,5},{1,3},{0,1},{10,8},{12,10},{14... | collective-permute-start | bytes 3932168 | tf_op jit(solution)/shard_map/cond/branch_1_fun/ppermute | solution.py:573
  300.7 39.8 %collective-permute-start.7 = (f32[304,2048]{1,0:T(8,128)}, f32[304,2048]{1,0:T(8,128)}, u32[]{:S(2)}, u32[]{:S(2)}) collective-permute-start(f32[304,2048]{1,0:T(8,128)} %collective-permute-done.5.refs_1_), channel_id=1, source_target_pairs={{0,8},{8,0},{16,24},{24,16},{1,9},{9,1},{17,25},{25,17},{2,10},{10... | collective-permute-start | bytes 7471112 | tf_op jit(solution)/shard_map/cond/branch_1_fun/ppermute | solution.py:592
  307.1 31.0 %copy-start.27 = (f32[80,4096]{1,0:T(8,128)}, f32[80,4096]{1,0:T(8,128)S(1)}, u32[]{:S(2)}) copy-start(f32[80,4096]{1,0:T(8,128)S(1)} %collective-permute-done.12.refs_8_) | copy-start | bytes 3932164 | tf_op jit(solution)/shard_map/cond
  307.1 31.0 %collective-permute-start.14 = (f32[80,4096]{1,0:T(8,128)S(1)}, f32[80,4096]{1,0:T(8,128)S(1)}, u32[]{:S(2)}, u32[]{:S(2)}) collective-permute-start(f32[80,4096]{1,0:T(8,128)S(1)} %collective-permute-done.12.refs_8_), channel_id=1, source_target_pairs={{0,2},{2,4},{4,6},{6,7},{7,5},{5,3},{3,1},{1,0},{8,10},{10,12},{12... | collective-permute-start | bytes 3932168 | tf_op jit(solution)/shard_map/cond/branch_1_fun/ppermute | solution.py:572
  308.2 29.9 %copy-start.28 = (f32[80,4096]{1,0:T(8,128)}, f32[80,4096]{1,0:T(8,128)S(1)}, u32[]{:S(2)}) copy-start(f32[80,4096]{1,0:T(8,128)S(1)} %collective-permute-done.13.refs_9_) | copy-start | bytes 3932164 | tf_op jit(solution)/shard_map/cond
  308.2 30.9 %collective-permute-start.15 = (f32[80,4096]{1,0:T(8,128)S(1)}, f32[80,4096]{1,0:T(8,128)}, u32[]{:S(2)}, u32[]{:S(2)}) collective-permute-start(f32[80,4096]{1,0:T(8,128)S(1)} %collective-permute-done.13.refs_9_), channel_id=1, source_target_pairs={{2,0},{4,2},{6,4},{7,6},{5,7},{3,5},{1,3},{0,1},{10,8},{12,10},{14... | collective-permute-start | bytes 3932168 | tf_op jit(solution)/shard_map/cond/branch_1_fun/ppermute | solution.py:573
  338.1 29.1 %copy-start.29 = (f32[80,4096]{1,0:T(8,128)}, f32[80,4096]{1,0:T(8,128)S(1)}, u32[]{:S(2)}) copy-start(f32[80,4096]{1,0:T(8,128)S(1)} %collective-permute-done.14.refs_10_) | copy-start | bytes 3932164 | tf_op jit(solution)/shard_map/cond
  338.1 29.1 %collective-permute-start.16 = (f32[80,4096]{1,0:T(8,128)S(1)}, f32[80,4096]{1,0:T(8,128)S(1)}, u32[]{:S(2)}, u32[]{:S(2)}) collective-permute-start(f32[80,4096]{1,0:T(8,128)S(1)} %collective-permute-done.14.refs_10_), channel_id=1, source_target_pairs={{0,2},{2,4},{4,6},{6,7},{7,5},{5,3},{3,1},{1,0},{8,10},{10,12},{12... | collective-permute-start | bytes 3932168 | tf_op jit(solution)/shard_map/cond/branch_1_fun/ppermute | solution.py:572
  339.2 29.1 %collective-permute-start.17 = (f32[80,4096]{1,0:T(8,128)}, f32[80,4096]{1,0:T(8,128)S(1)}, u32[]{:S(2)}, u32[]{:S(2)}) collective-permute-start(f32[80,4096]{1,0:T(8,128)} %collective-permute-done.15.refs_11_), channel_id=1, source_target_pairs={{2,0},{4,2},{6,4},{7,6},{5,7},{3,5},{1,3},{0,1},{10,8},{12,10},{14... | collective-permute-start | bytes 3932168 | tf_op jit(solution)/shard_map/cond/branch_1_fun/ppermute | solution.py:573
  367.2 64.0 %copy-start.2 = (f32[80,4096]{1,0:T(8,128)}, f32[80,4096]{1,0:T(8,128)S(1)}, u32[]{:S(2)}) copy-start(f32[80,4096]{1,0:T(8,128)S(1)} %collective-permute-done.16.refs_0_) | copy-start | bytes 3932164 | tf_op jit(solution)/shard_map/cond
  367.2 64.0 %collective-permute-start.18 = (f32[80,4096]{1,0:T(8,128)S(1)}, f32[80,4096]{1,0:T(8,128)S(1)}, u32[]{:S(2)}, u32[]{:S(2)}) collective-permute-start(f32[80,4096]{1,0:T(8,128)S(1)} %collective-permute-done.16.refs_0_), channel_id=1, source_target_pairs={{0,2},{2,4},{4,6},{6,7},{7,5},{5,3},{3,1},{1,0},{8,10},{10,12},{12... | collective-permute-start | bytes 3932168 | tf_op jit(solution)/shard_map/cond/branch_1_fun/ppermute | solution.py:572
  368.2 63.0 %copy-start.3 = (f32[80,4096]{1,0:T(8,128)}, f32[80,4096]{1,0:T(8,128)S(1)}, u32[]{:S(2)}) copy-start(f32[80,4096]{1,0:T(8,128)S(1)} %collective-permute-done.17.refs_1_) | copy-start | bytes 3932164 | tf_op jit(solution)/shard_map/cond
  368.3 63.0 %collective-permute-start.19 = (f32[80,4096]{1,0:T(8,128)S(1)}, f32[80,4096]{1,0:T(8,128)}, u32[]{:S(2)}, u32[]{:S(2)}) collective-permute-start(f32[80,4096]{1,0:T(8,128)S(1)} %collective-permute-done.17.refs_1_), channel_id=1, source_target_pairs={{2,0},{4,2},{6,4},{7,6},{5,7},{3,5},{1,3},{0,1},{10,8},{12,10},{14... | collective-permute-start | bytes 3932168 | tf_op jit(solution)/shard_map/cond/branch_1_fun/ppermute | solution.py:573
  431.2 1.1 copy-start.4
  (6 other events, 3.9 us)
